TPU v7x, 32 devices: a whole 2x2x4 slice. The times are simulated.
32 devices in a mesh: batch: 16 (over z, x, core), seq: 2 (over y).
Axes of the slice: x: 2, y: 2, z: 4, core: 2. Of those that a mesh axis runs over, the one named last changes fastest.
Arguments:
- latent_in: bfloat16 [32, 1024, 1152], P('batch', 'seq'), may hold values from -6 to 6
- conditioning: bfloat16 [32, 1152], P('batch'), may hold values from -6 to 6
- ada_weight: bfloat16 [7962624], P(('batch', 'seq')), may hold values from -0.1875 to 0.1875
- qkv_weight: bfloat16 [3981312], P(('batch', 'seq')), may hold values from -0.1875 to 0.1875
- proj_weight: bfloat16 [1327104], P(('batch', 'seq')), may hold values from -1 to 1
- up_weight: bfloat16 [5308416], P(('batch', 'seq')), may hold values from -0.1875 to 0.1875
- down_weight: bfloat16 [5308416], P(('batch', 'seq')), may hold values from -0.09375 to 0.09375
- bias_pack: bfloat16 [16128], P(('batch', 'seq')), may hold values from -2 to 2
- cotangent: bfloat16 [32, 1024, 1152], P('batch', 'seq'), may hold values from -6 to 6
Outputs:
- output: bfloat16 [32, 1024, 1152], P('batch', 'seq')
- grad_input: bfloat16 [32, 1024, 1152], P('batch', 'seq')
- grad_cond: bfloat16 [32, 1152], P('batch')
- grad_ada: float32 [7962624], P(('batch', 'seq'))
- grad_qkv: float32 [3981312], P(('batch', 'seq'))
- grad_proj: float32 [1327104], P(('batch', 'seq'))
- grad_up: float32 [5308416], P(('batch', 'seq'))
- grad_down: float32 [5308416], P(('batch', 'seq'))
- grad_bias: float32 [16128], P(('batch', 'seq'))
All inputs are finite; a program needn't handle non-finite values.
Results may differ from a plain program's by a relative error of at most 0.015.
The roundings to bfloat16 on the way count: a program that leaves them out, or rounds other values in their place, can miss the bound.
Values may be sent and summed in bfloat16 or wider, within the bound.
No kernel may reach another device: no remote copies, remote signals or barrier semaphores. Data moves between devices by JAX's collectives and lax.ppermute only.
A program may use at most 512 MiB of HBM per device.

v0:
```python
import jax
import jax.numpy as jnp
from jax import lax
from jax.sharding import PartitionSpec as P

H = 16
HD = 72
FF = 4608


EPS = 1e-06
GELU_COEF = 0.7978845608028654


def norm_modulate(inputs, shift_term, scale_term):
    center = inputs - jnp.mean(inputs, axis=-1, keepdims=True)
    spread = jnp.mean(center * center, axis=-1, keepdims=True)
    return center * lax.rsqrt(spread + EPS) * (1.0 + scale_term) + shift_term


def gelu_tanh(values):
    return (
        0.5 * values * (1.0 + jnp.tanh(GELU_COEF * (values + 0.044715 * values * values * values)))
    )


def flat_term(left, right):
    product = jnp.einsum("nd,nf->df", left, right, preferred_element_type=jnp.float32).reshape(-1)
    return product


def split_heads(queries, keys_values):
    query_rows = queries.shape[0]
    key_rows = keys_values.shape[0]
    model_width = queries.shape[1]
    query_heads = queries.reshape(query_rows, H, HD)
    key_heads = keys_values[:, :model_width].reshape(key_rows, H, HD)
    value_heads = keys_values[:, model_width:].reshape(key_rows, H, HD)
    scores = jnp.einsum(
        "qhe,khe->hqk", query_heads, key_heads, preferred_element_type=jnp.float32
    ) * HD ** (-0.5)
    return (query_heads, key_heads, value_heads, scores)


def attend_latent(block_items):
    queries, keys_values = block_items
    query_heads, key_heads, value_heads, scores = split_heads(queries, keys_values)
    top_score = jnp.max(scores, axis=-1, keepdims=True)
    exp_scores = jnp.exp(scores - top_score)
    exp_total = jnp.sum(exp_scores, axis=-1, keepdims=True)
    probs_low = (exp_scores / exp_total).astype(jnp.bfloat16)
    attended = jnp.einsum(
        "hqk,khe->qhe", probs_low, value_heads, preferred_element_type=jnp.float32
    )
    return (
        attended.reshape(queries.shape[0], queries.shape[1]),
        (top_score + jnp.log(exp_total))[..., 0],
    )


def attend_back(block_items):
    queries, keys_values, log_total, d_attended = block_items
    query_rows = queries.shape[0]
    key_rows = keys_values.shape[0]
    model_width = queries.shape[1]
    query_heads, key_heads, value_heads, scores = split_heads(queries, keys_values)
    attention_probs = jnp.exp(scores - log_total[..., None])
    d_heads = d_attended.reshape(query_rows, H, HD)
    d_probs = jnp.einsum("qhe,khe->hqk", d_heads, value_heads, preferred_element_type=jnp.float32)
    centered = d_probs - jnp.sum(attention_probs * d_probs, axis=-1, keepdims=True)
    d_scores = (HD ** (-0.5) * (attention_probs * centered)).astype(jnp.bfloat16)
    d_queries = jnp.einsum("hqk,khe->qhe", d_scores, key_heads, preferred_element_type=jnp.float32)
    d_keys = jnp.einsum("hqk,qhe->khe", d_scores, query_heads, preferred_element_type=jnp.float32)
    d_values = jnp.einsum(
        "hqk,qhe->khe",
        attention_probs.astype(jnp.bfloat16),
        d_heads,
        preferred_element_type=jnp.float32,
    )
    joined = jnp.concatenate(
        [d_keys.reshape(key_rows, model_width), d_values.reshape(key_rows, model_width)], axis=1
    )
    return (d_queries.reshape(query_rows, model_width), joined)


def shape_all(gathered, model_width):
    ada_full, qkv_full, proj_full, up_full, down_full, bias_full = gathered
    return (
        ada_full.reshape(model_width, 6 * model_width),
        qkv_full.reshape(model_width, 3 * model_width),
        proj_full.reshape(model_width, model_width),
        up_full.reshape(model_width, FF),
        down_full.reshape(FF, model_width),
        bias_full.astype(jnp.float32),
    )


def local(
    latent_in,
    conditioning,
    ada_weight,
    qkv_weight,
    proj_weight,
    up_weight,
    down_weight,
    bias_pack,
    cotangent,
):
    model_width = latent_in.shape[2]
    every_param = (
        lax.all_gather(ada_weight, ("batch", "seq"), axis=0, tiled=True),
        lax.all_gather(qkv_weight, ("batch", "seq"), axis=0, tiled=True),
        lax.all_gather(proj_weight, ("batch", "seq"), axis=0, tiled=True),
        lax.all_gather(up_weight, ("batch", "seq"), axis=0, tiled=True),
        lax.all_gather(down_weight, ("batch", "seq"), axis=0, tiled=True),
        lax.all_gather(bias_pack, ("batch", "seq"), axis=0, tiled=True),
    )
    ada_matrix, qkv_matrix, proj_matrix, up_matrix, down_matrix, biases = shape_all(
        every_param, model_width
    )
    ada_bias = biases[: 6 * model_width]
    query_bias = biases[6 * model_width : 7 * model_width]
    value_bias = biases[7 * model_width : 8 * model_width]
    proj_bias = biases[8 * model_width : 9 * model_width]
    up_bias = biases[9 * model_width : 9 * model_width + FF]
    down_bias = biases[9 * model_width + FF :]
    tokens = latent_in.astype(jnp.float32)
    conditions = conditioning.astype(jnp.float32)
    silu_cond = jax.nn.silu(conditions).astype(jnp.bfloat16)
    modulations = jnp.dot(silu_cond, ada_matrix, preferred_element_type=jnp.float32) + ada_bias
    shift_attention, scale_attention, gate_attention, shift_feed, scale_feed, gate_feed = jnp.split(
        modulations[:, None, :], 6, axis=2
    )
    normed = norm_modulate(tokens, shift_attention, scale_attention).astype(jnp.bfloat16)
    projected = jnp.einsum("btd,df->btf", normed, qkv_matrix, preferred_element_type=jnp.float32)
    queries = (projected[..., :model_width] + query_bias).astype(jnp.bfloat16)
    own_keys = jnp.concatenate(
        [
            projected[..., model_width : 2 * model_width],
            projected[..., 2 * model_width :] + value_bias,
        ],
        axis=2,
    ).astype(jnp.bfloat16)
    every_keys = lax.all_gather(own_keys, "seq", axis=1, tiled=True)
    attended, log_total = lax.map(attend_latent, (queries, every_keys))
    attended = attended.astype(jnp.bfloat16)
    branch = (
        jnp.einsum("btd,de->bte", attended, proj_matrix, preferred_element_type=jnp.float32)
        + proj_bias
    )
    middle = tokens + gate_attention * branch
    normed_feed = norm_modulate(middle, shift_feed, scale_feed).astype(jnp.bfloat16)
    before = (
        jnp.einsum("btd,df->btf", normed_feed, up_matrix, preferred_element_type=jnp.float32)
        + up_bias
    )
    activated = gelu_tanh(before).astype(jnp.bfloat16)
    feed_out = (
        jnp.einsum("btf,fd->btd", activated, down_matrix, preferred_element_type=jnp.float32)
        + down_bias
    )
    output = (middle + gate_feed * feed_out).astype(jnp.bfloat16)
    param_again = (
        lax.all_gather(ada_weight, ("batch", "seq"), axis=0, tiled=True),
        lax.all_gather(qkv_weight, ("batch", "seq"), axis=0, tiled=True),
        lax.all_gather(proj_weight, ("batch", "seq"), axis=0, tiled=True),
        lax.all_gather(up_weight, ("batch", "seq"), axis=0, tiled=True),
        lax.all_gather(down_weight, ("batch", "seq"), axis=0, tiled=True),
        lax.all_gather(bias_pack, ("batch", "seq"), axis=0, tiled=True),
    )
    ada_matrix, qkv_matrix, proj_matrix, up_matrix, down_matrix, biases = shape_all(
        param_again, model_width
    )
    upstream = cotangent.astype(jnp.float32)
    d_gate_feed = jnp.sum(upstream * feed_out, axis=1, keepdims=True)
    d_feed = (gate_feed * upstream).astype(jnp.bfloat16)
    d_activated = jnp.einsum("btd,fd->btf", d_feed, down_matrix, preferred_element_type=jnp.float32)
    unused_gelu, gelu_pull = jax.vjp(gelu_tanh, before)
    d_before = gelu_pull(d_activated)[0].astype(jnp.bfloat16)
    d_normed_feed = jnp.einsum(
        "btf,df->btd", d_before, up_matrix, preferred_element_type=jnp.float32
    )
    unused_norm, norm_pull = jax.vjp(norm_modulate, middle, shift_feed, scale_feed)
    d_middle_part, d_shift_feed, d_scale_feed = norm_pull(d_normed_feed)
    d_middle = upstream + d_middle_part
    d_gate_attention = jnp.sum(d_middle * branch, axis=1, keepdims=True)
    d_branch = (gate_attention * d_middle).astype(jnp.bfloat16)
    d_attended = jnp.einsum(
        "bte,de->btd", d_branch, proj_matrix, preferred_element_type=jnp.float32
    ).astype(jnp.bfloat16)
    d_queries, d_every = lax.map(attend_back, (queries, every_keys, log_total, d_attended))
    d_queries = d_queries.astype(jnp.bfloat16)
    d_own = lax.psum_scatter(d_every.astype(jnp.bfloat16), "seq", scatter_dimension=1, tiled=True)
    d_projected = jnp.concatenate([d_queries, d_own], axis=2)
    d_normed = jnp.einsum(
        "btf,df->btd", d_projected, qkv_matrix, preferred_element_type=jnp.float32
    )
    unused_first, first_pull = jax.vjp(norm_modulate, tokens, shift_attention, scale_attention)
    d_tokens_part, d_shift_attention, d_scale_attention = first_pull(d_normed)
    grad_input = (d_middle + d_tokens_part).astype(jnp.bfloat16)
    local_mods = jnp.concatenate(
        [
            d_shift_attention,
            d_scale_attention,
            d_gate_attention,
            d_shift_feed,
            d_scale_feed,
            d_gate_feed,
        ],
        axis=2,
    )[:, 0, :]
    d_mods = lax.psum(local_mods.astype(jnp.bfloat16), "seq")
    d_silu = jnp.einsum("bf,df->bd", d_mods, ada_matrix, preferred_element_type=jnp.float32)
    unused_silu, silu_pull = jax.vjp(jax.nn.silu, conditions)
    grad_cond = silu_pull(d_silu)[0].astype(jnp.bfloat16)
    is_owner = lax.axis_index("seq") == 0
    owned_mods = jnp.where(is_owner, d_mods, jnp.zeros_like(d_mods))
    bias_terms = jnp.concatenate(
        [
            jnp.sum(owned_mods, axis=0, dtype=jnp.float32),
            jnp.sum(d_queries, axis=(0, 1), dtype=jnp.float32),
            jnp.sum(d_own[..., model_width:], axis=(0, 1), dtype=jnp.float32),
            jnp.sum(d_branch, axis=(0, 1), dtype=jnp.float32),
            jnp.sum(d_before, axis=(0, 1), dtype=jnp.float32),
            jnp.sum(d_feed, axis=(0, 1), dtype=jnp.float32),
        ]
    )
    matrix_terms = [
        (silu_cond, owned_mods, ada_weight.shape[0]),
        (
            normed.reshape(-1, model_width),
            d_projected.reshape(-1, 3 * model_width),
            qkv_weight.shape[0],
        ),
        (
            attended.reshape(-1, model_width),
            d_branch.reshape(-1, model_width),
            proj_weight.shape[0],
        ),
        (normed_feed.reshape(-1, model_width), d_before.reshape(-1, FF), up_weight.shape[0]),
        (activated.reshape(-1, FF), d_feed.reshape(-1, model_width), down_weight.shape[0]),
    ]
    bias_share = bias_pack.shape[0]
    shard_rows = sum((entry[2] for entry in matrix_terms)) + bias_share
    block_count = shard_rows * lax.axis_size(("batch", "seq")) // shard_rows
    pieces = []
    for left, right, grad_shard_size in matrix_terms:
        pieces.append(flat_term(left, right).reshape(block_count, grad_shard_size))
    pieces.append(bias_terms.reshape(block_count, bias_share))
    owned_grads = lax.psum_scatter(
        jnp.concatenate(pieces, axis=1).reshape(-1),
        ("batch", "seq"),
        scatter_dimension=0,
        tiled=True,
    )
    results = []
    cursor = 0
    for shard_size in [entry[2] for entry in matrix_terms] + [bias_share]:
        results.append(owned_grads[cursor : cursor + shard_size])
        cursor = cursor + shard_size
    grad_ada, grad_qkv, grad_proj, grad_up, grad_down, grad_bias = results
    return (
        output,
        grad_input,
        grad_cond,
        grad_ada,
        grad_qkv,
        grad_proj,
        grad_up,
        grad_down,
        grad_bias,
    )


def solution(mesh):
    in_specs = (
        P("batch", "seq", None),
        P("batch", None),
        P(("batch", "seq")),
        P(("batch", "seq")),
        P(("batch", "seq")),
        P(("batch", "seq")),
        P(("batch", "seq")),
        P(("batch", "seq")),
        P("batch", "seq", None),
    )
    out_specs = (
        P("batch", "seq", None),
        P("batch", "seq", None),
        P("batch", None),
        P(("batch", "seq")),
        P(("batch", "seq")),
        P(("batch", "seq")),
        P(("batch", "seq")),
        P(("batch", "seq")),
        P(("batch", "seq")),
    )
    return jax.shard_map(local, mesh=mesh, in_specs=in_specs, out_specs=out_specs, check_vma=False)
```

profile of v0, /device:TPU:1, one launch (start us, length us, event | category | flops | bytes accessed | tf_op | source)
XLA Modules:
  0.0 2976.6 jit_solution(13369519791119738826)
XLA Ops:
  14.0 42.4 %all-reduce = bf16[16128]{0:T(1024)(128)(2,1)S(1)} all-reduce(bf16[16128]{0:T(1024)(128)(2,1)S(1)} %dynamic-update-slice), channel_id=1, replica_groups=mesh['batch'=16,'seq'=2] {'batch','seq'}, use_global_device_ids=true, to_apply=%add | all-reduce | flops 16128 | bytes 64512
  59.8 66.0 %all-gather.17.cloned.1.call-done = bf16[32,1,124416]{2,1,0:T(2,128)(2,1)} async-done(((bf16[1,1,124416]{2,1,0:T(2,128)(2,1)}), bf16[32,1,124416]{2,1,0:T(2,128)(2,1)}) %all-gather.17.cloned.1.call-update) | async-done | bytes 7962640 | tf_op jit(solution)/shard_map/all_gather | solution.py:112
  125.9 167.2 %reduce = bf16[32,124416]{1,0:T(8,128)(2,1)} reduce(bf16[32,1,124416]{2,1,0:T(2,128)(2,1)} %all-gather.17.cloned.1.call-done, bf16[]{:T(256)} %constant.87), dimensions={1}, to_apply=%all-gather.reduce_sub_computation | reduce | bytes 15925250 | tf_op jit(solution)/shard_map/all_gather | solution.py:112
  293.1 14.8 reshape.202
  307.9 29.3 reshape.183
  364.1 47.5 %reduce.1 = bf16[32,41472]{1,0:T(8,128)(2,1)S(1)} reduce(bf16[32,1,41472]{2,1,0:T(2,128)(2,1)} %all-gather.19.cloned.1.call-done, bf16[]{:T(256)} %constant.87), dimensions={1}, to_apply=%all-gather.1.reduce_sub_computation | reduce | bytes 5308418 | tf_op jit(solution)/shard_map/all_gather | solution.py:113
  416.6 20.4 reshape.205
  437.0 45.9 %all-gather.13.cloned.1.call-done = bf16[5308416]{0:T(1024)(128)(2,1)} async-done(((bf16[165888]{0:T(1024)(128)(2,1)}), bf16[5308416]{0:T(1024)(128)(2,1)}) %all-gather.13.cloned.1.call-update) | async-done | bytes 10616848 | tf_op jit(solution)/shard_map/all_gather | solution.py:114
  482.9 19.5 reshape.204
  505.2 93.1 %all-gather.11.cloned.1.call-done = bf16[2,1024,2304]{2,1,0:T(8,128)(2,1)} async-done(((bf16[2,512,2304]{2,1,0:T(8,128)(2,1)}), bf16[2,1024,2304]{2,1,0:T(8,128)(2,1)}) %all-gather.11.cloned.1.call-update) | async-done | bytes 9437200 | tf_op jit(solution)/shard_map/all_gather | solution.py:144
  611.0 92.2 %while.24 = (s32[]{:T(128)}, bf16[2,512,1152]{1,2,0:T(8,128)(2,1)}, f32[2,16,512]{2,1,0:T(8,128)S(1)}, bf16[2,1024,2304]{1,2,0:T(8,128)(2,1)}, bf16[2,512,1152]{1,2,0:T(8,128)(2,1)S(1)}, /*index=5*/s32[]{:T(128)}) while((s32[]{:T(128)}, bf16[2,512,1152]{1,2,0:T(8,128)(2,1)}, f32[2,16,512]{2,1,0:T(8,128)S(1)}, ...), condition=%wide.region_5.6_spmd, body=%wide.region_2.5_spmd.sunk | while | flops 2491408384 | bytes 150470816 | solution.py:145
  714.4 21.4 fusion.58
  735.9 30.5 %convert_reduce_fusion = (f32[4608]{0:T(1024)}, bf16[2,512,4608]{2,1,0:T(8,128)(2,1)}) fusion(bf16[4608,1152,1]{1,0,2:T(8,128)(2,1)S(1)} %bitcast.160, bf16[2,512,1152]{2,1,0:T(8,128)(2,1)S(1)} %copy-done.9, f32[2,1152]{1,0:T(2,128)S(1)} %copy-done.45, f32[2,512,4608]{2,1,0:T(8,128)} %fusion.58, f32[4608]{0:T(1024)S(1)} %copy-done.35), kind=kOutput, calls=%fused_computation.47 | convolution fusion | flops 11002572800 | bytes 41333760 | tf_op jit(solution)/shard_map/btd,fd->btf/dot_general | solution.py:177
  766.4 21.6 multiply_reduce_fusion.2
  793.8 30.8 %convert_reduce_fusion.2 = (f32[1152]{0:T(1024)}, bf16[2,1152]{1,0:T(2,128)(2,1)}, bf16[2,1152]{1,0:T(2,128)(2,1)}, f32[1152]{0:T(1024)}, bf16[2,512,1152]{2,1,0:T(8,128)(2,1)}, /*index=5*/bf16[2,512,1152]{2,1,0:T(8,128)(2,1)}) fusion(bf16[2,512,1152]{2,1,0:T(8,128)(2,1)} %param.21, f32[2,1152]{1,0:T(2,128)S(1)} %copy-done.45, ...), kind=kOutput, calls=%fused_computation.82 | convolution fusion | flops 10941229056 | bytes 50788864 | tf_op jit(solution)/shard_map/btf,fd->btd/dot_general | solution.py:159
  831.2 395.9 %while.25 = (s32[]{:T(128)}, bf16[2,512,1152]{2,1,0:T(8,128)(2,1)}, bf16[2,1024,2304]{2,1,0:T(8,128)(2,1)}, bf16[2,1024,2304]{1,2,0:T(8,128)(2,1)}, bf16[2,512,1...) while((s32[]{:T(128)}, bf16[2,512,1152]{2,1,0:T(8,128)(2,1)}, ...), condition=%wide.region_12.13_spmd, body=%wide.region_10.12_spmd.sunk | while | flops 6225414144 | bytes 335577312 | solution.py:191
  839.0 15.1 fusion.153
  867.9 68.9 %fusion.155 = bf16[16,72,512]{2,1,0:T(8,128)(2,1)} fusion(bf16[1024,16,72]{0,2,1:T(8,128)(2,1)S(1)} %bitcast.145, f32[16,512,1024]{2,1,0:T(8,128)} %fusion.153, f32[16,512,1024]{2,1,0:T(8,128)} %fusion.154, f32[16,512]{1,0:T(8,128)} %dynamic-slice_bitcast_fusion.8), kind=kOutput, calls=%fused_computation.23.clone.1 | convolution fusion | flops 1283466240 | bytes 70680576 | tf_op jit(solution)/shard_map/while/body/eval_jaxpr/hqk,khe->qhe/dot_general | solution.py:72
  953.2 59.9 %fusion.157 = bf16[16,72,1024]{2,1,0:T(8,128)(2,1)} fusion(bf16[512,16,72]{0,2,1:T(8,128)(2,1)} %bitcast.152, f32[16,512,1024]{2,1,0:T(8,128)} %fusion.153, f32[16,512,1024]{2,1,0:T(8,128)} %fusion.154, f32[16,512]{1,0:T(8,128)} %dynamic-slice_bitcast_fusion.8), kind=kOutput, calls=%fused_computation.22.clone.1 | convolution fusion | flops 1283466240 | bytes 70680576 | tf_op jit(solution)/shard_map/while/body/eval_jaxpr/hqk,qhe->khe/dot_general | solution.py:73
  1036.6 15.1 fusion.153
  1065.6 68.9 %fusion.155 = bf16[16,72,512]{2,1,0:T(8,128)(2,1)} fusion(bf16[1024,16,72]{0,2,1:T(8,128)(2,1)S(1)} %bitcast.145, f32[16,512,1024]{2,1,0:T(8,128)} %fusion.153, f32[16,512,1024]{2,1,0:T(8,128)} %fusion.154, f32[16,512]{1,0:T(8,128)} %dynamic-slice_bitcast_fusion.8), kind=kOutput, calls=%fused_computation.23.clone.1 | convolution fusion | flops 1283466240 | bytes 70680576 | tf_op jit(solution)/shard_map/while/body/eval_jaxpr/hqk,khe->qhe/dot_general | solution.py:72
  1150.9 59.9 %fusion.157 = bf16[16,72,1024]{2,1,0:T(8,128)(2,1)} fusion(bf16[512,16,72]{0,2,1:T(8,128)(2,1)} %bitcast.152, f32[16,512,1024]{2,1,0:T(8,128)} %fusion.153, f32[16,512,1024]{2,1,0:T(8,128)} %fusion.154, f32[16,512]{1,0:T(8,128)} %dynamic-slice_bitcast_fusion.8), kind=kOutput, calls=%fused_computation.22.clone.1 | convolution fusion | flops 1283466240 | bytes 70680576 | tf_op jit(solution)/shard_map/while/body/eval_jaxpr/hqk,qhe->khe/dot_general | solution.py:73
  1241.2 20.1 convolution_bitcast_fusion.1
  1261.3 30.5 %reshape_reshape.18 = f32[32,165888]{1,0:T(8,128)} reshape(f32[1152,4608]{1,0:T(8,128)} %convolution_bitcast_fusion.1) | data formatting | bytes 42467328 | tf_op jit(solution)/shard_map/reshape;reshape | solution.py:248
  1291.8 24.9 convolution_bitcast_fusion
  1316.8 22.7 reshape_reshape.19
  1341.6 14.4 fusion.44
  1380.0 36.1 %reshape_reshape.15 = f32[32,248832]{1,0:T(8,128)} reshape(f32[1152,6912]{1,0:T(8,128)} %fusion.59) | data formatting | bytes 63700992 | tf_op jit(solution)/shard_map/reshape;reshape | solution.py:248
  1416.1 22.4 constant_dynamic-update-slice_fusion.15
  1495.8 15.1 constant_dynamic-update-slice_fusion.11
  1511.6 122.9 %reshape.193 = f32[23904000]{0:T(1024)} reshape(f32[32,747000]{1,0:T(8,128)} %constant_dynamic-update-slice_fusion.10) | data formatting | bytes 191232000 | tf_op jit(solution)/shard_map/reshape | solution.py:251
  1651.8 1307.2 %all-reduce.4.cloned.1.call-done = f32[23904000]{0:T(1024)} async-done(((f32[23904000]{0:T(1024)}), f32[23904000]{0:T(1024)}) %all-reduce.4.cloned.1.call-update) | async-done | bytes 95616016
  (285 shorter events, 405.8 us)
Async XLA Ops:
  7.2 51.3 %copy-start.3 = (bf16[2,512,1152]{2,1,0:T(8,128)(2,1)S(1)}, bf16[2,512,1152]{2,1,0:T(8,128)(2,1)}, u32[]{:S(2)}) copy-start(bf16[2,512,1152]{2,1,0:T(8,128)(2,1)} %param.13) | copy-start | bytes 7077892
  7.2 118.7 %all-gather.17.cloned.1.call-start = ((), (), s32[]{:S(2)}) async-start(), calls=%async_computation.6 | async-start | bytes 16422912 | tf_op jit(solution)/shard_map/all_gather | solution.py:112
  9.4 298.5 %all-gather.9.cloned.1.call-start = ((), (), s32[]{:S(2)}) async-start(), calls=%async_computation.1 | async-start | bytes 16422912 | tf_op jit(solution)/shard_map/all_gather | solution.py:111
  10.1 354.0 %all-gather.19.cloned.1.call-start = ((), (), s32[]{:S(2)}) async-start(), calls=%async_computation.7 | async-start | bytes 5474304 | tf_op jit(solution)/shard_map/all_gather | solution.py:113
  11.9 404.8 %all-gather.15.cloned.1.call-start = ((), (), s32[]{:S(2)}) async-start(), calls=%async_computation.4 | async-start | bytes 10948608 | tf_op jit(solution)/shard_map/all_gather | solution.py:115
  12.4 470.4 %all-gather.13.cloned.1.call-start = ((), (), s32[]{:S(2)}) async-start(), calls=%async_computation.3 | async-start | bytes 10948608 | tf_op jit(solution)/shard_map/all_gather | solution.py:114
  13.0 585.3 %all-gather.11.cloned.1.call-start = ((), (), s32[]{:S(2)}) async-start(), calls=%async_computation.2 | async-start | bytes 14155776 | tf_op jit(solution)/shard_map/all_gather | solution.py:144
  58.4 287.2 %copy-start.19 = (f32[2,512]{1,0:T(2,128)}, f32[2,512]{1,0:T(2,128)S(1)}, u32[]{:S(2)}) copy-start(f32[2,512]{1,0:T(2,128)S(1)} %broadcast_multiply_fusion.1) | copy-start | bytes 12292
  59.2 233.9 %copy-start.31 = (f32[2,512]{1,0:T(2,128)}, f32[2,512]{1,0:T(2,128)S(1)}, u32[]{:S(2)}) copy-start(f32[2,512]{1,0:T(2,128)S(1)} %fusion.43) | copy-start | bytes 12292
  59.2 286.4 %copy-start.27 = (f32[2,512]{1,0:T(2,128)}, f32[2,512]{1,0:T(2,128)S(1)}, u32[]{:S(2)}) copy-start(f32[2,512]{1,0:T(2,128)S(1)} %fusion.70) | copy-start | bytes 12292
  307.9 29.3 copy-start.22
  363.5 978.1 %reduce-scatter.2.cloned.1.call-start = ((), (), s32[]{:S(2)}) async-start(), calls=%async_computation.5 | async-start | bytes 14155776 | tf_op jit(solution)/shard_map/reduce_scatter | solution.py:193
  611.0 92.2 %copy-start.49 = (f32[2,1152]{1,0:T(2,128)S(1)}, f32[2,1152]{1,0:T(2,128)}, u32[]{:S(2)}) copy-start(f32[2,1152]{1,0:T(2,128)} %get-tuple-element.184) | copy-start | bytes 27652
  611.0 92.2 %copy-start.53 = (f32[1152]{0:T(1024)S(1)}, f32[1152]{0:T(1024)}, u32[]{:S(2)}) copy-start(f32[1152]{0:T(1024)} %get-tuple-element.188) | copy-start | bytes 13828
  713.6 22.2 copy-start.6
  713.6 74.3 %copy-start.33 = (f32[2,512]{1,0:T(2,128)}, f32[2,512]{1,0:T(2,128)S(1)}, u32[]{:S(2)}) copy-start(f32[2,512]{1,0:T(2,128)S(1)} %broadcast_multiply_fusion) | copy-start | bytes 12292
  713.6 22.2 slice-start.6
  714.3 73.7 %copy-start.41 = (f32[2,512]{1,0:T(2,128)}, f32[2,512]{1,0:T(2,128)S(1)}, u32[]{:S(2)}) copy-start(f32[2,512]{1,0:T(2,128)S(1)} %fusion.71) | copy-start | bytes 12292
  714.4 21.5 copy-start.9
  714.4 21.5 copy-start.35
  714.4 21.5 copy-start.45
  793.8 30.8 %copy-start.38 = (f32[2,512]{1,0:T(2,128)}, f32[2,512]{1,0:T(2,128)S(1)}, u32[]{:S(2)}) copy-start(f32[2,512]{1,0:T(2,128)S(1)} %negate_multiply_fusion.1) | copy-start | bytes 12292
  793.8 30.8 %copy-start.8 = (bf16[1152,1152,1]{1,0,2:T(8,128)(2,1)S(1)}, bf16[1152,1152,1]{1,0,2:T(8,128)(2,1)}, u32[]{:S(2)}) copy-start(bf16[1152,1152,1]{1,0,2:T(8,128)(2,1)} %reshape.203) | copy-start | bytes 7962628
  1227.1 1731.9 %all-reduce.4.cloned.1.call-start = ((), (), s32[]{:S(2)}) async-start(), calls=%async_computation.8 | async-start | bytes 191234048
  1261.3 30.5 %copy-start.10 = (bf16[2,512,1152]{2,1,0:T(8,128)(2,1)S(1)}, bf16[2,512,1152]{2,1,0:T(8,128)(2,1)}, u32[]{:S(2)}) copy-start(bf16[2,512,1152]{2,1,0:T(8,128)(2,1)} %param.21) | copy-start | bytes 7077892
  1261.3 30.5 %copy-start.36 = (f32[4608]{0:T(1024)S(1)}, f32[4608]{0:T(1024)}, u32[]{:S(2)}) copy-start(f32[4608]{0:T(1024)} %slice.88) | copy-start | bytes 55300
  1261.3 30.5 %copy-start.46 = (f32[2,1152]{1,0:T(2,128)S(1)}, f32[2,1152]{1,0:T(2,128)}, u32[]{:S(2)}) copy-start(f32[2,1152]{1,0:T(2,128)} %get-tuple-element.179) | copy-start | bytes 27652
  1316.8 24.8 copy-start.4
  1316.8 24.8 copy-start.18
  1316.8 24.8 copy-start.20
  1416.1 22.4 copy-start.12
  1416.1 22.4 copy-start.44
  (52 other events, 518.9 us)
Sparse Core Ops, SparseCore 0:
  11.5 114.3 all-gather.16
  128.7 109.1 all-gather.8
  241.4 63.8 all-gather.18
  308.0 86.1 all-gather.14
  397.0 85.8 all-gather.12
  484.3 114.0 all-gather.10
  1227.2 110.5 reduce-scatter.1
  1634.6 1324.3 all-reduce.3
where the time goes:
time: 2990 us; the launch traced here: 2980 us
  waiting for transfers between devices  1510 us (51%)
  matrix products  640 us (21%)
  local copies, waits for them, and re-layouts  478 us (16%)
  other arithmetic  280 us (9%)
  blocking collectives  47.8 us (2%)
    unnamed x9, waiting for transfers between devices  1310 us
    all_gather x1, other arithmetic, local(): lax.all_gather(qkv_weight, ('batch', 'seq'), axis=0, tiled=True)  167 us
    dot_general x2, matrix products, attend_back(): jnp.einsum('hqk,khe->qhe', d_scores, key_heads, preferred_element_type=jn...  138 us
    reshape x1, local copies, waits for them, and re-layouts, local(): jnp.concatenate(pieces, axis=1).reshape(-1)  123 us
    dot_general x2, matrix products, attend_back(): jnp.einsum('hqk,qhe->khe', d_scores, query_heads, preferred_element_type=...  120 us
    another operation x5, local copies, waits for them, and re-layouts, local(): pieces.append(flat_term(left, right).reshape(block_count, grad_shard_size))  108 us
    all_gather x1, waiting for transfers between devices, local(): every_keys = lax.all_gather(own_keys, 'seq', axis=1, tiled=True)  93.1 us
    dot_general x5, matrix products, flat_term(): jnp.einsum('nd,nf->df', left, right, preferred_element_type=jnp.float32)  78.9 us
  transfers between devices with their start and end apart: 8, of which 4 were waited for; matrix products, arithmetic and copies ran while one was open for 16% of the time, Pallas kernels for 0%

commit v1 on v0

--- a/solution.py
+++ b/solution.py
@@ -1,6 +1,11 @@
+import functools
+
 import jax
 import jax.numpy as jnp
 from jax import lax
+from jax.experimental import pallas as pl
+from jax.experimental.pallas import tpu as pltpu
+from jax.sharding import Mesh
 from jax.sharding import PartitionSpec as P
 
 H = 16
@@ -10,6 +15,11 @@
 
 EPS = 1e-06
 GELU_COEF = 0.7978845608028654
+SCALE = HD ** (-0.5)
+LOG2E = 1.4426950408889634
+WIN = 256
+ALL = ("z", "x", "c", "y")
+SWAP = [(0, 1), (1, 0)]
 
 
 def norm_modulate(inputs, shift_term, scale_term):
@@ -95,7 +105,543 @@
     )
 
 
-def local(
+def head_window(head, width):
+    start = jnp.minimum((head * HD) // 128, width // 128 - 2) * 128
+    return pl.multiple_of(start, 128), head * HD - start
+
+
+def attn_fwd_kernel(q_ref, k_ref, v_ref, *refs, tile, first):
+    o_ref, lse_ref = refs[-2:]
+    head = pl.program_id(0) + first
+    rows, width = q_ref.shape
+
+    if len(refs) > 2:
+
+        @pl.when(pl.program_id(0) == 0)
+        def _():
+            o_ref[...] = refs[0][...]
+            lse_ref[...] = refs[1][...]
+
+    lo, off = head_window(head, width)
+    lane = lax.broadcasted_iota(jnp.int32, (1, WIN), 1)
+    inside = (lane >= off) & (lane < off + HD)
+    keep = inside.astype(jnp.bfloat16)
+    kw = k_ref[:, pl.ds(lo, WIN)]
+    vw = v_ref[:, pl.ds(lo, WIN)]
+    col = lax.broadcasted_iota(jnp.int32, (1, 128), 1) == head
+    for t in range(rows // tile):
+        r = pl.ds(t * tile, tile)
+        qm = q_ref[r, pl.ds(lo, WIN)] * keep
+        s = lax.dot_general(qm, kw, (((1,), (1,)), ((), ())), preferred_element_type=jnp.float32)
+        top = jnp.max(s, axis=-1, keepdims=True)
+        p = jnp.exp2((s - top) * (SCALE * LOG2E))
+        total = jnp.sum(p, axis=-1, keepdims=True)
+        o = jnp.dot(p.astype(jnp.bfloat16), vw, preferred_element_type=jnp.float32)
+        o = o * (1.0 / total)
+        old = o_ref[r, pl.ds(lo, WIN)].astype(jnp.float32)
+        o_ref[r, pl.ds(lo, WIN)] = jnp.where(inside, o, old).astype(jnp.bfloat16)
+        lse_ref[r, :] = jnp.where(col, top * SCALE + jnp.log(total), lse_ref[r, :])
+
+
+def whole(array_or_shape):
+    shape = array_or_shape.shape
+    return pl.BlockSpec(shape, lambda h: (0,) * len(shape), pipeline_mode=pl.Buffered(1))
+
+
+def attn_fwd(q, k, v, heads, into=(), tile=256):
+    rows, width = q.shape
+    keys = k.shape[0]
+    first, count = heads
+    outs = [
+        jax.ShapeDtypeStruct(q.shape, jnp.bfloat16),
+        jax.ShapeDtypeStruct((rows, 128), jnp.float32),
+    ]
+    ins = (q, k, v, *into)
+    return pl.pallas_call(
+        functools.partial(attn_fwd_kernel, tile=tile, first=first),
+        grid=(count,),
+        in_specs=[whole(a) for a in ins],
+        out_specs=[whole(a) for a in outs],
+        out_shape=outs,
+        compiler_params=pltpu.CompilerParams(vmem_limit_bytes=40 << 20),
+        cost_estimate=pl.CostEstimate(
+            flops=4 * count * rows * keys * WIN,
+            bytes_accessed=8 * rows * width,
+            transcendentals=count * rows * keys,
+        ),
+        name="attention_forward",
+    )(*ins)
+
+
+def attn_bwd_kernel(q_ref, k_ref, v_ref, g_ref, lse_ref, *refs, tile, first):
+    dq_ref, dk_ref, dv_ref = refs[-3:]
+    head = pl.program_id(0) + first
+    rows, width = q_ref.shape
+    keys = k_ref.shape[0]
+
+    if len(refs) > 3:
+
+        @pl.when(pl.program_id(0) == 0)
+        def _():
+            dq_ref[...] = refs[0][...]
+            dk_ref[...] = refs[1][...]
+            dv_ref[...] = refs[2][...]
+
+    lo, off = head_window(head, width)
+    lane = lax.broadcasted_iota(jnp.int32, (1, WIN), 1)
+    inside = (lane >= off) & (lane < off + HD)
+    keep = inside.astype(jnp.bfloat16)
+    kw = k_ref[:, pl.ds(lo, WIN)]
+    vw = v_ref[:, pl.ds(lo, WIN)]
+    ktw = kw.T
+    dk = jnp.zeros((keys, WIN), jnp.float32)
+    dv = jnp.zeros((keys, WIN), jnp.float32)
+    for t in range(rows // tile):
+        r = pl.ds(t * tile, tile)
+        lse = lse_ref[pl.ds(head, 1), r]
+        qw = q_ref[r, pl.ds(lo, WIN)]
+        gw = g_ref[r, pl.ds(lo, WIN)]
+        st = jnp.dot(kw, (qw * keep).T, preferred_element_type=jnp.float32)
+        pt = jnp.exp2(st * (SCALE * LOG2E) - lse * LOG2E)
+        dpt = jnp.dot(vw, (gw * keep).T, preferred_element_type=jnp.float32)
+        delta = jnp.sum(pt * dpt, axis=0, keepdims=True)
+        dst = (pt * (dpt - delta) * SCALE).astype(jnp.bfloat16)
+        dv = dv + jnp.dot(pt.astype(jnp.bfloat16), gw, preferred_element_type=jnp.float32)
+        dk = dk + jnp.dot(dst, qw, preferred_element_type=jnp.float32)
+        dq = jnp.dot(ktw, dst, preferred_element_type=jnp.float32).T
+        old = dq_ref[r, pl.ds(lo, WIN)].astype(jnp.float32)
+        dq_ref[r, pl.ds(lo, WIN)] = jnp.where(inside, dq, old).astype(jnp.bfloat16)
+    old = dk_ref[:, pl.ds(lo, WIN)].astype(jnp.float32)
+    dk_ref[:, pl.ds(lo, WIN)] = jnp.where(inside, dk, old).astype(jnp.bfloat16)
+    old = dv_ref[:, pl.ds(lo, WIN)].astype(jnp.float32)
+    dv_ref[:, pl.ds(lo, WIN)] = jnp.where(inside, dv, old).astype(jnp.bfloat16)
+
+
+def attn_bwd(q, k, v, g, lse_rows, heads, into=(), tile=512):
+    rows, width = q.shape
+    keys = k.shape[0]
+    first, count = heads
+    outs = [jax.ShapeDtypeStruct(a.shape, jnp.bfloat16) for a in (q, k, v)]
+    ins = (q, k, v, g, lse_rows, *into)
+    return pl.pallas_call(
+        functools.partial(attn_bwd_kernel, tile=tile, first=first),
+        grid=(count,),
+        in_specs=[whole(a) for a in ins],
+        out_specs=[whole(a) for a in outs],
+        out_shape=outs,
+        compiler_params=pltpu.CompilerParams(vmem_limit_bytes=52 << 20),
+        cost_estimate=pl.CostEstimate(
+            flops=10 * count * rows * keys * WIN,
+            bytes_accessed=14 * rows * width,
+            transcendentals=count * rows * keys,
+        ),
+        name="attention_backward",
+    )(*ins)
+
+
+def after(array, *earlier):
+    return lax.optimization_barrier((array, earlier))[0]
+
+
+def assemble(pieces, places, where, kind, height):
+    width = pieces[0].shape[-1]
+    blocks = [(i, b) for i, piece in enumerate(pieces) for b in range(piece.shape[0])]
+
+    def body(where_ref, *refs):
+        ins, out = refs[: len(pieces)], refs[len(pieces)]
+        held, arrived, left = refs[len(pieces) + 1 :]
+        zi = where_ref[0]
+        loads, stores = [], []
+        start = 0
+        for piece, (first, x_bit, c_bit, y_bit, offset) in zip(ins, places):
+            xi = where_ref[1] if x_bit == 0 else 1 - where_ref[1]
+            ci = where_ref[2] if c_bit == 0 else 1 - where_ref[2]
+            yi = where_ref[3] if y_bit == 0 else 1 - where_ref[3]
+            size = piece.shape[1]
+            for block in range(piece.shape[0]):
+                slot = start + block
+                row = ((zi ^ (first + block)) * 2 + xi) * height + offset
+                quarter = (ci * 2 + yi) * (8 * height)
+                if kind == "columns":
+                    rows = pl.ds(pl.multiple_of(row, 16), size)
+                    quarter = (ci * 2 + yi) * width
+                    target = out.at[rows, pl.ds(pl.multiple_of(quarter, 128), width)]
+                else:
+                    target = out.at[pl.ds(pl.multiple_of(quarter + row, 16), size), :]
+                here = held.at[slot, pl.ds(0, size)]
+                loads.append(pltpu.make_async_copy(piece.at[block], here, arrived.at[slot]))
+                stores.append(pltpu.make_async_copy(here, target, left.at[slot]))
+            start += piece.shape[0]
+        for load in loads:
+            load.start()
+        for load, store in zip(loads, stores):
+            load.wait()
+            store.start()
+        for store in stores:
+            store.wait()
+
+    shape = (8 * height, 4 * width) if kind == "columns" else (32 * height, width)
+    tallest = max(piece.shape[1] for piece in pieces)
+    return pl.pallas_call(
+        body,
+        grid_spec=pltpu.PrefetchScalarGridSpec(
+            num_scalar_prefetch=1,
+            grid=(1,),
+            in_specs=[pl.BlockSpec(memory_space=pl.ANY)] * len(pieces),
+            out_specs=pl.BlockSpec(memory_space=pl.ANY),
+            scratch_shapes=[
+                pltpu.VMEM((len(blocks), tallest, width), pieces[0].dtype),
+                pltpu.SemaphoreType.DMA((len(blocks),)),
+                pltpu.SemaphoreType.DMA((len(blocks),)),
+            ],
+        ),
+        out_shape=jax.ShapeDtypeStruct(shape, pieces[0].dtype),
+        compiler_params=pltpu.CompilerParams(vmem_limit_bytes=20 << 20),
+        cost_estimate=pl.CostEstimate(
+            flops=0, bytes_accessed=4 * shape[0] * shape[1], transcendentals=0
+        ),
+        name="assemble_" + kind,
+    )(where, *pieces)
+
+
+def swap(array, axis):
+    return lax.ppermute(array, axis, SWAP)
+
+
+def line_gather(unit):
+    hops = [lax.ppermute(unit, "z", [(i, i ^ step) for i in range(4)]) for step in range(1, 4)]
+    return jnp.stack([unit] + hops)
+
+
+def plane_gather(line):
+    return swap(line, "x"), swap(line, "y")
+
+
+def corner_gather(from_x, from_y):
+    return swap(from_x[:2], "y"), swap(from_y[2:], "x")
+
+
+PLACES = [(0, 0, 0, 0), (0, 1, 0, 0), (0, 0, 0, 1), (0, 1, 0, 1), (2, 1, 0, 1)]
+
+
+def with_core(pieces, others, offset=0):
+    places = [(first, x, c, y, offset) for first, x, c, y in PLACES]
+    places += [(first, x, 1 - c, y, offset) for first, x, c, y in PLACES]
+    return list(pieces) + list(others), places
+
+
+def add_low(*terms):
+    total = terms[0].astype(jnp.float32)
+    for term in terms[1:]:
+        total = total + term.astype(jnp.float32)
+    return total.astype(jnp.bfloat16)
+
+
+def part_columns(half, yy, xx):
+    width = half.shape[1] // 2
+    cut = lax.dynamic_slice(
+        half.reshape(4, 2, 144, 2 * width), (0, xx, 0, yy * width), (4, 1, 144, width)
+    )
+    return cut.reshape(4, 144, width)
+
+
+def part_rows(half, yy, xx):
+    width = half.shape[1]
+    cut = lax.dynamic_slice(
+        half.reshape(2, 4, 2, 144, width), (yy, 0, xx, 0, 0), (1, 4, 1, 144, width)
+    )
+    return cut.reshape(4, 144, width)
+
+
+class ScatterSum:
+    def __init__(self, part, xi, yi, zi):
+        self.part, self.xi, self.yi, self.zi = part, xi, yi, zi
+
+    def corner(self, half):
+        self.half = half
+        corner = self.part(half, 1 - self.yi, 1 - self.xi)
+        self.low, self.high = swap(corner[:2], "x"), swap(corner[2:], "y")
+        return self.low, self.high
+
+    def plane(self, *earlier):
+        half = after(self.half, *earlier) if earlier else self.half
+        to_y, to_x = self.part(half, 1 - self.yi, self.xi), self.part(half, self.yi, 1 - self.xi)
+        to_y = jnp.concatenate([add_low(to_y[:2], self.low), to_y[2:]])
+        to_x = jnp.concatenate([to_x[:2], add_low(to_x[2:], self.high)])
+        self.from_y, self.from_x = swap(to_y, "y"), swap(to_x, "x")
+        return self.from_y, self.from_x
+
+    def line(self, *earlier):
+        half = after(self.half, *earlier) if earlier else self.half
+        own = add_low(self.part(half, self.yi, self.xi), self.from_y, self.from_x)
+        self.own = lax.dynamic_index_in_dim(own, self.zi, 0, False)
+        self.hops = []
+        for step in range(1, 4):
+            block = lax.dynamic_index_in_dim(own, self.zi ^ step, 0, False)
+            self.hops.append(lax.ppermute(block, "z", [(i, i ^ step) for i in range(4)]))
+        return self.hops
+
+    def total(self):
+        total = self.own.astype(jnp.float32)
+        for hop in self.hops:
+            total = total + hop.astype(jnp.float32)
+        return total
+
+
+def local_pairs(
+    latent_in,
+    conditioning,
+    ada_weight,
+    qkv_weight,
+    proj_weight,
+    up_weight,
+    down_weight,
+    bias_pack,
+    cotangent,
+):
+    width = latent_in.shape[2]
+    half_rows = latent_in.shape[1]
+    zi, xi, ci, yi = [lax.axis_index(name) for name in ALL]
+    device = ((zi * 2 + xi) * 2 + ci) * 2 + yi
+    where = jnp.stack([zi, xi, ci, yi]).astype(jnp.int32)
+    rows = width // 32
+
+    def whole_latent(array):
+        own = lax.dynamic_index_in_dim(array, yi, 0, False)
+        other = lax.dynamic_index_in_dim(array, 1 - yi, 0, False)
+        return jnp.concatenate([own, swap(other, "y")])
+
+    def half_latents(array):
+        back = swap(array[half_rows:], "y")
+        own = array[:half_rows]
+        first = jnp.where(yi == 0, own, back)
+        second = jnp.where(yi == 0, back, own)
+        return jnp.stack([first, second])
+
+    def exchange(array):
+        return lax.all_to_all(array, ALL, 0, 0, tiled=True)
+
+    def to_all(vector):
+        return exchange(jnp.broadcast_to(vector, (32,) + vector.shape))
+
+    def over_tokens(left, right):
+        return lax.dot_general(
+            left, right, (((0,), (0,)), ((), ())), preferred_element_type=jnp.float32
+        )
+
+    def times_transposed(left, right):
+        return lax.dot_general(
+            left, right, (((1,), (1,)), ((), ())), preferred_element_type=jnp.float32
+        )
+
+    qkv_rows = qkv_weight.reshape(rows, 3 * width)
+    quarters = jnp.stack(
+        [qkv_rows[:, i * width : (i + 1) * width] for i in range(3)]
+        + [proj_weight.reshape(rows, width)]
+    )
+    unit_a = lax.all_to_all(quarters, ("c", "y"), 0, 0, tiled=True).reshape(4 * rows, width)
+    line_a0 = line_gather(unit_a[:64])
+    line_a1 = line_gather(after(unit_a[64:], line_a0))
+    own_condition = lax.dynamic_index_in_dim(conditioning, yi, 0, False)
+    small = to_all(jnp.concatenate([bias_pack, own_condition]))
+    bias_share = bias_pack.shape[0]
+    biases = small[:, :bias_share].reshape(-1).astype(jnp.float32)
+    conditions = small[:, bias_share:].astype(jnp.float32)
+    tokens_low = whole_latent(latent_in)
+    silu_all = jax.nn.silu(conditions).astype(jnp.bfloat16)
+    silu_cut = lax.dynamic_slice(silu_all, (0, device * rows), (32, rows))
+    ada_rows = ada_weight.reshape(rows, 6 * width)
+    shares = exchange(jnp.dot(silu_cut, ada_rows, preferred_element_type=jnp.float32))
+    modulations = jnp.sum(shares, axis=0, keepdims=True) + biases[: 6 * width]
+    shift_attention, scale_attention, gate_attention, shift_feed, scale_feed, gate_feed = jnp.split(
+        modulations, 6, axis=1
+    )
+
+    up_quarters = up_weight.reshape(rows, 8, 4, 144).transpose(2, 0, 1, 3).reshape(4, rows, width)
+    unit_u = lax.all_to_all(after(up_quarters, unit_a), ("c", "y"), 0, 0, tiled=True)
+    unit_u = unit_u.reshape(4 * rows, width)
+    unit_d = down_weight.reshape(4 * rows, width)
+
+    plane_a0 = plane_gather(line_a0)
+    core_a0 = [swap(p, "c") for p in (line_a0, *plane_a0)]
+    line_u = line_gather(after(unit_u, line_a1))
+    corner_a0 = corner_gather(*plane_a0)
+    plane_a1 = plane_gather(after(line_a1, *plane_a0))
+    core_a0 += [swap(p, "c") for p in corner_a0]
+    core_a1 = [swap(p, "c") for p in (line_a1, *plane_a1)]
+    corner_a1 = corner_gather(*plane_a1)
+    core_a1 += [swap(p, "c") for p in corner_a1]
+    pieces_0, places_0 = with_core((line_a0, *plane_a0, *corner_a0), core_a0)
+    pieces_1, places_1 = with_core((line_a1, *plane_a1, *corner_a1), core_a1, 64)
+    attention_matrix = assemble(
+        pieces_0 + pieces_1, places_0 + places_1, where, "columns", 4 * rows
+    )
+    plane_u = plane_gather(after(line_u, *corner_a1))
+    line_d = line_gather(after(unit_d, line_u))
+    qkv_matrix = attention_matrix[:, : 3 * width]
+    proj_matrix = attention_matrix[:, 3 * width :]
+
+    query_bias = biases[6 * width : 7 * width]
+    value_bias = biases[7 * width : 8 * width]
+    proj_bias = biases[8 * width : 9 * width]
+    up_bias = biases[9 * width : 9 * width + FF].reshape(8, 4, 144).transpose(1, 0, 2).reshape(-1)
+    down_bias = biases[9 * width + FF :]
+
+    tokens = tokens_low.astype(jnp.float32)
+    normed = norm_modulate(tokens, shift_attention, scale_attention).astype(jnp.bfloat16)
+    projected = jnp.dot(normed, qkv_matrix, preferred_element_type=jnp.float32)
+    queries = (projected[:, :width] + query_bias).astype(jnp.bfloat16)
+    keys = projected[:, width : 2 * width].astype(jnp.bfloat16)
+    values = (projected[:, 2 * width :] + value_bias).astype(jnp.bfloat16)
+    part_one = attn_fwd(queries, keys, values, (0, 8))
+
+    plane_u = [after(p, *part_one) for p in plane_u]
+    corner_u = corner_gather(*plane_u)
+    core_u = [swap(p, "c") for p in (after(line_u, *part_one), *plane_u)]
+    plane_d = plane_gather(after(line_d, *plane_u))
+    upstream_low = whole_latent(after(cotangent, *part_one))
+
+    attended, log_total = attn_fwd(queries, keys, values, (8, 8), tuple(part_one))
+    corner_u = [after(p, attended) for p in corner_u]
+    core_u += [swap(p, "c") for p in corner_u]
+    branch = jnp.dot(attended, proj_matrix, preferred_element_type=jnp.float32) + proj_bias
+    middle = tokens + gate_attention * branch
+    normed_feed = norm_modulate(middle, shift_feed, scale_feed).astype(jnp.bfloat16)
+    pieces, places = with_core((line_u, *plane_u, *corner_u), core_u)
+    up_matrix = assemble(
+        [after(p, normed_feed) for p in pieces], places, where, "columns", 4 * rows
+    )
+    plane_d = [after(p, up_matrix) for p in plane_d]
+    corner_d = corner_gather(*plane_d)
+    core_d = [swap(p, "c") for p in (after(line_d, up_matrix), *plane_d)]
+
+    before = jnp.dot(normed_feed, up_matrix, preferred_element_type=jnp.float32) + up_bias
+    activated = gelu_tanh(before).astype(jnp.bfloat16)
+    corner_d = [after(p, activated) for p in corner_d]
+    core_d += [swap(p, "c") for p in corner_d]
+    pieces, places = with_core((line_d, *plane_d, *corner_d), core_d)
+    down_matrix = assemble(
+        [after(p, activated) for p in pieces], places, where, "rows", 4 * rows
+    )
+    upstream = upstream_low.astype(jnp.float32)
+    d_feed = (gate_feed * upstream).astype(jnp.bfloat16)
+
+    def pick(array, core):
+        return lax.dynamic_slice_in_dim(array, core * 2 * width, 2 * width, 1)
+
+    down_sent = over_tokens(pick(activated, 1 - ci), d_feed).astype(jnp.bfloat16)
+    down_received = swap(down_sent, "c")
+    feed_out = jnp.dot(
+        after(activated, down_sent), down_matrix, preferred_element_type=jnp.float32
+    )
+    feed_out = feed_out + down_bias
+    output_low = (middle + gate_feed * feed_out).astype(jnp.bfloat16)
+    d_gate_feed = jnp.sum(upstream * feed_out, axis=0, keepdims=True)
+    down_half = over_tokens(pick(after(activated, output_low), ci), d_feed)
+    down_half = add_low(down_half, down_received)
+    down_scatter = ScatterSum(part_rows, xi, yi, zi)
+    down_scatter.corner(down_half)
+    output = half_latents(after(output_low, down_half))
+
+    d_activated = times_transposed(after(d_feed, down_half), down_matrix)
+    unused_gelu, gelu_pull = jax.vjp(gelu_tanh, before)
+    d_before = gelu_pull(d_activated)[0].astype(jnp.bfloat16)
+    down_scatter.plane(d_before)
+    up_sent = over_tokens(normed_feed, pick(d_before, 1 - ci)).astype(jnp.bfloat16)
+    up_received = swap(up_sent, "c")
+    d_normed_feed = times_transposed(after(d_before, up_sent), up_matrix)
+    up_half = over_tokens(normed_feed, pick(after(d_before, d_normed_feed), ci))
+    up_half = add_low(up_half, up_received)
+    up_scatter = ScatterSum(part_columns, xi, yi, zi)
+    up_scatter.corner(up_half)
+    down_scatter.line(up_half)
+    unused_norm, norm_pull = jax.vjp(norm_modulate, middle, shift_feed, scale_feed)
+    d_middle_part, d_shift_feed, d_scale_feed = norm_pull(after(d_normed_feed, up_half))
+    d_middle = upstream + d_middle_part
+    d_gate_attention = jnp.sum(d_middle * branch, axis=0, keepdims=True)
+    d_branch = (gate_attention * d_middle).astype(jnp.bfloat16)
+    d_attended = times_transposed(d_branch, proj_matrix).astype(jnp.bfloat16)
+    up_scatter.plane(d_attended)
+    log_rows = log_total[:, :H].T
+    part_one = attn_bwd(
+        queries, keys, values, after(d_attended, up_scatter.half), log_rows, (0, 8)
+    )
+    up_scatter.line(*part_one)
+    d_queries, d_keys, d_values = attn_bwd(
+        queries, keys, values, d_attended, log_rows, (8, 8), tuple(part_one)
+    )
+    proj_grad = over_tokens(attended, d_branch)
+    d_projected = jnp.concatenate([d_queries, d_keys, d_values], axis=1)
+    qkv_grad = over_tokens(normed, d_projected)
+    first_half = qkv_grad[:, : 2 * width]
+    second_half = jnp.concatenate([qkv_grad[:, 2 * width :], proj_grad], axis=1)
+    sent = jnp.where(ci == 0, second_half, first_half).astype(jnp.bfloat16)
+    received = swap(sent, "c")
+    d_normed = times_transposed(after(d_projected, sent), qkv_matrix)
+    attention_half = add_low(jnp.where(ci == 0, first_half, second_half), received)
+    attention_scatter = ScatterSum(part_columns, xi, yi, zi)
+    attention_scatter.corner(attention_half)
+    unused_first, first_pull = jax.vjp(norm_modulate, tokens, shift_attention, scale_attention)
+    d_tokens_part, d_shift_attention, d_scale_attention = first_pull(d_normed)
+    grad_low = (d_middle + d_tokens_part).astype(jnp.bfloat16)
+    attention_scatter.plane()
+    attention_scatter.line()
+
+    d_mods = jnp.concatenate(
+        [
+            d_shift_attention,
+            d_scale_attention,
+            d_gate_attention,
+            d_shift_feed,
+            d_scale_feed,
+            d_gate_feed,
+        ],
+        axis=1,
+    ).astype(jnp.bfloat16)
+    every_mods = to_all(d_mods[0])
+    grad_input = half_latents(grad_low)
+    grad_ada = over_tokens(silu_cut, every_mods).reshape(-1)
+    d_silu_rows = times_transposed(every_mods, ada_rows)
+    d_silu = exchange(jnp.repeat(d_silu_rows.reshape(16, 1, 2, rows), 2, axis=1).reshape(32, 2, rows))
+    d_silu = d_silu.transpose(1, 0, 2).reshape(2, width)
+    unused_silu, silu_pull = jax.vjp(jax.nn.silu, conditioning.astype(jnp.float32))
+    grad_cond = silu_pull(d_silu)[0].astype(jnp.bfloat16)
+
+    up_bias_grad = jnp.sum(d_before, axis=0, dtype=jnp.float32)
+    bias_terms = jnp.concatenate(
+        [
+            d_mods[0].astype(jnp.float32),
+            jnp.sum(d_queries, axis=0, dtype=jnp.float32),
+            jnp.sum(d_values, axis=0, dtype=jnp.float32),
+            jnp.sum(d_branch, axis=0, dtype=jnp.float32),
+            up_bias_grad.reshape(4, 8, 144).transpose(1, 0, 2).reshape(-1),
+            jnp.sum(d_feed, axis=0, dtype=jnp.float32),
+        ]
+    )
+    grad_bias = jnp.sum(exchange(bias_terms.reshape(32, -1)), axis=0)
+
+    up_sum = up_scatter.total().reshape(4, rows, width)
+    up_sum = lax.all_to_all(up_sum, ("c", "y"), 0, 0, tiled=True)
+    grad_up = up_sum.reshape(4, rows, 8, 144).transpose(1, 2, 0, 3).reshape(-1)
+    grad_down = down_scatter.total().reshape(-1)
+    sums = attention_scatter.total().reshape(4, rows, width)
+    sums = lax.all_to_all(sums, ("c", "y"), 0, 0, tiled=True)
+    grad_qkv = jnp.concatenate([sums[0], sums[1], sums[2]], axis=1).reshape(-1)
+    grad_proj = sums[3].reshape(-1)
+    return (
+        output,
+        grad_input,
+        grad_cond,
+        grad_ada,
+        grad_qkv,
+        grad_proj,
+        grad_up,
+        grad_down,
+        grad_bias,
+    )
+
+
+def local_any(
     latent_in,
     conditioning,
     ada_weight,
@@ -273,26 +819,16 @@
 
 
 def solution(mesh):
-    in_specs = (
-        P("batch", "seq", None),
-        P("batch", None),
-        P(("batch", "seq")),
-        P(("batch", "seq")),
-        P(("batch", "seq")),
-        P(("batch", "seq")),
-        P(("batch", "seq")),
-        P(("batch", "seq")),
-        P("batch", "seq", None),
-    )
-    out_specs = (
-        P("batch", "seq", None),
-        P("batch", "seq", None),
-        P("batch", None),
-        P(("batch", "seq")),
-        P(("batch", "seq")),
-        P(("batch", "seq")),
-        P(("batch", "seq")),
-        P(("batch", "seq")),
-        P(("batch", "seq")),
-    )
-    return jax.shard_map(local, mesh=mesh, in_specs=in_specs, out_specs=out_specs, check_vma=False)
+    batch, seq = mesh.shape["batch"], mesh.shape["seq"]
+    if (batch, seq) == (16, 2):
+        inner = Mesh(mesh.devices.reshape(4, 2, 2, 2), ALL)
+        body, tokens = local_pairs, ("z", "x", "c")
+        flat, split = P(ALL), "y"
+    else:
+        inner, body, tokens, split = mesh, local_any, "batch", "seq"
+        flat = P(("batch", "seq"))
+    activations = P(tokens, split, None)
+    vectors = P(tokens, None)
+    in_specs = (activations, vectors) + (flat,) * 6 + (activations,)
+    out_specs = (activations, activations, vectors) + (flat,) * 6
+    return jax.shard_map(body, mesh=inner, in_specs=in_specs, out_specs=out_specs, check_vma=False)

time: 2990 us -> 881 us (0.29)
  waiting for transfers between devices: 1510 us -> 144 us
  matrix products: 640 us -> 198 us
  local copies, waits for them, and re-layouts: 478 us -> 103 us
  other arithmetic: 280 us -> 112 us
  starting transfers between devices: 0.32 us -> 160 us
  Pallas kernels: 0 us -> 136 us
  blocking collectives: 47.8 us -> 10.3 us
    unnamed x9 -> x0, waiting for transfers between devices: 1310 us -> none
    dot_general x29 -> x17, matrix products: 640 us -> 198 us  [the longest x7 68 us: over_tokens(): lax.dot_general(left, right, (((0,), (0,)), ((), ())), preferred_element_...]
    all_gather x2 -> x0, other arithmetic: 215 us -> none  [the longest x1 167 us: local(): lax.all_gather(qkv_weight, ('batch', 'seq'), axis=0, tiled=True)]
    all_gather x6 -> x0, waiting for transfers between devices: 205 us -> none  [the longest x1 93.1 us: local(): every_keys = lax.all_gather(own_keys, 'seq', axis=1, tiled=True)]
    reshape x7 -> x18, local copies, waits for them, and re-layouts: 212 us -> 20.2 us  [the longest x2 3.79 us: local_pairs(): ada_rows = ada_weight.reshape(rows, 6 * width)]
    pallas_call x0 -> x7, Pallas kernels: none -> 136 us  [the longest x2 78.8 us: attn_bwd(): pl.pallas_call(functools.partial(attn_bwd_kernel, tile=tile, first=first)...]
    ppermute x0 -> x76, waiting for transfers between devices: none -> 123 us  [the longest x55 62.9 us: swap(): return lax.ppermute(array, axis, SWAP)]
    another operation x5, local copies, waits for them, and re-layouts: 108 us -> 3.68 us  [local(): pieces.append(flat_term(left, right).reshape(block_count, grad_shard_size))]
  transfers between devices with their start and end apart: 8 -> 84, of which waited for: 4 -> 18; matrix products, arithmetic and copies ran while one was open for 16% -> 38% of each run, Pallas kernels for 0% -> 16%
where the time goes in v1:
time: 881 us; the launch traced here: 866 us
  matrix products  198 us (22%)
  starting transfers between devices  160 us (18%)
  waiting for transfers between devices  144 us (16%)
  Pallas kernels  136 us (15%)
  other arithmetic  112 us (13%)
  local copies, waits for them, and re-layouts  103 us (12%)
  blocking collectives  10.3 us (1%)
    pallas_call x2, Pallas kernels, attn_bwd(): pl.pallas_call(functools.partial(attn_bwd_kernel, tile=tile, first=first)...  78.8 us
    dot_general x7, matrix products, over_tokens(): lax.dot_general(left, right, (((0,), (0,)), ((), ())), preferred_element_...  68 us
    dot_general x5, matrix products, times_transposed(): lax.dot_general(left, right, (((1,), (1,)), ((), ())), preferred_element_...  66 us
    ppermute x55, waiting for transfers between devices, swap(): return lax.ppermute(array, axis, SWAP)  62.9 us
    ppermute x55, starting transfers between devices, swap(): return lax.ppermute(array, axis, SWAP)  50 us
    all_to_all x5, starting transfers between devices, exchange(): return lax.all_to_all(array, ALL, 0, 0, tiled=True)  44.7 us
    ppermute x12, waiting for transfers between devices, line_gather(): lax.ppermute(unit, 'z', [(i, i ^ step) for i in range(4)])  37.5 us
    pallas_call x2, Pallas kernels, attn_fwd(): pl.pallas_call(functools.partial(attn_fwd_kernel, tile=tile, first=first)...  35.1 us
  transfers between devices with their start and end apart: 84, of which 18 were waited for; matrix products, arithmetic and copies ran while one was open for 38% of the time, Pallas kernels for 16%

profile of v1, /device:TPU:1, one launch (start us, length us, event | category | flops | bytes accessed | tf_op | source)
XLA Modules:
  0.0 865.5 jit_solution(8786831988057269166)
XLA Ops:
  3.0 10.3 %all_to_all.61 = bf16[4,36,1152]{2,1,0:T(8,128)(2,1)S(1)} all-to-all(bf16[4,36,1152]{2,1,0:T(8,128)(2,1)S(1)} %pad_maximum_fusion.16), channel_id=1, replica_groups=mesh['z'=4,'x'=2,'c'=2,'y'=2] {'c','y'}, dimensions={0} | all-to-all | bytes 663552 | tf_op jit(solution)/shard_map/all_to_all | solution.py:442
  66.4 6.8 collective-permute-done.27
  80.2 14.9 %all-to-all-start.1 = ((f32[32,1,6912]{2,1,0:T(1,128)}), f32[32,1,6912]{2,1,0:T(1,128)}, u32[]{:S(2)}, u32[]{:S(2)}) async-start(f32[32,1,6912]{2,1,0:T(1,128)} %copy.144), calls=%async_computation.1 | async-start | bytes 1769472 | tf_op jit(solution)/shard_map/all_to_all | solution.py:422
  106.7 24.6 %collective-permute-done.39 = bf16[144,1152]{1,0:T(8,128)(2,1)} collective-permute-done((bf16[144,1152]{1,0:T(8,128)(2,1)}, bf16[144,1152]{1,0:T(8,128)(2,1)}, u32[]{:S(2)}, u32[]{:S(2)}) %collective-permute-start.39) | collective-permute-done | bytes 331808 | tf_op jit(solution)/shard_map/ppermute | solution.py:312
  173.7 11.6 %assemble_columns.2 = bf16[1152,4608]{1,0:T(8,128)(2,1)S(1)} custom-call(s32[4]{0:T(128)S(1)} %pad_add_fusion.where_ref, bf16[4,64,1152]{2,1,0:T(8,128)(2,1)S(1)} %copy-done.5, bf16[4,64,1152]{2,1,0:T(8,128)(2,1)} %collective-permute-done.4.refs_1_, bf16[4,64,1152]{2,1,0:T(8,128)(2,1)} %collective-permute-done.5.refs_2_, ...), custom_call_target="tpu_custom_call" | custom-call | bytes 21233664 | tf_op jit(solution)/shard_map/assemble_columns/pallas_call | solution.py:285
  185.3 14.2 %fusion.12 = f32[1024,3456]{1,0:T(8,128)} fusion(bf16[1152,4608]{1,0:T(8,128)(2,1)S(1)} %assemble_columns.2, f32[1152]{0:T(1024)S(1)} %get-tuple-element.142, f32[1152]{0:T(1024)S(1)} %get-tuple-element.143, f32[1024]{0:T(1024)S(1)} %copy-done.79, f32[1024]{0:T(1024)S(1)} %broadcast_multiply_fusion.1, bf16[512,1152]{1,0:T(8,128)(2,1)} %collective-permute-done, ...), kind=kOutput, calls=%fused_computation.34 | convolution fusion | flops 8164343808 | bytes 24502272 | tf_op jit(solution)/shard_map/dot_general | solution.py:492
  207.5 17.3 %attention_forward.2 = (bf16[1024,1152]{1,0:T(8,128)(2,1)S(1)}, f32[1024,128]{1,0:T(8,128)S(1)}) custom-call(bf16[1024,1152]{1,0:T(8,128)(2,1)S(1)} %get-tuple-element.156.q_ref, bf16[1024,1152]{1,0:T(8,128)(2,1)S(1)} %slice.342.k_ref, bf16[1024,1152]{1,0:T(8,128)(2,1)S(1)} %get-tuple-element.155.v_ref), custom_call_target="tpu_custom_call" | custom-call | flops 8589934592 | bytes 9437184 | tf_op jit(solution)/shard_map/attention_forward/pallas_call | solution.py:160
  230.2 17.8 %attention_forward.3 = (bf16[1024,1152]{1,0:T(8,128)(2,1)S(1)}, f32[1024,128]{1,0:T(8,128)S(1)}) custom-call(bf16[1024,1152]{1,0:T(8,128)(2,1)S(1)} %copy-done.9, bf16[1024,1152]{1,0:T(8,128)(2,1)S(1)} %slice.342.k_ref, bf16[1024,1152]{1,0:T(8,128)(2,1)S(1)} %get-tuple-element.155.v_ref, bf16[1024,1152]{1,0:T(8,128)(2,1)S(1)} %get-tuple-element.72.refs_0_, ...), custom_call_target="tpu_custom_call" | custom-call | flops 8589934592 | bytes 9437184 | tf_op jit(solution)/shard_map/attention_forward/pallas_call | solution.py:160
  250.8 6.8 fusion.82
  267.7 7.6 collective-permute-done.30.refs_3_
  288.1 24.0 %multiply_convert_fusion = (bf16[1024,4608]{1,0:T(8,128)(2,1)}, f32[1024,4608]{1,0:T(8,128)}) fusion(f32[4608]{0:T(1024)S(1)} %copy-done.88, bf16[1024,1152]{1,0:T(8,128)(2,1)} %add_convert_fusion.5, bf16[1152,4608]{1,0:T(8,128)(2,1)S(1)} %assemble_columns.3), kind=kOutput, calls=%fused_computation.11 | convolution fusion | flops 10918821888 | bytes 41306112 | tf_op jit(solution)/shard_map/dot_general | solution.py:518
  312.1 9.7 %convolution_convert_fusion.1 = bf16[2304,1152]{1,0:T(8,128)(2,1)} fusion(bf16[1024,1152]{1,0:T(8,128)(2,1)S(1)} %copy-done.52, bf16[1024,4608]{1,0:T(8,128)(2,1)} %get-tuple-element.112, s32[]{:T(128)S(6)} %select_n.111), kind=kOutput, calls=%fused_computation.13 | convolution fusion | flops 5438472192 | bytes 12386308 | tf_op jit(solution)/shard_map/dot_general | solution.py:428
  327.6 13.1 %collective-permute-done.44.refs_4_ = bf16[2,144,1152]{2,1,0:T(8,128)(2,1)S(1)} collective-permute-done((bf16[2,144,1152]{2,1,0:T(8,128)(2,1)S(1)}, bf16[2,144,1152]{2,1,0:T(8,128)(2,1)S(1)}, u32[]{:S(2)}, u32[]{:S(2)}) %collective-permute-start.44) | collective-permute-done | bytes 663584 | tf_op jit(solution)/shard_map/ppermute | solution.py:308
  358.1 17.0 %add_convert_fusion.4 = (bf16[1024,1152]{1,0:T(8,128)(2,1)S(1)}, f32[1024,1152]{1,0:T(8,128)}) fusion(f32[1024,1152]{1,0:T(8,128)S(1)} %copy-done.32, f32[1152]{0:T(1024)S(1)} %copy-done.81, f32[1152]{0:T(1024)S(1)} %copy-done.93, bf16[1024,4608]{1,0:T(8,128)(2,1)} %get-tuple-element.112, bf16[4608,1152]{1,0:T(8,128)(2,1)S(1)} %assemble_rows.1), kind=kOutput, calls=%fused_computation.65 | convolution fusion | flops 10876354560 | bytes 31859712 | tf_op jit(solution)/shard_map/dot_general | solution.py:534
  375.2 13.0 %add_convert_fusion.2 = bf16[2304,1152]{1,0:T(8,128)(2,1)} fusion(bf16[2304,1152]{1,0:T(8,128)(2,1)} %collective-permute-done.50, bf16[1024,1152]{1,0:T(8,128)(2,1)S(1)} %copy-done.53, bf16[1024,4608]{1,0:T(8,128)(2,1)} %get-tuple-element.112, s32[]{:T(128)S(6)} %select_n.112), kind=kOutput, calls=%fused_computation.18 | convolution fusion | flops 5443780608 | bytes 17694724 | tf_op jit(solution)/shard_map/dot_general | solution.py:428
  388.2 30.0 %convert_reduce_fusion = (f32[4608]{0:T(1024)S(1)}, bf16[1024,4608]{1,0:T(8,128)(2,1)}) fusion(f32[1024,4608]{1,0:T(8,128)} %get-tuple-element.208, f32[4608]{0:T(1024)S(1)} %copy-done.88, bf16[1024,1152]{1,0:T(8,128)(2,1)} %get-tuple-element.114, bf16[4608,1152]{1,0:T(8,128)(2,1)S(1)} %assemble_rows.1), kind=kOutput, calls=%fused_computation.10 | convolution fusion | flops 10999033856 | bytes 41324544 | tf_op jit(solution)/shard_map/dot_general | solution.py:433
  418.2 10.9 %convolution_convert_fusion = bf16[1152,2304]{1,0:T(8,128)(2,1)} fusion(bf16[1024,1152]{1,0:T(8,128)(2,1)} %add_convert_fusion.5, bf16[1024,4608]{1,0:T(8,128)(2,1)} %get-tuple-element.116, s32[]{:T(128)S(6)} %select_n.111), kind=kOutput, calls=%fused_computation.12 | convolution fusion | flops 5438472192 | bytes 12386308 | tf_op jit(solution)/shard_map/dot_general | solution.py:428
  433.3 16.0 %fusion.86 = f32[1024,1152]{1,0:T(8,128)} fusion(bf16[1024,4608]{1,0:T(8,128)(2,1)} %get-tuple-element.116, bf16[1152,4608]{1,0:T(8,128)(2,1)S(1)} %bitcast.240), kind=kOutput, calls=%fused_computation.225 | convolution fusion | flops 10871635968 | bytes 24772608 | tf_op jit(solution)/shard_map/dot_general | solution.py:433
  455.8 16.0 %collective-permute-done.51 = bf16[512,1152]{1,0:T(8,128)(2,1)} collective-permute-done((bf16[512,1152]{1,0:T(8,128)(2,1)}, bf16[512,1152]{1,0:T(8,128)(2,1)}, u32[]{:S(2)}, u32[]{:S(2)}) %collective-permute-start.51) | collective-permute-done | bytes 1179680 | tf_op jit(solution)/shard_map/ppermute | solution.py:308
  474.9 11.1 %add_convert_fusion.1 = bf16[1152,2304]{1,0:T(8,128)(2,1)} fusion(bf16[1152,2304]{1,0:T(8,128)(2,1)} %collective-permute-done.52, bf16[1024,1152]{1,0:T(8,128)(2,1)S(1)} %copy-done.55, bf16[1024,4608]{1,0:T(8,128)(2,1)} %get-tuple-element.116, s32[]{:T(128)S(6)} %select_n.112), kind=kOutput, calls=%fused_computation.17 | convolution fusion | flops 5443780608 | bytes 17694724 | tf_op jit(solution)/shard_map/dot_general | solution.py:428
  506.0 37.8 %attention_backward.2 = (bf16[1024,1152]{1,0:T(8,128)(2,1)}, bf16[1024,1152]{1,0:T(8,128)(2,1)}, bf16[1024,1152]{1,0:T(8,128)(2,1)}) custom-call(bf16[1024,1152]{1,0:T(8,128)(2,1)} %copy-done.8, bf16[1024,1152]{1,0:T(8,128)(2,1)} %copy-done.6, bf16[1024,1152]{1,0:T(8,128)(2,1)} %copy-done.7, bf16[1024,1152]{1,0:T(8,128)(2,1)} %convolution_convert_fusion.2.g_ref, ...), custom_call_target="tpu_custom_call" | custom-call | flops 21474836480 | bytes 16515072 | tf_op jit(solution)/shard_map/attention_backward/pallas_call | solution.py:226
  543.8 41.0 %attention_backward.3 = (bf16[1024,1152]{1,0:T(8,128)(2,1)}, bf16[1024,1152]{1,0:T(8,128)(2,1)}, bf16[1024,1152]{1,0:T(8,128)(2,1)}) custom-call(bf16[1024,1152]{1,0:T(8,128)(2,1)} %copy-done.8, bf16[1024,1152]{1,0:T(8,128)(2,1)} %copy-done.6, bf16[1024,1152]{1,0:T(8,128)(2,1)} %copy-done.7, bf16[1024,1152]{1,0:T(8,128)(2,1)} %convolution_convert_fusion.2.g_ref, ...), custom_call_target="tpu_custom_call" | custom-call | flops 21474836480 | bytes 16515072 | tf_op jit(solution)/shard_map/attention_backward/pallas_call | solution.py:226
  591.6 15.4 %fusion.75 = f32[1152,3456]{1,0:T(8,128)} fusion(bf16[1024,3456]{1,0:T(8,128)(2,1)} %constant_dynamic-update-slice_fusion, f32[1152]{0:T(1024)S(1)} %copy-done.92, f32[1152]{0:T(1024)S(1)} %copy-done.68, f32[1024]{0:T(1024)S(1)} %copy-done.80, f32[1024]{0:T(1024)S(1)} %copy-done.71, bf16[512,1152]{1,0:T(8,128)(2,1)} %collective-permute-done, ...), kind=kOutput, calls=%fused_computation.218 | convolution fusion | flops 8164343808 | bytes 25379840 | tf_op jit(solution)/shard_map/dot_general | solution.py:428
  609.9 9.6 %select_convert_fusion = bf16[1152,2304]{1,0:T(8,128)(2,1)} fusion(f32[1152,3456]{1,0:T(8,128)} %fusion.75, f32[1152,1152]{1,0:T(8,128)S(1)} %bitcast.244, f32[1152,1152]{1,0:T(8,128)S(1)} %slice.300, pred[]{:T(512)S(6)} %eq.5), kind=kLoop, calls=%fused_computation.16 | loop fusion | flops 13271040 | bytes 21233664 | tf_op jit(solution)/shard_map/convert_element_type | solution.py:578
  630.6 13.7 %fusion.20 = (f32[1024]{0:T(1024)S(1)}, f32[1024,1152]{1,0:T(8,128)}) fusion(f32[1152]{0:T(1024)S(1)} %copy-done.68, f32[1024]{0:T(1024)S(1)} %copy-done.71, bf16[512,1152]{1,0:T(8,128)(2,1)} %collective-permute-done, bf16[512,1152]{1,0:T(8,128)(2,1)S(1)} %copy-done.37, bf16[1024,3456]{1,0:T(8,128)(2,1)} %constant_dynamic-update-slice_fusion, ...), kind=kOutput, calls=%fused_computation.43 | convolution fusion | flops 8163163136 | bytes 22134784 | tf_op jit(solution)/shard_map/dot_general | solution.py:433
  650.1 10.5 %fusion.22 = (bf16[1152]{0:T(1024)(128)(2,1)S(1)}, bf16[1152]{0:T(1024)(128)(2,1)S(1)}, bf16[1024,1152]{1,0:T(8,128)(2,1)}) fusion(f32[1024,1152]{1,0:T(8,128)} %get-tuple-element.210, bf16[512,1152]{1,0:T(8,128)(2,1)} %collective-permute-done.37, bf16[512,1152]{1,0:T(8,128)(2,1)S(1)} %copy-done.41, f32[1024,1152]{1,0:T(8,128)} %get-tuple-element.206, ...), kind=kLoop, calls=%fused_computation.45 | loop fusion | flops 27129600 | bytes 25981952 | tf_op jit(solution)/shard_map/reduce_sum | solution.py:539
  703.6 9.3 %add_convert_fusion = bf16[1152,2304]{1,0:T(8,128)(2,1)S(1)} fusion(bf16[1152,2304]{1,0:T(8,128)(2,1)} %collective-permute-done.54, f32[1152,3456]{1,0:T(8,128)} %fusion.75, f32[1152,1152]{1,0:T(8,128)} %fusion.87, f32[1152,1152]{1,0:T(8,128)} %copy-done.33, pred[]{:T(512)S(6)} %eq.5), kind=kLoop, calls=%fused_computation.15 | loop fusion | flops 13271040 | bytes 31850496 | tf_op jit(solution)/shard_map/convert_element_type | solution.py:337
  731.2 16.2 %all-to-all-start.5 = ((f32[32,2,36]{2,1,0:T(2,128)}), f32[32,2,36]{2,1,0:T(2,128)S(1)}, u32[]{:S(2)}, u32[]{:S(2)}) async-start(f32[32,2,36]{2,1,0:T(2,128)} %bitcast.35), calls=%async_computation.5 | async-start | bytes 65536 | tf_op jit(solution)/shard_map/all_to_all | solution.py:422
  752.0 17.2 %all-to-all-done.5 = f32[32,2,36]{2,1,0:T(2,128)S(1)} async-done(((f32[32,2,36]{2,1,0:T(2,128)}), f32[32,2,36]{2,1,0:T(2,128)S(1)}, u32[]{:S(2)}, u32[]{:S(2)}) %all-to-all-start.5) | async-done | bytes 9248 | tf_op jit(solution)/shard_map/all_to_all | solution.py:422
  777.5 6.5 collective-permute-start.66
  785.1 17.8 %collective-permute-done.56 = bf16[4,144,1152]{2,1,0:T(8,128)(2,1)S(1)} collective-permute-done((bf16[4,144,1152]{2,1,0:T(8,128)(2,1)S(1)}, bf16[4,144,1152]{2,1,0:T(8,128)(2,1)S(1)}, u32[]{:S(2)}, u32[]{:S(2)}) %collective-permute-start.56) | collective-permute-done | bytes 1327136 | tf_op jit(solution)/shard_map/ppermute | solution.py:308
  822.7 20.4 %collective-permute-done.60 = bf16[144,1152]{1,0:T(8,128)(2,1)} collective-permute-done((bf16[144,1152]{1,0:T(8,128)(2,1)}, bf16[144,1152]{1,0:T(8,128)(2,1)}, u32[]{:S(2)}, u32[]{:S(2)}) %collective-permute-start.60) | collective-permute-done | bytes 331808 | tf_op jit(solution)/shard_map/ppermute | solution.py:381
  (535 shorter events, 354.8 us)
Async XLA Ops:
  54.3 47.5 %collective-permute-start = (bf16[512,1152]{1,0:T(8,128)(2,1)}, bf16[512,1152]{1,0:T(8,128)(2,1)}, u32[]{:S(2)}, u32[]{:S(2)}) collective-permute-start(bf16[512,1152]{1,0:T(8,128)(2,1)} %get-tuple-element.181), channel_id=1, source_target_pairs={{0,1},{1,0},{2,3},{3,2},{4,5},{5,4},{6,7},{7,6},{8,9},{9,8},{10,11... | collective-permute-start | bytes 3538952 | tf_op jit(solution)/shard_map/ppermute | solution.py:308
  57.7 37.4 %collective-permute-start.4 = (bf16[4,64,1152]{2,1,0:T(8,128)(2,1)S(1)}, bf16[4,64,1152]{2,1,0:T(8,128)(2,1)}, u32[]{:S(2)}, u32[]{:S(2)}) collective-permute-start(bf16[4,64,1152]{2,1,0:T(8,128)(2,1)S(1)} %pad_maximum_fusion.14.refs_0_), channel_id=1, source_target_pairs={{0,4},{4,0},{1,5},{5,1},{2,6},{6,2},{3,7},{7,3},{8,12},{12,8},{9,1... | collective-permute-start | bytes 1769480 | tf_op jit(solution)/shard_map/ppermute | solution.py:308
  59.0 38.5 %collective-permute-start.5 = (bf16[4,64,1152]{2,1,0:T(8,128)(2,1)S(1)}, bf16[4,64,1152]{2,1,0:T(8,128)(2,1)}, u32[]{:S(2)}, u32[]{:S(2)}) collective-permute-start(bf16[4,64,1152]{2,1,0:T(8,128)(2,1)S(1)} %pad_maximum_fusion.14.refs_0_), channel_id=1, source_target_pairs={{0,1},{1,0},{2,3},{3,2},{4,5},{5,4},{6,7},{7,6},{8,9},{9,8},{10,11... | collective-permute-start | bytes 1769480 | tf_op jit(solution)/shard_map/ppermute | solution.py:308
  62.8 35.9 %collective-permute-start.8 = (bf16[4,64,1152]{2,1,0:T(8,128)(2,1)S(1)}, bf16[4,64,1152]{2,1,0:T(8,128)(2,1)S(1)}, u32[]{:S(2)}, u32[]{:S(2)}) collective-permute-start(bf16[4,64,1152]{2,1,0:T(8,128)(2,1)S(1)} %pad_maximum_fusion.14.refs_0_), channel_id=1, source_target_pairs={{0,2},{2,0},{1,3},{3,1},{4,6},{6,4},{5,7},{7,5},{8,10},{10,8},{9,1... | collective-permute-start | bytes 1769480 | tf_op jit(solution)/shard_map/ppermute | solution.py:308
  80.2 77.8 %all-to-all-start.1 = ((f32[32,1,6912]{2,1,0:T(1,128)}), f32[32,1,6912]{2,1,0:T(1,128)}, u32[]{:S(2)}, u32[]{:S(2)}) async-start(f32[32,1,6912]{2,1,0:T(1,128)} %copy.144), calls=%async_computation.1 | async-start | bytes 1769472 | tf_op jit(solution)/shard_map/all_to_all | solution.py:422
  95.1 36.2 %collective-permute-start.39 = (bf16[144,1152]{1,0:T(8,128)(2,1)}, bf16[144,1152]{1,0:T(8,128)(2,1)}, u32[]{:S(2)}, u32[]{:S(2)}) collective-permute-start(bf16[144,1152]{1,0:T(8,128)(2,1)} %reshape.282), channel_id=1, source_target_pairs={{0,16},{8,24},{16,0},{24,8},{1,17},{9,25},{17,1},{25,9},{2,18},{10... | collective-permute-start | bytes 995336 | tf_op jit(solution)/shard_map/ppermute | solution.py:312
  97.5 43.3 %collective-permute-start.16 = (bf16[4,80,1152]{2,1,0:T(8,128)(2,1)S(1)}, bf16[4,80,1152]{2,1,0:T(8,128)(2,1)}, u32[]{:S(2)}, u32[]{:S(2)}) collective-permute-start(bf16[4,80,1152]{2,1,0:T(8,128)(2,1)S(1)} %pad_maximum_fusion.13.refs_10_), channel_id=1, source_target_pairs={{0,4},{4,0},{1,5},{5,1},{2,6},{6,2},{3,7},{7,3},{8,12},{12,8},{9,1... | collective-permute-start | bytes 2211848 | tf_op jit(solution)/shard_map/ppermute | solution.py:308
  99.5 41.3 %collective-permute-start.17 = (bf16[4,80,1152]{2,1,0:T(8,128)(2,1)S(1)}, bf16[4,80,1152]{2,1,0:T(8,128)(2,1)S(1)}, u32[]{:S(2)}, u32[]{:S(2)}) collective-permute-start(bf16[4,80,1152]{2,1,0:T(8,128)(2,1)S(1)} %pad_maximum_fusion.13.refs_10_), channel_id=1, source_target_pairs={{0,1},{1,0},{2,3},{3,2},{4,5},{5,4},{6,7},{7,6},{8,9},{9,8},{10,11... | collective-permute-start | bytes 2211848 | tf_op jit(solution)/shard_map/ppermute | solution.py:308
  101.9 42.7 %collective-permute-start.20 = (bf16[4,80,1152]{2,1,0:T(8,128)(2,1)S(1)}, bf16[4,80,1152]{2,1,0:T(8,128)(2,1)}, u32[]{:S(2)}, u32[]{:S(2)}) collective-permute-start(bf16[4,80,1152]{2,1,0:T(8,128)(2,1)S(1)} %pad_maximum_fusion.13.refs_10_), channel_id=1, source_target_pairs={{0,2},{2,0},{1,3},{3,1},{4,6},{6,4},{5,7},{7,5},{8,10},{10,8},{9,1... | collective-permute-start | bytes 2211848 | tf_op jit(solution)/shard_map/ppermute | solution.py:308
  161.8 86.2 %collective-permute-start.29 = (bf16[4,144,1152]{2,1,0:T(8,128)(2,1)S(1)}, bf16[4,144,1152]{2,1,0:T(8,128)(2,1)}, u32[]{:S(2)}, u32[]{:S(2)}) collective-permute-start(bf16[4,144,1152]{2,1,0:T(8,128)(2,1)S(1)} %pad_maximum_fusion.5.refs_0_), channel_id=1, source_target_pairs={{0,1},{1,0},{2,3},{3,2},{4,5},{5,4},{6,7},{7,6},{8,9},{9,8},{10,11... | collective-permute-start | bytes 3981320 | tf_op jit(solution)/shard_map/ppermute | solution.py:308
  162.1 95.6 %collective-permute-start.28 = (bf16[4,144,1152]{2,1,0:T(8,128)(2,1)S(1)}, bf16[4,144,1152]{2,1,0:T(8,128)(2,1)}, u32[]{:S(2)}, u32[]{:S(2)}) collective-permute-start(bf16[4,144,1152]{2,1,0:T(8,128)(2,1)S(1)} %pad_maximum_fusion.5.refs_0_), channel_id=1, source_target_pairs={{0,4},{4,0},{1,5},{5,1},{2,6},{6,2},{3,7},{7,3},{8,12},{12,8},{9,1... | collective-permute-start | bytes 3981320 | tf_op jit(solution)/shard_map/ppermute | solution.py:308
  224.9 58.0 %collective-permute-start.32 = (bf16[4,144,1152]{2,1,0:T(8,128)(2,1)S(1)}, bf16[4,144,1152]{2,1,0:T(8,128)(2,1)}, u32[]{:S(2)}, u32[]{:S(2)}) collective-permute-start(bf16[4,144,1152]{2,1,0:T(8,128)(2,1)S(1)} %pad_maximum_fusion.5.refs_0_), channel_id=1, source_target_pairs={{0,2},{2,0},{1,3},{3,1},{4,6},{6,4},{5,7},{7,5},{8,10},{10,8},{9,1... | collective-permute-start | bytes 3981320 | tf_op jit(solution)/shard_map/ppermute | solution.py:308
  229.0 47.7 %collective-permute-start.37 = (bf16[512,1152]{1,0:T(8,128)(2,1)}, bf16[512,1152]{1,0:T(8,128)(2,1)}, u32[]{:S(2)}, u32[]{:S(2)}) collective-permute-start(bf16[512,1152]{1,0:T(8,128)(2,1)} %get-tuple-element.179), channel_id=1, source_target_pairs={{0,1},{1,0},{2,3},{3,2},{4,5},{5,4},{6,7},{7,6},{8,9},{9,8},{10,11... | collective-permute-start | bytes 3538952 | tf_op jit(solution)/shard_map/ppermute | solution.py:308
  282.9 40.0 %collective-permute-start.42 = (bf16[4,144,1152]{2,1,0:T(8,128)(2,1)}, bf16[4,144,1152]{2,1,0:T(8,128)(2,1)}, u32[]{:S(2)}, u32[]{:S(2)}) collective-permute-start(bf16[4,144,1152]{2,1,0:T(8,128)(2,1)} %pad_maximum_fusion.6.refs_0_), channel_id=1, source_target_pairs={{0,1},{1,0},{2,3},{3,2},{4,5},{5,4},{6,7},{7,6},{8,9},{9,8},{10,11... | collective-permute-start | bytes 3981320 | tf_op jit(solution)/shard_map/ppermute | solution.py:308
  283.3 41.9 %collective-permute-start.41 = (bf16[4,144,1152]{2,1,0:T(8,128)(2,1)}, bf16[4,144,1152]{2,1,0:T(8,128)(2,1)}, u32[]{:S(2)}, u32[]{:S(2)}) collective-permute-start(bf16[4,144,1152]{2,1,0:T(8,128)(2,1)} %pad_maximum_fusion.6.refs_0_), channel_id=1, source_target_pairs={{0,4},{4,0},{1,5},{5,1},{2,6},{6,2},{3,7},{7,3},{8,12},{12,8},{9,1... | collective-permute-start | bytes 3981320 | tf_op jit(solution)/shard_map/ppermute | solution.py:308
  321.8 53.3 %collective-permute-start.50 = (bf16[2304,1152]{1,0:T(8,128)(2,1)}, bf16[2304,1152]{1,0:T(8,128)(2,1)}, u32[]{:S(2)}, u32[]{:S(2)}) collective-permute-start(bf16[2304,1152]{1,0:T(8,128)(2,1)} %convolution_convert_fusion.1), channel_id=1, source_target_pairs={{0,2},{2,0},{1,3},{3,1},{4,6},{6,4},{5,7},{7,5},{8,10},{10,8},{9,1... | collective-permute-start | bytes 15925256 | tf_op jit(solution)/shard_map/ppermute | solution.py:308
  429.1 45.8 %collective-permute-start.52 = (bf16[1152,2304]{1,0:T(8,128)(2,1)}, bf16[1152,2304]{1,0:T(8,128)(2,1)}, u32[]{:S(2)}, u32[]{:S(2)}) collective-permute-start(bf16[1152,2304]{1,0:T(8,128)(2,1)} %convolution_convert_fusion), channel_id=1, source_target_pairs={{0,2},{2,0},{1,3},{3,1},{4,6},{6,4},{5,7},{7,5},{8,10},{10,8},{9,1... | collective-permute-start | bytes 15925256 | tf_op jit(solution)/shard_map/ppermute | solution.py:308
  432.9 38.8 %collective-permute-start.51 = (bf16[512,1152]{1,0:T(8,128)(2,1)}, bf16[512,1152]{1,0:T(8,128)(2,1)}, u32[]{:S(2)}, u32[]{:S(2)}) collective-permute-start(bf16[512,1152]{1,0:T(8,128)(2,1)} %slice.237), channel_id=1, source_target_pairs={{0,1},{1,0},{2,3},{3,2},{4,5},{5,4},{6,7},{7,6},{8,9},{9,8},{10,11... | collective-permute-start | bytes 3538952 | tf_op jit(solution)/shard_map/ppermute | solution.py:308
  453.1 169.1 %collective-permute-start.70 = (bf16[4,144,1152]{2,1,0:T(8,128)(2,1)}, bf16[4,144,1152]{2,1,0:T(8,128)(2,1)}, u32[]{:S(2)}, u32[]{:S(2)}) collective-permute-start(bf16[4,144,1152]{2,1,0:T(8,128)(2,1)} %pad_maximum_fusion.11), channel_id=1, source_target_pairs={{0,1},{1,0},{2,3},{3,2},{4,5},{5,4},{6,7},{7,6},{8,9},{9,8},{10,11... | collective-permute-start | bytes 3981320 | tf_op jit(solution)/shard_map/ppermute | solution.py:308
  455.4 166.7 %collective-permute-start.72 = (bf16[4,144,1152]{2,1,0:T(8,128)(2,1)}, bf16[4,144,1152]{2,1,0:T(8,128)(2,1)}, u32[]{:S(2)}, u32[]{:S(2)}) collective-permute-start(bf16[4,144,1152]{2,1,0:T(8,128)(2,1)} %pad_maximum_fusion.12), channel_id=1, source_target_pairs={{0,4},{4,0},{1,5},{5,1},{2,6},{6,2},{3,7},{7,3},{8,12},{12,8},{9,1... | collective-permute-start | bytes 3981320 | tf_op jit(solution)/shard_map/ppermute | solution.py:308
  619.5 84.2 %collective-permute-start.54 = (bf16[1152,2304]{1,0:T(8,128)(2,1)}, bf16[1152,2304]{1,0:T(8,128)(2,1)}, u32[]{:S(2)}, u32[]{:S(2)}) collective-permute-start(bf16[1152,2304]{1,0:T(8,128)(2,1)} %select_convert_fusion), channel_id=1, source_target_pairs={{0,2},{2,0},{1,3},{3,1},{4,6},{6,4},{5,7},{7,5},{8,10},{10,8},{9,1... | collective-permute-start | bytes 15925256 | tf_op jit(solution)/shard_map/ppermute | solution.py:308
  626.1 49.7 %collective-permute-start.73 = (bf16[144,1152]{1,0:T(8,128)(2,1)}, bf16[144,1152]{1,0:T(8,128)(2,1)S(1)}, u32[]{:S(2)}, u32[]{:S(2)}) collective-permute-start(bf16[144,1152]{1,0:T(8,128)(2,1)} %get-tuple-element.182), channel_id=1, source_target_pairs={{0,8},{8,0},{16,24},{24,16},{1,9},{9,1},{17,25},{25,17},{2,10},{10... | collective-permute-start | bytes 995336 | tf_op jit(solution)/shard_map/ppermute | solution.py:381
  687.0 33.9 %all-to-all-start.4 = ((bf16[32,2,3456]{2,1,0:T(2,128)(2,1)}), bf16[32,2,3456]{2,1,0:T(2,128)(2,1)}, u32[]{:S(2)}, u32[]{:S(2)}) async-start(bf16[32,2,3456]{2,1,0:T(2,128)(2,1)} %reshape.327), calls=%async_computation.4 | async-start | bytes 884736 | tf_op jit(solution)/shard_map/all_to_all | solution.py:422
  694.6 157.5 %collective-permute-start.53 = (bf16[512,1152]{1,0:T(8,128)(2,1)}, bf16[512,1152]{1,0:T(8,128)(2,1)}, u32[]{:S(2)}, u32[]{:S(2)}) collective-permute-start(bf16[512,1152]{1,0:T(8,128)(2,1)} %slice.303), channel_id=1, source_target_pairs={{0,1},{1,0},{2,3},{3,2},{4,5},{5,4},{6,7},{7,6},{8,9},{9,8},{10,11... | collective-permute-start | bytes 3538952 | tf_op jit(solution)/shard_map/ppermute | solution.py:308
  703.6 71.2 %collective-permute-start.63 = (bf16[4,144,1152]{2,1,0:T(8,128)(2,1)}, bf16[4,144,1152]{2,1,0:T(8,128)(2,1)}, u32[]{:S(2)}, u32[]{:S(2)}) collective-permute-start(bf16[4,144,1152]{2,1,0:T(8,128)(2,1)} %pad_maximum_fusion.9), channel_id=1, source_target_pairs={{0,1},{1,0},{2,3},{3,2},{4,5},{5,4},{6,7},{7,6},{8,9},{9,8},{10,11... | collective-permute-start | bytes 3981320 | tf_op jit(solution)/shard_map/ppermute | solution.py:308
  716.8 52.5 %collective-permute-start.55 = (bf16[2,144,1152]{2,1,0:T(8,128)(2,1)}, bf16[2,144,1152]{2,1,0:T(8,128)(2,1)}, u32[]{:S(2)}, u32[]{:S(2)}) collective-permute-start(bf16[2,144,1152]{2,1,0:T(8,128)(2,1)} %get-tuple-element.170), channel_id=1, source_target_pairs={{0,4},{4,0},{1,5},{5,1},{2,6},{6,2},{3,7},{7,3},{8,12},{12,8},{9,1... | collective-permute-start | bytes 1990664 | tf_op jit(solution)/shard_map/ppermute | solution.py:308
  718.3 51.0 %collective-permute-start.57 = (bf16[2,144,1152]{2,1,0:T(8,128)(2,1)}, bf16[2,144,1152]{2,1,0:T(8,128)(2,1)}, u32[]{:S(2)}, u32[]{:S(2)}) collective-permute-start(bf16[2,144,1152]{2,1,0:T(8,128)(2,1)} %get-tuple-element.172), channel_id=1, source_target_pairs={{0,1},{1,0},{2,3},{3,2},{4,5},{5,4},{6,7},{7,6},{8,9},{9,8},{10,11... | collective-permute-start | bytes 1990664 | tf_op jit(solution)/shard_map/ppermute | solution.py:308
  720.7 54.1 %collective-permute-start.65 = (bf16[4,144,1152]{2,1,0:T(8,128)(2,1)}, bf16[4,144,1152]{2,1,0:T(8,128)(2,1)}, u32[]{:S(2)}, u32[]{:S(2)}) collective-permute-start(bf16[4,144,1152]{2,1,0:T(8,128)(2,1)} %pad_maximum_fusion.10), channel_id=1, source_target_pairs={{0,4},{4,0},{1,5},{5,1},{2,6},{6,2},{3,7},{7,3},{8,12},{12,8},{9,1... | collective-permute-start | bytes 3981320 | tf_op jit(solution)/shard_map/ppermute | solution.py:308
  731.2 38.0 %all-to-all-start.5 = ((f32[32,2,36]{2,1,0:T(2,128)}), f32[32,2,36]{2,1,0:T(2,128)S(1)}, u32[]{:S(2)}, u32[]{:S(2)}) async-start(f32[32,2,36]{2,1,0:T(2,128)} %bitcast.35), calls=%async_computation.5 | async-start | bytes 65536 | tf_op jit(solution)/shard_map/all_to_all | solution.py:422
  773.6 32.4 %collective-permute-start.58 = (bf16[4,144,1152]{2,1,0:T(8,128)(2,1)S(1)}, bf16[4,144,1152]{2,1,0:T(8,128)(2,1)S(1)}, u32[]{:S(2)}, u32[]{:S(2)}) collective-permute-start(bf16[4,144,1152]{2,1,0:T(8,128)(2,1)S(1)} %pad_maximum_fusion.8), channel_id=1, source_target_pairs={{0,4},{4,0},{1,5},{5,1},{2,6},{6,2},{3,7},{7,3},{8,12},{12,8},{9,1... | collective-permute-start | bytes 3981320 | tf_op jit(solution)/shard_map/ppermute | solution.py:308
  777.5 36.4 %collective-permute-start.66 = (bf16[144,1152]{1,0:T(8,128)(2,1)S(1)}, bf16[144,1152]{1,0:T(8,128)(2,1)S(1)}, u32[]{:S(2)}, u32[]{:S(2)}) collective-permute-start(bf16[144,1152]{1,0:T(8,128)(2,1)S(1)} %get-tuple-element.185), channel_id=1, source_target_pairs={{0,8},{8,0},{16,24},{24,16},{1,9},{9,1},{17,25},{25,17},{2,10},{10... | collective-permute-start | bytes 995336 | tf_op jit(solution)/shard_map/ppermute | solution.py:381
  784.0 30.6 %collective-permute-start.67 = (bf16[144,1152]{1,0:T(8,128)(2,1)S(1)}, bf16[144,1152]{1,0:T(8,128)(2,1)S(1)}, u32[]{:S(2)}, u32[]{:S(2)}) collective-permute-start(bf16[144,1152]{1,0:T(8,128)(2,1)S(1)} %get-tuple-element.187), channel_id=1, source_target_pairs={{0,16},{8,24},{16,0},{24,8},{1,17},{9,25},{17,1},{25,9},{2,18},{10... | collective-permute-start | bytes 995336 | tf_op jit(solution)/shard_map/ppermute | solution.py:381
  (160 other events, 2410.3 us)

commit v2 on v1

--- a/solution.py
+++ b/solution.py
@@ -1,4 +1,5 @@
 import functools
+import itertools
 
 import jax
 import jax.numpy as jnp
@@ -240,6 +241,8 @@
 
 
 def after(array, *earlier):
+    if not earlier:
+        return array
     return lax.optimization_barrier((array, earlier))[0]
 
 
@@ -296,7 +299,7 @@
             ],
         ),
         out_shape=jax.ShapeDtypeStruct(shape, pieces[0].dtype),
-        compiler_params=pltpu.CompilerParams(vmem_limit_bytes=20 << 20),
+        compiler_params=pltpu.CompilerParams(vmem_limit_bytes=56 << 20),
         cost_estimate=pl.CostEstimate(
             flops=0, bytes_accessed=4 * shape[0] * shape[1], transcendentals=0
         ),
@@ -308,25 +311,34 @@
     return lax.ppermute(array, axis, SWAP)
 
 
-def line_gather(unit):
-    hops = [lax.ppermute(unit, "z", [(i, i ^ step) for i in range(4)]) for step in range(1, 4)]
-    return jnp.stack([unit] + hops)
+def line_hops(block_of):
+    return [
+        lax.ppermute(block_of(step), "z", [(i, i ^ step) for i in range(4)]) for step in range(1, 4)
+    ]
 
 
 def plane_gather(line):
     return swap(line, "x"), swap(line, "y")
 
 
+def corner_swap(array, first):
+    pairs = []
+    for x, c, y in itertools.product(range(2), repeat=3):
+        along_x = c == first
+        target = (1 - x, c, y) if along_x else (x, c, 1 - y)
+        pairs.append((x * 4 + c * 2 + y, target[0] * 4 + target[1] * 2 + target[2]))
+    return lax.ppermute(array, ("x", "c", "y"), pairs)
+
+
 def corner_gather(from_x, from_y):
-    return swap(from_x[:2], "y"), swap(from_y[2:], "x")
-
-
-PLACES = [(0, 0, 0, 0), (0, 1, 0, 0), (0, 0, 0, 1), (0, 1, 0, 1), (2, 1, 0, 1)]
-
-
-def with_core(pieces, others, offset=0):
-    places = [(first, x, c, y, offset) for first, x, c, y in PLACES]
-    places += [(first, x, 1 - c, y, offset) for first, x, c, y in PLACES]
+    return corner_swap(jnp.where(lax.axis_index("c") == 0, from_x, from_y), 1)
+
+
+PLACES = [(0, 0, 0), (1, 0, 0), (0, 0, 1), (1, 0, 1)]
+
+
+def with_core(pieces, others):
+    places = [(0, x, c, y, 0) for x, c, y in PLACES] + [(0, x, 1 - c, y, 0) for x, c, y in PLACES]
     return list(pieces) + list(others), places
 
 
@@ -354,36 +366,33 @@
 
 
 class ScatterSum:
-    def __init__(self, part, xi, yi, zi):
-        self.part, self.xi, self.yi, self.zi = part, xi, yi, zi
-
-    def corner(self, half):
-        self.half = half
-        corner = self.part(half, 1 - self.yi, 1 - self.xi)
-        self.low, self.high = swap(corner[:2], "x"), swap(corner[2:], "y")
-        return self.low, self.high
+    def __init__(self, part, half):
+        self.part, self.half = part, half
+        self.zi, self.xi, self.yi = [lax.axis_index(name) for name in ("z", "x", "y")]
+
+    def corner(self):
+        self.sent = (self.part(self.half, 1 - self.yi, 1 - self.xi),)
+        self.got = (corner_swap(self.sent[0], 0),)
 
     def plane(self, *earlier):
-        half = after(self.half, *earlier) if earlier else self.half
+        half, got = after(self.half, *earlier), self.got[0]
         to_y, to_x = self.part(half, 1 - self.yi, self.xi), self.part(half, self.yi, 1 - self.xi)
-        to_y = jnp.concatenate([add_low(to_y[:2], self.low), to_y[2:]])
-        to_x = jnp.concatenate([to_x[:2], add_low(to_x[2:], self.high)])
-        self.from_y, self.from_x = swap(to_y, "y"), swap(to_x, "x")
-        return self.from_y, self.from_x
+        even = lax.axis_index("c") == 0
+        to_y = jnp.where(even, add_low(to_y, got), to_y)
+        to_x = jnp.where(even, to_x, add_low(to_x, got))
+        self.sent = to_y, to_x
+        self.got = swap(to_y, "y"), swap(to_x, "x")
 
     def line(self, *earlier):
-        half = after(self.half, *earlier) if earlier else self.half
-        own = add_low(self.part(half, self.yi, self.xi), self.from_y, self.from_x)
-        self.own = lax.dynamic_index_in_dim(own, self.zi, 0, False)
-        self.hops = []
-        for step in range(1, 4):
-            block = lax.dynamic_index_in_dim(own, self.zi ^ step, 0, False)
-            self.hops.append(lax.ppermute(block, "z", [(i, i ^ step) for i in range(4)]))
-        return self.hops
-
-    def total(self):
-        total = self.own.astype(jnp.float32)
-        for hop in self.hops:
+        half = after(self.half, *earlier)
+        own = add_low(self.part(half, self.yi, self.xi), *self.got)
+        blocks = [lax.dynamic_index_in_dim(own, self.zi ^ step, 0, False) for step in range(4)]
+        self.own, self.sent = blocks[0], blocks[1:]
+        self.got = line_hops(lambda step: blocks[step])
+
+    def total(self, *earlier):
+        total = after(self.own, *earlier).astype(jnp.float32)
+        for hop in self.got:
             total = total + hop.astype(jnp.float32)
         return total
 
@@ -406,18 +415,6 @@
     where = jnp.stack([zi, xi, ci, yi]).astype(jnp.int32)
     rows = width // 32
 
-    def whole_latent(array):
-        own = lax.dynamic_index_in_dim(array, yi, 0, False)
-        other = lax.dynamic_index_in_dim(array, 1 - yi, 0, False)
-        return jnp.concatenate([own, swap(other, "y")])
-
-    def half_latents(array):
-        back = swap(array[half_rows:], "y")
-        own = array[:half_rows]
-        first = jnp.where(yi == 0, own, back)
-        second = jnp.where(yi == 0, back, own)
-        return jnp.stack([first, second])
-
     def exchange(array):
         return lax.all_to_all(array, ALL, 0, 0, tiled=True)
 
@@ -439,45 +436,49 @@
         [qkv_rows[:, i * width : (i + 1) * width] for i in range(3)]
         + [proj_weight.reshape(rows, width)]
     )
-    unit_a = lax.all_to_all(quarters, ("c", "y"), 0, 0, tiled=True).reshape(4 * rows, width)
-    line_a0 = line_gather(unit_a[:64])
-    line_a1 = line_gather(after(unit_a[64:], line_a0))
+    up_quarters = up_weight.reshape(rows, 8, 4, 144).transpose(2, 0, 1, 3).reshape(4, rows, width)
+    units = lax.all_to_all(
+        jnp.concatenate([quarters, up_quarters], axis=1), ("c", "y"), 0, 0, tiled=True
+    )
+    unit_a = units[:, :rows].reshape(4 * rows, width)
+    unit_u = units[:, rows:].reshape(4 * rows, width)
+    unit_d = down_weight.reshape(4 * rows, width)
+    hops_a = line_hops(lambda step: unit_a)
+    other_half = after(lax.dynamic_index_in_dim(latent_in, 1 - yi, 0, False), unit_a)
+    half_received = swap(other_half, "y")
+    line_a = jnp.stack([after(unit_a, half_received), *hops_a])
+    plane_a = plane_gather(line_a)
+    unit_u = after(unit_u, line_a)
+    hops_u = line_hops(lambda step: unit_u)
     own_condition = lax.dynamic_index_in_dim(conditioning, yi, 0, False)
-    small = to_all(jnp.concatenate([bias_pack, own_condition]))
+    small = to_all(after(jnp.concatenate([bias_pack, own_condition]), line_a))
     bias_share = bias_pack.shape[0]
     biases = small[:, :bias_share].reshape(-1).astype(jnp.float32)
     conditions = small[:, bias_share:].astype(jnp.float32)
-    tokens_low = whole_latent(latent_in)
     silu_all = jax.nn.silu(conditions).astype(jnp.bfloat16)
     silu_cut = lax.dynamic_slice(silu_all, (0, device * rows), (32, rows))
     ada_rows = ada_weight.reshape(rows, 6 * width)
-    shares = exchange(jnp.dot(silu_cut, ada_rows, preferred_element_type=jnp.float32))
-    modulations = jnp.sum(shares, axis=0, keepdims=True) + biases[: 6 * width]
-    shift_attention, scale_attention, gate_attention, shift_feed, scale_feed, gate_feed = jnp.split(
-        modulations, 6, axis=1
-    )
-
-    up_quarters = up_weight.reshape(rows, 8, 4, 144).transpose(2, 0, 1, 3).reshape(4, rows, width)
-    unit_u = lax.all_to_all(after(up_quarters, unit_a), ("c", "y"), 0, 0, tiled=True)
-    unit_u = unit_u.reshape(4 * rows, width)
-    unit_d = down_weight.reshape(4 * rows, width)
-
-    plane_a0 = plane_gather(line_a0)
-    core_a0 = [swap(p, "c") for p in (line_a0, *plane_a0)]
-    line_u = line_gather(after(unit_u, line_a1))
-    corner_a0 = corner_gather(*plane_a0)
-    plane_a1 = plane_gather(after(line_a1, *plane_a0))
-    core_a0 += [swap(p, "c") for p in corner_a0]
-    core_a1 = [swap(p, "c") for p in (line_a1, *plane_a1)]
-    corner_a1 = corner_gather(*plane_a1)
-    core_a1 += [swap(p, "c") for p in corner_a1]
-    pieces_0, places_0 = with_core((line_a0, *plane_a0, *corner_a0), core_a0)
-    pieces_1, places_1 = with_core((line_a1, *plane_a1, *corner_a1), core_a1, 64)
-    attention_matrix = assemble(
-        pieces_0 + pieces_1, places_0 + places_1, where, "columns", 4 * rows
-    )
-    plane_u = plane_gather(after(line_u, *corner_a1))
-    line_d = line_gather(after(unit_d, line_u))
+    shares = jnp.dot(silu_cut, ada_rows, preferred_element_type=jnp.float32)
+    first_shares, later_shares = shares[:, : 2 * width], shares[:, 2 * width :]
+    modulations = jnp.sum(exchange(first_shares), axis=0, keepdims=True)
+    modulations = modulations + biases[: 2 * width]
+    shift_attention, scale_attention = jnp.split(modulations, 2, axis=1)
+    own_half = lax.dynamic_index_in_dim(latent_in, yi, 0, False)
+    tokens_low = jnp.concatenate([own_half, half_received])
+    tokens = tokens_low.astype(jnp.float32)
+    normed = norm_modulate(tokens, shift_attention, scale_attention).astype(jnp.bfloat16)
+    line_a, plane_a, hops_u = lax.optimization_barrier((line_a, plane_a, hops_u))
+    corner_a = corner_gather(*plane_a)
+    core_a = [swap(p, "c") for p in (line_a, *plane_a)]
+    line_u = jnp.stack([unit_u, *hops_u])
+    unit_d = after(unit_d, line_u, *core_a)
+    hops_d = line_hops(lambda step: unit_d)
+    corner_a = after(corner_a, unit_d)
+    core_a.append(swap(corner_a, "c"))
+    line_u = after(line_u, core_a[3])
+    plane_u = plane_gather(line_u)
+    pieces, places = with_core((line_a, *plane_a, corner_a), core_a)
+    attention_matrix = assemble(after(pieces, line_u, unit_d), places, where, "columns", 4 * rows)
     qkv_matrix = attention_matrix[:, : 3 * width]
     proj_matrix = attention_matrix[:, 3 * width :]
 
@@ -487,145 +488,211 @@
     up_bias = biases[9 * width : 9 * width + FF].reshape(8, 4, 144).transpose(1, 0, 2).reshape(-1)
     down_bias = biases[9 * width + FF :]
 
-    tokens = tokens_low.astype(jnp.float32)
-    normed = norm_modulate(tokens, shift_attention, scale_attention).astype(jnp.bfloat16)
+    later_modulations = jnp.sum(
+        exchange(after(later_shares, attention_matrix)), axis=0, keepdims=True
+    )
+    later_modulations = later_modulations + biases[2 * width : 6 * width]
+    gate_attention, shift_feed, scale_feed, gate_feed = jnp.split(later_modulations, 4, axis=1)
     projected = jnp.dot(normed, qkv_matrix, preferred_element_type=jnp.float32)
     queries = (projected[:, :width] + query_bias).astype(jnp.bfloat16)
     keys = projected[:, width : 2 * width].astype(jnp.bfloat16)
     values = (projected[:, 2 * width :] + value_bias).astype(jnp.bfloat16)
-    part_one = attn_fwd(queries, keys, values, (0, 8))
-
-    plane_u = [after(p, *part_one) for p in plane_u]
+    line_d = jnp.stack([after(unit_d, values), *hops_d])
+    plane_u = after(plane_u, line_d)
     corner_u = corner_gather(*plane_u)
-    core_u = [swap(p, "c") for p in (after(line_u, *part_one), *plane_u)]
-    plane_d = plane_gather(after(line_d, *plane_u))
-    upstream_low = whole_latent(after(cotangent, *part_one))
-
-    attended, log_total = attn_fwd(queries, keys, values, (8, 8), tuple(part_one))
-    corner_u = [after(p, attended) for p in corner_u]
-    core_u += [swap(p, "c") for p in corner_u]
-    branch = jnp.dot(attended, proj_matrix, preferred_element_type=jnp.float32) + proj_bias
+    core_u = [swap(p, "c") for p in (after(line_u, line_d), *plane_u)]
+    part_one = attn_fwd(after(queries, *plane_u, line_d), keys, values, (0, 8))
+    line_d, corner_u, core_u = after((line_d, corner_u, core_u), *part_one)
+    core_u.append(swap(corner_u, "c"))
+    plane_d = plane_gather(line_d)
+    attended, log_total = attn_fwd(
+        after(queries, line_d, *core_u[:3]), keys, values, (8, 8), tuple(part_one)
+    )
+    branch = (
+        jnp.dot(attended, proj_matrix, preferred_element_type=jnp.float32)
+        + proj_bias
+    )
     middle = tokens + gate_attention * branch
     normed_feed = norm_modulate(middle, shift_feed, scale_feed).astype(jnp.bfloat16)
-    pieces, places = with_core((line_u, *plane_u, *corner_u), core_u)
+    pieces, places = with_core((line_u, *plane_u, corner_u), core_u)
+    plane_d = after(plane_d, normed_feed)
+    corner_d = corner_gather(*plane_d)
+    core_d = [swap(p, "c") for p in (after(line_d, normed_feed), *plane_d)]
     up_matrix = assemble(
-        [after(p, normed_feed) for p in pieces], places, where, "columns", 4 * rows
-    )
-    plane_d = [after(p, up_matrix) for p in plane_d]
-    corner_d = corner_gather(*plane_d)
-    core_d = [swap(p, "c") for p in (after(line_d, up_matrix), *plane_d)]
-
+        after(pieces, normed_feed, *plane_d), places, where, "columns", 4 * rows
+    )
+    other_cotangent = after(lax.dynamic_index_in_dim(cotangent, 1 - yi, 0, False), corner_d)
+    cotangent_received = swap(other_cotangent, "y")
+    core_d.append(swap(corner_d, "c"))
+    up_matrix = after(up_matrix, *core_d[:3], corner_d, other_cotangent)
     before = jnp.dot(normed_feed, up_matrix, preferred_element_type=jnp.float32) + up_bias
     activated = gelu_tanh(before).astype(jnp.bfloat16)
-    corner_d = [after(p, activated) for p in corner_d]
-    core_d += [swap(p, "c") for p in corner_d]
-    pieces, places = with_core((line_d, *plane_d, *corner_d), core_d)
-    down_matrix = assemble(
-        [after(p, activated) for p in pieces], places, where, "rows", 4 * rows
-    )
-    upstream = upstream_low.astype(jnp.float32)
-    d_feed = (gate_feed * upstream).astype(jnp.bfloat16)
-
+    activated, core_d[3] = lax.optimization_barrier((activated, core_d[3]))
+    own_cotangent = lax.dynamic_index_in_dim(cotangent, yi, 0, False)
     def pick(array, core):
         return lax.dynamic_slice_in_dim(array, core * 2 * width, 2 * width, 1)
 
-    down_sent = over_tokens(pick(activated, 1 - ci), d_feed).astype(jnp.bfloat16)
+    pieces, places = with_core((line_d, *plane_d, corner_d), core_d)
+    down_matrix = assemble(after(pieces, activated), places, where, "rows", 4 * rows)
+    feed_out = jnp.dot(activated, down_matrix, preferred_element_type=jnp.float32) + down_bias
+    output_low = (middle + gate_feed * feed_out).astype(jnp.bfloat16)
+    cotangent_received, output_low = lax.optimization_barrier((cotangent_received, output_low))
+    upstream = jnp.concatenate([own_cotangent, cotangent_received]).astype(jnp.float32)
+    d_feed = (gate_feed * upstream).astype(jnp.bfloat16)
+    down_sent = over_tokens(pick(after(activated, output_low), 1 - ci), d_feed)
+    down_sent = down_sent.astype(jnp.bfloat16)
     down_received = swap(down_sent, "c")
-    feed_out = jnp.dot(
-        after(activated, down_sent), down_matrix, preferred_element_type=jnp.float32
-    )
-    feed_out = feed_out + down_bias
-    output_low = (middle + gate_feed * feed_out).astype(jnp.bfloat16)
+    output_received = swap(output_low[half_rows:], "y")
     d_gate_feed = jnp.sum(upstream * feed_out, axis=0, keepdims=True)
-    down_half = over_tokens(pick(after(activated, output_low), ci), d_feed)
-    down_half = add_low(down_half, down_received)
-    down_scatter = ScatterSum(part_rows, xi, yi, zi)
-    down_scatter.corner(down_half)
-    output = half_latents(after(output_low, down_half))
-
-    d_activated = times_transposed(after(d_feed, down_half), down_matrix)
+
+    d_activated = times_transposed(after(d_feed, down_sent), down_matrix)
     unused_gelu, gelu_pull = jax.vjp(gelu_tanh, before)
     d_before = gelu_pull(d_activated)[0].astype(jnp.bfloat16)
-    down_scatter.plane(d_before)
-    up_sent = over_tokens(normed_feed, pick(d_before, 1 - ci)).astype(jnp.bfloat16)
+    up_sent = over_tokens(
+        after(normed_feed, output_received, down_received), pick(d_before, 1 - ci)
+    ).astype(jnp.bfloat16)
     up_received = swap(up_sent, "c")
-    d_normed_feed = times_transposed(after(d_before, up_sent), up_matrix)
-    up_half = over_tokens(normed_feed, pick(after(d_before, d_normed_feed), ci))
-    up_half = add_low(up_half, up_received)
-    up_scatter = ScatterSum(part_columns, xi, yi, zi)
-    up_scatter.corner(up_half)
-    down_scatter.line(up_half)
+    down_half = over_tokens(pick(after(activated, up_sent), ci), d_feed)
+    down = ScatterSum(part_rows, add_low(down_half, down_received))
+    down.corner()
+    d_normed_feed = times_transposed(after(d_before, *down.sent, up_received), up_matrix)
+    down.plane(d_normed_feed)
+    up_half = over_tokens(after(normed_feed, *down.sent), pick(d_before, ci))
+    up = ScatterSum(part_columns, add_low(up_half, up_received))
+    up.corner()
     unused_norm, norm_pull = jax.vjp(norm_modulate, middle, shift_feed, scale_feed)
-    d_middle_part, d_shift_feed, d_scale_feed = norm_pull(after(d_normed_feed, up_half))
+    d_middle_part, d_shift_feed, d_scale_feed = norm_pull(
+        after(d_normed_feed, *up.sent)
+    )
     d_middle = upstream + d_middle_part
     d_gate_attention = jnp.sum(d_middle * branch, axis=0, keepdims=True)
     d_branch = (gate_attention * d_middle).astype(jnp.bfloat16)
-    d_attended = times_transposed(d_branch, proj_matrix).astype(jnp.bfloat16)
-    up_scatter.plane(d_attended)
+    d_attended = times_transposed(after(d_branch, down.got[0]), proj_matrix).astype(jnp.bfloat16)
+    mods_early = jnp.concatenate([d_gate_attention, d_shift_feed, d_scale_feed, d_gate_feed], 1)
+    mods_early = mods_early.astype(jnp.bfloat16)
+    early_every = to_all(mods_early[0])
+    down.line(d_attended)
+    up.plane(d_attended)
     log_rows = log_total[:, :H].T
-    part_one = attn_bwd(
-        queries, keys, values, after(d_attended, up_scatter.half), log_rows, (0, 8)
-    )
-    up_scatter.line(*part_one)
-    d_queries, d_keys, d_values = attn_bwd(
-        queries, keys, values, d_attended, log_rows, (8, 8), tuple(part_one)
-    )
-    proj_grad = over_tokens(attended, d_branch)
-    d_projected = jnp.concatenate([d_queries, d_keys, d_values], axis=1)
-    qkv_grad = over_tokens(normed, d_projected)
-    first_half = qkv_grad[:, : 2 * width]
-    second_half = jnp.concatenate([qkv_grad[:, 2 * width :], proj_grad], axis=1)
-    sent = jnp.where(ci == 0, second_half, first_half).astype(jnp.bfloat16)
-    received = swap(sent, "c")
-    d_normed = times_transposed(after(d_projected, sent), qkv_matrix)
-    attention_half = add_low(jnp.where(ci == 0, first_half, second_half), received)
-    attention_scatter = ScatterSum(part_columns, xi, yi, zi)
-    attention_scatter.corner(attention_half)
+    gradients = attn_bwd(
+        queries,
+        keys,
+        values,
+        after(d_attended, *up.sent, *down.sent, mods_early),
+        log_rows,
+        (0, 8),
+    )
+
+    def attention_terms(start, stop, core, *earlier):
+        d_q, d_k, d_v, d_b = [a[:, start:stop] for a in (*gradients, d_branch)]
+        left = after(normed, *earlier)
+        first = over_tokens(left, jnp.where(core == 0, d_q, d_v))
+        second = over_tokens(
+            jnp.where(core == 0, left, attended), jnp.where(core == 0, d_k, d_b)
+        )
+        return jnp.concatenate([first, second])
+
+    left_sent = attention_terms(
+        0, 512, 1 - ci, *gradients, *down.got, *up.got, early_every
+    ).astype(jnp.bfloat16)
+    left_received = swap(left_sent, "c")
+    up.line(left_sent)
+    left_half = attention_terms(0, 512, ci, left_sent, *up.sent)
+    left = ScatterSum(part_rows, add_low(left_half, left_received))
+    left.corner()
+    down_sum = down.total(left_half)
+    gradients = attn_bwd(
+        queries,
+        keys,
+        values,
+        after(d_attended, *left.sent, down_sum),
+        log_rows,
+        (8, 4),
+        tuple(gradients),
+    )
+    gradients = after(tuple(gradients), *left.got, *up.got)
+    left.plane(*gradients)
+    up_terms = up.total(*gradients).reshape(4, rows, width)
+    up_sum = lax.all_to_all(up_terms, ("c", "y"), 0, 0, tiled=True)
+    gradients = attn_bwd(
+        queries,
+        keys,
+        values,
+        after(d_attended, *left.sent, up_terms),
+        log_rows,
+        (12, 4),
+        tuple(gradients),
+    )
+    gradients = after(tuple(gradients), *left.got, up_sum)
+    d_queries, d_keys, d_values = gradients
+    left.line(*gradients)
+    right_sent = attention_terms(512, width, 1 - ci, *left.sent).astype(jnp.bfloat16)
+    right_received = swap(right_sent, "c")
+    right_half = attention_terms(512, width, ci, right_sent)
+    right = ScatterSum(part_rows, add_low(right_half, right_received))
+    right.corner()
+    d_projected = jnp.concatenate(after((d_queries, d_keys, d_values), *right.sent), axis=1)
+    d_normed = times_transposed(d_projected, qkv_matrix)
+    right.plane(d_normed)
     unused_first, first_pull = jax.vjp(norm_modulate, tokens, shift_attention, scale_attention)
-    d_tokens_part, d_shift_attention, d_scale_attention = first_pull(d_normed)
+    d_tokens_part, d_shift_attention, d_scale_attention = first_pull(after(d_normed, *right.sent))
     grad_low = (d_middle + d_tokens_part).astype(jnp.bfloat16)
-    attention_scatter.plane()
-    attention_scatter.line()
-
-    d_mods = jnp.concatenate(
+    quarter_rows = half_rows // 2
+    grad_first = swap(grad_low[half_rows : half_rows + quarter_rows], "y")
+    mods_late = jnp.concatenate([d_shift_attention, d_scale_attention], axis=1)
+    mods_late = mods_late.astype(jnp.bfloat16)
+    left_terms = left.total(grad_low)
+    right.line(grad_low, mods_late, left_terms)
+    late_every = to_all(after(mods_late, *right.sent)[0])
+    bias_terms = jnp.concatenate(
         [
-            d_shift_attention,
-            d_scale_attention,
-            d_gate_attention,
-            d_shift_feed,
-            d_scale_feed,
-            d_gate_feed,
-        ],
-        axis=1,
-    ).astype(jnp.bfloat16)
-    every_mods = to_all(d_mods[0])
-    grad_input = half_latents(grad_low)
-    grad_ada = over_tokens(silu_cut, every_mods).reshape(-1)
-    d_silu_rows = times_transposed(every_mods, ada_rows)
-    d_silu = exchange(jnp.repeat(d_silu_rows.reshape(16, 1, 2, rows), 2, axis=1).reshape(32, 2, rows))
-    d_silu = d_silu.transpose(1, 0, 2).reshape(2, width)
+            mods_late[0].astype(jnp.float32),
+            mods_early[0].astype(jnp.float32),
+            jnp.sum(after(d_queries, *right.sent), axis=0, dtype=jnp.float32),
+            jnp.sum(after(d_values, *right.sent), axis=0, dtype=jnp.float32),
+            jnp.sum(after(d_branch, *right.sent), axis=0, dtype=jnp.float32),
+            jnp.sum(after(d_before, *right.sent), axis=0, dtype=jnp.float32)
+            .reshape(4, 8, 144)
+            .transpose(1, 0, 2)
+            .reshape(-1),
+            jnp.sum(after(d_feed, *right.sent), axis=0, dtype=jnp.float32),
+        ]
+    )
+    grad_last = swap(after(grad_low, grad_first)[half_rows + quarter_rows :], "y")
+    late_every, early_every = after((late_every, early_every), *right.sent)
+
+    late_width = late_every.shape[1]
+    grad_ada = jnp.concatenate(
+        [over_tokens(silu_cut, late_every), over_tokens(silu_cut, early_every)], axis=1
+    ).reshape(-1)
+    d_silu_rows = times_transposed(late_every, ada_rows[:, :late_width])
+    d_silu_rows = d_silu_rows + times_transposed(early_every, ada_rows[:, late_width:])
+    d_silu_parts = jnp.repeat(d_silu_rows.reshape(16, 1, 2, rows), 2, axis=1)
+    parts = exchange(
+        jnp.concatenate([d_silu_parts.reshape(32, 2 * rows), bias_terms.reshape(32, -1)], axis=1)
+    )
+    d_silu = parts[:, : 2 * rows].reshape(32, 2, rows).transpose(1, 0, 2).reshape(2, width)
+    grad_bias = jnp.sum(parts[:, 2 * rows :], axis=0)
     unused_silu, silu_pull = jax.vjp(jax.nn.silu, conditioning.astype(jnp.float32))
     grad_cond = silu_pull(d_silu)[0].astype(jnp.bfloat16)
 
-    up_bias_grad = jnp.sum(d_before, axis=0, dtype=jnp.float32)
-    bias_terms = jnp.concatenate(
-        [
-            d_mods[0].astype(jnp.float32),
-            jnp.sum(d_queries, axis=0, dtype=jnp.float32),
-            jnp.sum(d_values, axis=0, dtype=jnp.float32),
-            jnp.sum(d_branch, axis=0, dtype=jnp.float32),
-            up_bias_grad.reshape(4, 8, 144).transpose(1, 0, 2).reshape(-1),
-            jnp.sum(d_feed, axis=0, dtype=jnp.float32),
-        ]
-    )
-    grad_bias = jnp.sum(exchange(bias_terms.reshape(32, -1)), axis=0)
-
-    up_sum = up_scatter.total().reshape(4, rows, width)
-    up_sum = lax.all_to_all(up_sum, ("c", "y"), 0, 0, tiled=True)
-    grad_up = up_sum.reshape(4, rows, 8, 144).transpose(1, 2, 0, 3).reshape(-1)
-    grad_down = down_scatter.total().reshape(-1)
-    sums = attention_scatter.total().reshape(4, rows, width)
+    right_terms = right.total(d_silu_rows, grad_first)
+    sums = jnp.concatenate([left_terms, right_terms], axis=1).reshape(4, rows, width)
     sums = lax.all_to_all(sums, ("c", "y"), 0, 0, tiled=True)
+    down_sum, output_low, output_received, grad_last = after(
+        (down_sum, output_low, output_received, grad_last), right_terms
+    )
+    grad_received = jnp.concatenate([grad_first, grad_last])
+    grad_up = after(up_sum, right_terms).reshape(4, rows, 8, 144).transpose(1, 2, 0, 3).reshape(-1)
+    def both_halves(own_rows, received):
+        first = jnp.where(yi == 0, own_rows, received)
+        second = jnp.where(yi == 0, received, own_rows)
+        return jnp.stack([first, second])
+
+    output = both_halves(output_low[:half_rows], output_received)
+    grad_input = both_halves(grad_low[:half_rows], grad_received)
+
+    grad_down = down_sum.reshape(-1)
     grad_qkv = jnp.concatenate([sums[0], sums[1], sums[2]], axis=1).reshape(-1)
     grad_proj = sums[3].reshape(-1)
     return (

time: 881 us -> 724 us (0.82)
  starting transfers between devices: 160 us -> 103 us
  waiting for transfers between devices: 144 us -> 94.7 us
  local copies, waits for them, and re-layouts: 103 us -> 66.3 us
  Pallas kernels: 136 us -> 150 us
  blocking collectives: 10.3 us -> 0 us
    ppermute x21 -> x28, waiting for transfers between devices: 60.3 us -> 17.4 us  [the longest x7 11.5 us: corner_swap(): return lax.ppermute(array, ('x', 'c', 'y'), pairs)]
    ppermute x55 -> x35, waiting for transfers between devices: 62.9 us -> 38.1 us  [swap(): return lax.ppermute(array, axis, SWAP)]
    ppermute x55 -> x35, starting transfers between devices: 50 us -> 26.3 us  [swap(): return lax.ppermute(array, axis, SWAP)]
    slice x18 -> x7, local copies, waits for them, and re-layouts: 20.6 us -> 2.09 us  [the longest x1 1.09 us: local_pairs(): output_received = swap(output_low[half_rows:], 'y')]
    select_n x0 -> x7, other arithmetic: none -> 17.2 us  [the longest x3 8.45 us: plane(): to_x = jnp.where(even, to_x, add_low(to_x, got))]
    ppermute x21 -> x28, starting transfers between devices: 49.9 us -> 33 us  [the longest x21 25.9 us: line_hops(): lax.ppermute(block_of(step), 'z', [(i, i ^ step) for i in range(4)])]
    all_to_all x5 -> x6, waiting for transfers between devices: 17.2 us -> 32.8 us  [exchange(): return lax.all_to_all(array, ALL, 0, 0, tiled=True)]
    all_to_all x5 -> x6, starting transfers between devices: 44.7 us -> 30 us  [exchange(): return lax.all_to_all(array, ALL, 0, 0, tiled=True)]
  transfers between devices with their start and end apart: 84 -> 72, of which waited for: 18 -> 12; matrix products, arithmetic and copies ran while one was open for 38% -> 43% of each run, Pallas kernels for 16% -> 21%
where the time goes in v2:
time: 724 us; the launch traced here: 716 us
  matrix products  195 us (27%)
  Pallas kernels  150 us (21%)
  other arithmetic  104 us (14%)
  starting transfers between devices  103 us (14%)
  waiting for transfers between devices  94.7 us (13%)
  local copies, waits for them, and re-layouts  66.3 us (9%)
    pallas_call x3, Pallas kernels, attn_bwd(): pl.pallas_call(functools.partial(attn_bwd_kernel, tile=tile, first=first)...  87.9 us
    dot_general x6, matrix products, times_transposed(): lax.dot_general(left, right, (((1,), (1,)), ((), ())), preferred_element_...  66.5 us
    dot_general x14, matrix products, over_tokens(): lax.dot_general(left, right, (((0,), (0,)), ((), ())), preferred_element_...  60.7 us
    ppermute x35, waiting for transfers between devices, swap(): return lax.ppermute(array, axis, SWAP)  38.1 us
    pallas_call x2, Pallas kernels, attn_fwd(): pl.pallas_call(functools.partial(attn_fwd_kernel, tile=tile, first=first)...  34.9 us
    all_to_all x6, waiting for transfers between devices, exchange(): return lax.all_to_all(array, ALL, 0, 0, tiled=True)  32.8 us
    all_to_all x6, starting transfers between devices, exchange(): return lax.all_to_all(array, ALL, 0, 0, tiled=True)  30 us
    pallas_call x3, Pallas kernels, assemble(): pl.pallas_call(body, grid_spec=pltpu.PrefetchScalarGridSpec(num_scalar_pr...  27.4 us
  transfers between devices with their start and end apart: 72, of which 12 were waited for; matrix products, arithmetic and copies ran while one was open for 43% of the time, Pallas kernels for 21%

profile of v2, /device:TPU:1, one launch (start us, length us, event | category | flops | bytes accessed | tf_op | source)
XLA Modules:
  0.0 715.8 jit_solution(16155214362772884197)
XLA Ops:
  11.7 6.5 all-to-all-done
  23.3 21.8 %collective-permute-done = bf16[512,1152]{1,0:T(8,128)(2,1)S(1)} collective-permute-done((bf16[512,1152]{1,0:T(8,128)(2,1)}, bf16[512,1152]{1,0:T(8,128)(2,1)S(1)}, u32[]{:S(2)}, u32[]{:S(2)}) %collective-permute-start) | collective-permute-done | bytes 1179680 | tf_op jit(solution)/shard_map/ppermute | solution.py:311
  45.1 5.8 collective-permute-done.2
  65.1 5.5 all-to-all-start.1
  71.8 21.5 %all-to-all-done.1 = bf16[32,2,828]{2,1,0:T(2,128)(2,1)S(1)} async-done(((bf16[32,2,828]{2,1,0:T(2,128)(2,1)}), bf16[32,2,828]{2,1,0:T(2,128)(2,1)S(1)}, u32[]{:S(2)}, u32[]{:S(2)}) %all-to-all-start.1) | async-done | bytes 106016 | tf_op jit(solution)/shard_map/all_to_all | solution.py:419
  107.3 9.5 %collective-permute-done.9.refs_3_ = bf16[4,144,1152]{2,1,0:T(8,128)(2,1)} collective-permute-done((bf16[4,144,1152]{2,1,0:T(8,128)(2,1)}, bf16[4,144,1152]{2,1,0:T(8,128)(2,1)}, u32[]{:S(2)}, u32[]{:S(2)}) %collective-permute-start.9) | collective-permute-done | bytes 1327136 | tf_op jit(solution)/shard_map/ppermute | solution.py:330
  128.6 8.9 %assemble_columns.2 = bf16[1152,4608]{1,0:T(8,128)(2,1)} custom-call(s32[4]{0:T(128)} %pad_add_fusion.where_ref, bf16[4,144,1152]{2,1,0:T(8,128)(2,1)} %pad_maximum_fusion.7.refs_0_, bf16[4,144,1152]{2,1,0:T(8,128)(2,1)} %collective-permute-done.4.refs_1_, bf16[4,144,1152]{2,1,0:T(8,128)(2,1)} %collective-permute-done.5.refs_2_, ...), custom_call_target="tpu_custom_call" | custom-call | bytes 21233664 | tf_op jit(solution)/shard_map/assemble_columns/pallas_call | solution.py:288
  137.6 14.8 %fusion.17 = f32[1024,3456]{1,0:T(8,128)} fusion(bf16[1024,1152]{1,0:T(8,128)(2,1)S(1)} %fusion.23, bf16[1152,4608]{1,0:T(8,128)(2,1)} %assemble_columns.2), kind=kOutput, calls=%fused_computation.35 | convolution fusion | flops 8153726976 | bytes 24477696 | tf_op jit(solution)/shard_map/dot_general | solution.py:496
  158.0 6.7 fusion.30
  179.6 17.1 %attention_forward.2 = (bf16[1024,1152]{1,0:T(8,128)(2,1)S(1)}, f32[1024,128]{1,0:T(8,128)S(1)}) custom-call(bf16[1024,1152]{1,0:T(8,128)(2,1)S(1)} %copy-done.1, bf16[1024,1152]{1,0:T(8,128)(2,1)S(1)} %slice.317.k_ref, bf16[1024,1152]{1,0:T(8,128)(2,1)S(1)} %copy-done.2), custom_call_target="tpu_custom_call" | custom-call | flops 8589934592 | bytes 9437184 | tf_op jit(solution)/shard_map/attention_forward/pallas_call | solution.py:161
  198.0 17.7 %attention_forward.3 = (bf16[1024,1152]{1,0:T(8,128)(2,1)S(1)}, f32[1024,128]{1,0:T(8,128)S(1)}) custom-call(bf16[1024,1152]{1,0:T(8,128)(2,1)S(1)} %copy-done.1, bf16[1024,1152]{1,0:T(8,128)(2,1)S(1)} %slice.317.k_ref, bf16[1024,1152]{1,0:T(8,128)(2,1)S(1)} %copy-done.2, bf16[1024,1152]{1,0:T(8,128)(2,1)S(1)} %get-tuple-element.158.refs_0_, ...), custom_call_target="tpu_custom_call" | custom-call | flops 8589934592 | bytes 9437184 | tf_op jit(solution)/shard_map/attention_forward/pallas_call | solution.py:161
  215.8 8.3 %fusion.135 = (f32[1024]{0:T(1024)S(1)}, f32[1024,1152]{1,0:T(8,128)S(1)}, f32[1024,1152]{1,0:T(8,128)}) fusion(f32[1152]{0:T(1024)S(1)} %get-tuple-element.264, bf16[512,1152]{1,0:T(8,128)(2,1)S(1)} %copy-done.10, bf16[512,1152]{1,0:T(8,128)(2,1)S(1)} %copy-done.7, f32[1152]{0:T(1024)S(1)} %copy-done.80, bf16[1024,1152]{1,0:T(8,128)(2,1)S(1)} %get-tuple-element.165, ...), kind=kOutput, calls=%fused_computation.287 | convolution fusion | flops 2727345152 | bytes 16823296 | tf_op jit(solution)/shard_map/dot_general | solution.py:512
  235.7 9.7 %assemble_columns.3 = bf16[1152,4608]{1,0:T(8,128)(2,1)} custom-call(s32[4]{0:T(128)} %pad_add_fusion.where_ref, bf16[4,144,1152]{2,1,0:T(8,128)(2,1)} %pad_maximum_fusion.8.refs_0_, bf16[4,144,1152]{2,1,0:T(8,128)(2,1)} %collective-permute-done.17.refs_1_, bf16[4,144,1152]{2,1,0:T(8,128)(2,1)} %collective-permute-done.18.refs_2_, ...), custom_call_target="tpu_custom_call" | custom-call | bytes 21233664 | tf_op jit(solution)/shard_map/assemble_columns/pallas_call | solution.py:288
  250.1 23.6 %multiply_convert_fusion = (bf16[1024,4608]{1,0:T(8,128)(2,1)}, f32[1024,4608]{1,0:T(8,128)}) fusion(f32[4608]{0:T(1024)S(1)} %reshape.367, bf16[1024,1152]{1,0:T(8,128)(2,1)} %add_convert_fusion.5, bf16[1152,4608]{1,0:T(8,128)(2,1)} %assemble_columns.3), kind=kOutput, calls=%fused_computation.11 | convolution fusion | flops 10918821888 | bytes 41306112 | tf_op jit(solution)/shard_map/dot_general | solution.py:528
  273.7 8.9 %assemble_rows.1 = bf16[4608,1152]{1,0:T(8,128)(2,1)} custom-call(s32[4]{0:T(128)} %pad_add_fusion.where_ref, bf16[4,144,1152]{2,1,0:T(8,128)(2,1)} %pad_maximum_fusion.9.refs_0_, bf16[4,144,1152]{2,1,0:T(8,128)(2,1)} %collective-permute-done.24.refs_1_, bf16[4,144,1152]{2,1,0:T(8,128)(2,1)} %collective-permute-done.25.refs_2_, ...), custom_call_target="tpu_custom_call" | custom-call | bytes 21233664 | tf_op jit(solution)/shard_map/assemble_rows/pallas_call | solution.py:288
  282.6 19.6 %add_convert_fusion.4 = (bf16[1024,1152]{1,0:T(8,128)(2,1)S(1)}, f32[1024,1152]{1,0:T(8,128)}) fusion(f32[1024,1152]{1,0:T(8,128)S(1)} %bitcast.195, f32[1152]{0:T(1024)S(1)} %get-tuple-element.262, f32[1152]{0:T(1024)S(1)} %get-tuple-element.317, bf16[1024,4608]{1,0:T(8,128)(2,1)} %get-tuple-element.195, bf16[4608,1152]{1,0:T(8,128)(2,1)} %assemble_rows.1), kind=kOutput, calls=%fused_computation.71 | convolution fusion | flops 10876354560 | bytes 31859712 | tf_op jit(solution)/shard_map/dot_general | solution.py:537
  303.3 8.3 %convolution_convert_fusion.1 = bf16[2304,1152]{1,0:T(8,128)(2,1)} fusion(bf16[1024,1152]{1,0:T(8,128)(2,1)S(1)} %fusion.27, bf16[1024,4608]{1,0:T(8,128)(2,1)S(1)} %copy-done.85, s32[]{:T(128)S(6)} %select_n.239), kind=kOutput, calls=%fused_computation.13 | convolution fusion | flops 5438472192 | bytes 12386308 | tf_op jit(solution)/shard_map/dot_general | solution.py:425
  314.0 28.5 %fusion.3 = bf16[1024,4608]{1,0:T(8,128)(2,1)} fusion(f32[1024,4608]{1,0:T(8,128)} %get-tuple-element.323, f32[4608]{0:T(1024)S(1)} %reshape.367, bf16[1024,1152]{1,0:T(8,128)(2,1)S(1)} %copy-done.29, bf16[4608,1152]{1,0:T(8,128)(2,1)S(1)} %bitcast.204), kind=kOutput, calls=%fused_computation.7 | convolution fusion | flops 10989600768 | bytes 41306112 | tf_op jit(solution)/shard_map/dot_general | solution.py:430
  342.5 10.5 %convolution_convert_fusion = bf16[1152,2304]{1,0:T(8,128)(2,1)} fusion(bf16[1024,1152]{1,0:T(8,128)(2,1)} %add_convert_fusion.5, bf16[1024,4608]{1,0:T(8,128)(2,1)} %fusion.3, s32[]{:T(128)S(6)} %select_n.239), kind=kOutput, calls=%fused_computation.12 | convolution fusion | flops 5438472192 | bytes 12386308 | tf_op jit(solution)/shard_map/dot_general | solution.py:425
  353.8 9.6 %add_convert_fusion.1 = bf16[2304,1152]{1,0:T(8,128)(2,1)S(1)} fusion(bf16[2304,1152]{1,0:T(8,128)(2,1)} %collective-permute-done.33, bf16[1024,1152]{1,0:T(8,128)(2,1)S(1)} %copy-done.29, bf16[1024,4608]{1,0:T(8,128)(2,1)} %get-tuple-element.195, s32[]{:T(128)S(6)} %select_n.240), kind=kOutput, calls=%fused_computation.15 | convolution fusion | flops 5443780608 | bytes 17694724 | tf_op jit(solution)/shard_map/dot_general | solution.py:425
  364.3 16.1 %fusion.140 = f32[1024,1152]{1,0:T(8,128)S(1)} fusion(bf16[1024,4608]{1,0:T(8,128)(2,1)S(1)} %copy-done.27, bf16[1152,4608]{1,0:T(8,128)(2,1)} %assemble_columns.3), kind=kOutput, calls=%fused_computation.292 | convolution fusion | flops 10871635968 | bytes 24772608 | tf_op jit(solution)/shard_map/dot_general | solution.py:430
  383.8 7.8 %add_convert_fusion = bf16[1152,2304]{1,0:T(8,128)(2,1)S(1)} fusion(bf16[1152,2304]{1,0:T(8,128)(2,1)} %collective-permute-done.34, bf16[1024,1152]{1,0:T(8,128)(2,1)S(1)} %copy-done.46, bf16[1024,4608]{1,0:T(8,128)(2,1)S(1)} %copy-done.27, s32[]{:T(128)S(6)} %select_n.240), kind=kOutput, calls=%fused_computation.14 | convolution fusion | flops 5443780608 | bytes 17694724 | tf_op jit(solution)/shard_map/dot_general | solution.py:425
  398.3 6.2 multiply_reduce_fusion.1
  416.4 9.6 %all-to-all-done.4 = bf16[32,2,2304]{2,1,0:T(2,128)(2,1)} async-done(((bf16[32,2,2304]{2,1,0:T(2,128)(2,1)}), bf16[32,2,2304]{2,1,0:T(2,128)(2,1)}, u32[]{:S(2)}, u32[]{:S(2)}) %all-to-all-start.4) | async-done | bytes 294944 | tf_op jit(solution)/shard_map/all_to_all | solution.py:419
  429.0 7.0 convolution_convert_fusion.2.g_ref
  446.7 38.5 %attention_backward.3 = (bf16[1024,1152]{1,0:T(8,128)(2,1)}, bf16[1024,1152]{1,0:T(8,128)(2,1)}, bf16[1024,1152]{1,0:T(8,128)(2,1)}) custom-call(bf16[1024,1152]{1,0:T(8,128)(2,1)} %get-tuple-element.164.q_ref, bf16[1024,1152]{1,0:T(8,128)(2,1)} %copy-done, bf16[1024,1152]{1,0:T(8,128)(2,1)} %get-tuple-element.272.v_ref, ...), custom_call_target="tpu_custom_call" | custom-call | flops 21474836480 | bytes 16515072 | tf_op jit(solution)/shard_map/attention_backward/pallas_call | solution.py:227
  507.2 24.9 %attention_backward.4 = (bf16[1024,1152]{1,0:T(8,128)(2,1)}, bf16[1024,1152]{1,0:T(8,128)(2,1)}, bf16[1024,1152]{1,0:T(8,128)(2,1)}) custom-call(bf16[1024,1152]{1,0:T(8,128)(2,1)} %get-tuple-element.164.q_ref, bf16[1024,1152]{1,0:T(8,128)(2,1)} %copy-done, bf16[1024,1152]{1,0:T(8,128)(2,1)} %get-tuple-element.272.v_ref, ...), custom_call_target="tpu_custom_call" | custom-call | flops 10737418240 | bytes 16515072 | tf_op jit(solution)/shard_map/attention_backward/pallas_call | solution.py:227
  544.7 24.5 %attention_backward.5 = (bf16[1024,1152]{1,0:T(8,128)(2,1)}, bf16[1024,1152]{1,0:T(8,128)(2,1)}, bf16[1024,1152]{1,0:T(8,128)(2,1)}) custom-call(bf16[1024,1152]{1,0:T(8,128)(2,1)} %get-tuple-element.164.q_ref, bf16[1024,1152]{1,0:T(8,128)(2,1)} %copy-done, bf16[1024,1152]{1,0:T(8,128)(2,1)} %get-tuple-element.272.v_ref, ...), custom_call_target="tpu_custom_call" | custom-call | flops 10737418240 | bytes 16515072 | tf_op jit(solution)/shard_map/attention_backward/pallas_call | solution.py:227
  596.6 14.5 %fusion.6 = f32[1024,1152]{1,0:T(8,128)S(1)} fusion(bf16[1024,1152]{1,0:T(8,128)(2,1)} %get-tuple-element.247, bf16[1024,1152]{1,0:T(8,128)(2,1)} %get-tuple-element.232, bf16[1024,1152]{1,0:T(8,128)(2,1)} %get-tuple-element.246, bf16[1152,4608]{1,0:T(8,128)(2,1)} %assemble_columns.2), kind=kOutput, calls=%fused_computation.16 | convolution fusion | flops 8174960640 | bytes 19759104 | tf_op jit(solution)/shard_map/dot_general | solution.py:430
  628.5 16.1 %collective-permute-done.53 = bf16[256,1152]{1,0:T(8,128)(2,1)S(1)} collective-permute-done((bf16[256,1152]{1,0:T(8,128)(2,1)S(1)}, bf16[256,1152]{1,0:T(8,128)(2,1)S(1)}, u32[]{:S(2)}, u32[]{:S(2)}) %collective-permute-start.53) | collective-permute-done | bytes 589856 | tf_op jit(solution)/shard_map/ppermute | solution.py:311
  654.6 5.9 all-to-all-start.6
  685.0 5.9 all-to-all-start.7
  (511 shorter events, 272.7 us)
Async XLA Ops:
  52.1 41.4 %collective-permute-start.4 = (bf16[4,144,1152]{2,1,0:T(8,128)(2,1)}, bf16[4,144,1152]{2,1,0:T(8,128)(2,1)}, u32[]{:S(2)}, u32[]{:S(2)}) collective-permute-start(bf16[4,144,1152]{2,1,0:T(8,128)(2,1)} %pad_maximum_fusion.7.refs_0_), channel_id=1, source_target_pairs={{0,4},{4,0},{1,5},{5,1},{2,6},{6,2},{3,7},{7,3},{8,12},{12,8},{9,1... | collective-permute-start | bytes 3981320 | tf_op jit(solution)/shard_map/ppermute | solution.py:311
  53.3 40.2 %collective-permute-start.5 = (bf16[4,144,1152]{2,1,0:T(8,128)(2,1)}, bf16[4,144,1152]{2,1,0:T(8,128)(2,1)}, u32[]{:S(2)}, u32[]{:S(2)}) collective-permute-start(bf16[4,144,1152]{2,1,0:T(8,128)(2,1)} %pad_maximum_fusion.7.refs_0_), channel_id=1, source_target_pairs={{0,1},{1,0},{2,3},{3,2},{4,5},{5,4},{6,7},{7,6},{8,9},{9,8},{10,11... | collective-permute-start | bytes 3981320 | tf_op jit(solution)/shard_map/ppermute | solution.py:311
  58.8 34.8 %collective-permute-start.6 = (bf16[144,1152]{1,0:T(8,128)(2,1)S(1)}, bf16[144,1152]{1,0:T(8,128)(2,1)S(1)}, u32[]{:S(2)}, u32[]{:S(2)}) collective-permute-start(bf16[144,1152]{1,0:T(8,128)(2,1)S(1)} %reshape.327), channel_id=1, source_target_pairs={{0,8},{8,0},{16,24},{24,16},{1,9},{9,1},{17,25},{25,17},{2,10},{10... | collective-permute-start | bytes 995336 | tf_op jit(solution)/shard_map/ppermute | solution.py:316
  58.9 34.7 %collective-permute-start.7 = (bf16[144,1152]{1,0:T(8,128)(2,1)S(1)}, bf16[144,1152]{1,0:T(8,128)(2,1)}, u32[]{:S(2)}, u32[]{:S(2)}) collective-permute-start(bf16[144,1152]{1,0:T(8,128)(2,1)S(1)} %reshape.327), channel_id=1, source_target_pairs={{0,16},{8,24},{16,0},{24,8},{1,17},{9,25},{17,1},{25,9},{2,18},{10... | collective-permute-start | bytes 995336 | tf_op jit(solution)/shard_map/ppermute | solution.py:316
  60.7 32.9 %collective-permute-start.8 = (bf16[144,1152]{1,0:T(8,128)(2,1)S(1)}, bf16[144,1152]{1,0:T(8,128)(2,1)}, u32[]{:S(2)}, u32[]{:S(2)}) collective-permute-start(bf16[144,1152]{1,0:T(8,128)(2,1)S(1)} %reshape.327), channel_id=1, source_target_pairs={{0,24},{8,16},{16,8},{24,0},{1,25},{9,17},{17,9},{25,1},{2,26},{10... | collective-permute-start | bytes 995336 | tf_op jit(solution)/shard_map/ppermute | solution.py:316
  122.7 42.1 %collective-permute-start.16 = (bf16[144,1152]{1,0:T(8,128)(2,1)S(1)}, bf16[144,1152]{1,0:T(8,128)(2,1)S(1)}, u32[]{:S(2)}, u32[]{:S(2)}) collective-permute-start(bf16[144,1152]{1,0:T(8,128)(2,1)S(1)} %copy-done.47), channel_id=1, source_target_pairs={{0,24},{8,16},{16,8},{24,0},{1,25},{9,17},{17,9},{25,1},{2,26},{10... | collective-permute-start | bytes 995336 | tf_op jit(solution)/shard_map/ppermute | solution.py:316
  124.7 40.1 %collective-permute-start.15 = (bf16[144,1152]{1,0:T(8,128)(2,1)S(1)}, bf16[144,1152]{1,0:T(8,128)(2,1)S(1)}, u32[]{:S(2)}, u32[]{:S(2)}) collective-permute-start(bf16[144,1152]{1,0:T(8,128)(2,1)S(1)} %copy-done.47), channel_id=1, source_target_pairs={{0,16},{8,24},{16,0},{24,8},{1,17},{9,25},{17,1},{25,9},{2,18},{10... | collective-permute-start | bytes 995336 | tf_op jit(solution)/shard_map/ppermute | solution.py:316
  124.7 40.1 %collective-permute-start.14 = (bf16[144,1152]{1,0:T(8,128)(2,1)S(1)}, bf16[144,1152]{1,0:T(8,128)(2,1)S(1)}, u32[]{:S(2)}, u32[]{:S(2)}) collective-permute-start(bf16[144,1152]{1,0:T(8,128)(2,1)S(1)} %copy-done.47), channel_id=1, source_target_pairs={{0,8},{8,0},{16,24},{24,16},{1,9},{9,1},{17,25},{25,17},{2,10},{10... | collective-permute-start | bytes 995336 | tf_op jit(solution)/shard_map/ppermute | solution.py:316
  126.3 39.9 %collective-permute-start.17 = (bf16[4,144,1152]{2,1,0:T(8,128)(2,1)}, bf16[4,144,1152]{2,1,0:T(8,128)(2,1)}, u32[]{:S(2)}, u32[]{:S(2)}) collective-permute-start(bf16[4,144,1152]{2,1,0:T(8,128)(2,1)} %pad_maximum_fusion.8.refs_0_), channel_id=1, source_target_pairs={{0,4},{4,0},{1,5},{5,1},{2,6},{6,2},{3,7},{7,3},{8,12},{12,8},{9,1... | collective-permute-start | bytes 3981320 | tf_op jit(solution)/shard_map/ppermute | solution.py:311
  127.0 39.2 %collective-permute-start.18 = (bf16[4,144,1152]{2,1,0:T(8,128)(2,1)}, bf16[4,144,1152]{2,1,0:T(8,128)(2,1)}, u32[]{:S(2)}, u32[]{:S(2)}) collective-permute-start(bf16[4,144,1152]{2,1,0:T(8,128)(2,1)} %pad_maximum_fusion.8.refs_0_), channel_id=1, source_target_pairs={{0,1},{1,0},{2,3},{3,2},{4,5},{5,4},{6,7},{7,6},{8,9},{9,8},{10,11... | collective-permute-start | bytes 3981320 | tf_op jit(solution)/shard_map/ppermute | solution.py:311
  196.8 31.7 %collective-permute-start.24 = (bf16[4,144,1152]{2,1,0:T(8,128)(2,1)}, bf16[4,144,1152]{2,1,0:T(8,128)(2,1)}, u32[]{:S(2)}, u32[]{:S(2)}) collective-permute-start(bf16[4,144,1152]{2,1,0:T(8,128)(2,1)} %pad_maximum_fusion.9.refs_0_), channel_id=1, source_target_pairs={{0,4},{4,0},{1,5},{5,1},{2,6},{6,2},{3,7},{7,3},{8,12},{12,8},{9,1... | collective-permute-start | bytes 3981320 | tf_op jit(solution)/shard_map/ppermute | solution.py:311
  247.3 54.9 %collective-permute-start.31 = (bf16[512,1152]{1,0:T(8,128)(2,1)}, bf16[512,1152]{1,0:T(8,128)(2,1)S(1)}, u32[]{:S(2)}, u32[]{:S(2)}) collective-permute-start(bf16[512,1152]{1,0:T(8,128)(2,1)} %get-tuple-element.178), channel_id=1, source_target_pairs={{0,1},{1,0},{2,3},{3,2},{4,5},{5,4},{6,7},{7,6},{8,9},{9,8},{10,11... | collective-permute-start | bytes 3538952 | tf_op jit(solution)/shard_map/ppermute | solution.py:311
  382.7 46.3 %collective-permute-start.36 = (bf16[4,144,1152]{2,1,0:T(8,128)(2,1)}, bf16[4,144,1152]{2,1,0:T(8,128)(2,1)}, u32[]{:S(2)}, u32[]{:S(2)}) collective-permute-start(bf16[4,144,1152]{2,1,0:T(8,128)(2,1)} %get-tuple-element.276), channel_id=1, source_target_pairs={{0,1},{1,0},{2,3},{3,2},{4,5},{5,4},{6,7},{7,6},{8,9},{9,8},{10,11... | collective-permute-start | bytes 3981320 | tf_op jit(solution)/shard_map/ppermute | solution.py:311
  383.4 52.6 %collective-permute-start.37 = (bf16[4,144,1152]{2,1,0:T(8,128)(2,1)}, bf16[4,144,1152]{2,1,0:T(8,128)(2,1)}, u32[]{:S(2)}, u32[]{:S(2)}) collective-permute-start(bf16[4,144,1152]{2,1,0:T(8,128)(2,1)} %get-tuple-element.277), channel_id=1, source_target_pairs={{0,4},{4,0},{1,5},{5,1},{2,6},{6,2},{3,7},{7,3},{8,12},{12,8},{9,1... | collective-permute-start | bytes 3981320 | tf_op jit(solution)/shard_map/ppermute | solution.py:311
  438.8 46.5 %collective-permute-start.39 = (bf16[144,1152]{1,0:T(8,128)(2,1)S(1)}, bf16[144,1152]{1,0:T(8,128)(2,1)S(1)}, u32[]{:S(2)}, u32[]{:S(2)}) collective-permute-start(bf16[144,1152]{1,0:T(8,128)(2,1)S(1)} %get-tuple-element.297), channel_id=1, source_target_pairs={{0,8},{8,0},{16,24},{24,16},{1,9},{9,1},{17,25},{25,17},{2,10},{10... | collective-permute-start | bytes 995336 | tf_op jit(solution)/shard_map/ppermute | solution.py:316
  439.4 45.8 %collective-permute-start.40 = (bf16[144,1152]{1,0:T(8,128)(2,1)S(1)}, bf16[144,1152]{1,0:T(8,128)(2,1)S(1)}, u32[]{:S(2)}, u32[]{:S(2)}) collective-permute-start(bf16[144,1152]{1,0:T(8,128)(2,1)S(1)} %get-tuple-element.296), channel_id=1, source_target_pairs={{0,16},{8,24},{16,0},{24,8},{1,17},{9,25},{17,1},{25,9},{2,18},{10... | collective-permute-start | bytes 995336 | tf_op jit(solution)/shard_map/ppermute | solution.py:316
  440.2 45.1 %collective-permute-start.41 = (bf16[144,1152]{1,0:T(8,128)(2,1)S(1)}, bf16[144,1152]{1,0:T(8,128)(2,1)}, u32[]{:S(2)}, u32[]{:S(2)}) collective-permute-start(bf16[144,1152]{1,0:T(8,128)(2,1)S(1)} %get-tuple-element.295), channel_id=1, source_target_pairs={{0,24},{8,16},{16,8},{24,0},{1,25},{9,17},{17,9},{25,1},{2,26},{10... | collective-permute-start | bytes 995336 | tf_op jit(solution)/shard_map/ppermute | solution.py:316
  446.0 39.3 %collective-permute-start.42 = (bf16[4,144,1152]{2,1,0:T(8,128)(2,1)}, bf16[4,144,1152]{2,1,0:T(8,128)(2,1)}, u32[]{:S(2)}, u32[]{:S(2)}) collective-permute-start(bf16[4,144,1152]{2,1,0:T(8,128)(2,1)} %get-tuple-element.275), channel_id=1, source_target_pairs={{0,1},{1,0},{2,3},{3,2},{4,5},{5,4},{6,7},{7,6},{8,9},{9,8},{10,11... | collective-permute-start | bytes 3981320 | tf_op jit(solution)/shard_map/ppermute | solution.py:311
  446.0 39.3 %collective-permute-start.43 = (bf16[4,144,1152]{2,1,0:T(8,128)(2,1)}, bf16[4,144,1152]{2,1,0:T(8,128)(2,1)}, u32[]{:S(2)}, u32[]{:S(2)}) collective-permute-start(bf16[4,144,1152]{2,1,0:T(8,128)(2,1)} %get-tuple-element.274), channel_id=1, source_target_pairs={{0,4},{4,0},{1,5},{5,1},{2,6},{6,2},{3,7},{7,3},{8,12},{12,8},{9,1... | collective-permute-start | bytes 3981320 | tf_op jit(solution)/shard_map/ppermute | solution.py:311
  496.9 35.2 %collective-permute-start.46 = (bf16[144,1152]{1,0:T(8,128)(2,1)S(1)}, bf16[144,1152]{1,0:T(8,128)(2,1)S(1)}, u32[]{:S(2)}, u32[]{:S(2)}) collective-permute-start(bf16[144,1152]{1,0:T(8,128)(2,1)S(1)} %get-tuple-element.293), channel_id=1, source_target_pairs={{0,8},{8,0},{16,24},{24,16},{1,9},{9,1},{17,25},{25,17},{2,10},{10... | collective-permute-start | bytes 995336 | tf_op jit(solution)/shard_map/ppermute | solution.py:316
  497.0 35.2 %collective-permute-start.47 = (bf16[144,1152]{1,0:T(8,128)(2,1)S(1)}, bf16[144,1152]{1,0:T(8,128)(2,1)}, u32[]{:S(2)}, u32[]{:S(2)}) collective-permute-start(bf16[144,1152]{1,0:T(8,128)(2,1)S(1)} %get-tuple-element.292), channel_id=1, source_target_pairs={{0,16},{8,24},{16,0},{24,8},{1,17},{9,25},{17,1},{25,9},{2,18},{10... | collective-permute-start | bytes 995336 | tf_op jit(solution)/shard_map/ppermute | solution.py:316
  498.5 33.7 %collective-permute-start.48 = (bf16[144,1152]{1,0:T(8,128)(2,1)S(1)}, bf16[144,1152]{1,0:T(8,128)(2,1)}, u32[]{:S(2)}, u32[]{:S(2)}) collective-permute-start(bf16[144,1152]{1,0:T(8,128)(2,1)S(1)} %get-tuple-element.291), channel_id=1, source_target_pairs={{0,24},{8,16},{16,8},{24,0},{1,25},{9,17},{17,9},{25,1},{2,26},{10... | collective-permute-start | bytes 995336 | tf_op jit(solution)/shard_map/ppermute | solution.py:316
  537.9 31.3 %collective-permute-start.49 = (bf16[4,144,512]{2,1,0:T(8,128)(2,1)}, bf16[4,144,512]{2,1,0:T(8,128)(2,1)}, u32[]{:S(2)}, u32[]{:S(2)}) collective-permute-start(bf16[4,144,512]{2,1,0:T(8,128)(2,1)} %get-tuple-element.285), channel_id=1, source_target_pairs={{0,1},{1,0},{2,3},{3,2},{4,5},{5,4},{6,7},{7,6},{8,9},{9,8},{10,11... | collective-permute-start | bytes 1769480 | tf_op jit(solution)/shard_map/ppermute | solution.py:311
  580.3 42.9 %collective-permute-start.57 = (bf16[144,512]{1,0:T(8,128)(2,1)}, bf16[144,512]{1,0:T(8,128)(2,1)}, u32[]{:S(2)}, u32[]{:S(2)}) collective-permute-start(bf16[144,512]{1,0:T(8,128)(2,1)} %get-tuple-element.309), channel_id=1, source_target_pairs={{0,24},{8,16},{16,8},{24,0},{1,25},{9,17},{17,9},{25,1},{2,26},{10... | collective-permute-start | bytes 442376 | tf_op jit(solution)/shard_map/ppermute | solution.py:316
  581.6 43.1 %collective-permute-start.56 = (bf16[144,512]{1,0:T(8,128)(2,1)S(1)}, bf16[144,512]{1,0:T(8,128)(2,1)}, u32[]{:S(2)}, u32[]{:S(2)}) collective-permute-start(bf16[144,512]{1,0:T(8,128)(2,1)S(1)} %get-tuple-element.310), channel_id=1, source_target_pairs={{0,16},{8,24},{16,0},{24,8},{1,17},{9,25},{17,1},{25,9},{2,18},{10... | collective-permute-start | bytes 442376 | tf_op jit(solution)/shard_map/ppermute | solution.py:316
  581.6 43.1 %collective-permute-start.55 = (bf16[144,512]{1,0:T(8,128)(2,1)S(1)}, bf16[144,512]{1,0:T(8,128)(2,1)}, u32[]{:S(2)}, u32[]{:S(2)}) collective-permute-start(bf16[144,512]{1,0:T(8,128)(2,1)S(1)} %get-tuple-element.311), channel_id=1, source_target_pairs={{0,8},{8,0},{16,24},{24,16},{1,9},{9,1},{17,25},{25,17},{2,10},{10... | collective-permute-start | bytes 442376 | tf_op jit(solution)/shard_map/ppermute | solution.py:316
  613.3 33.1 %collective-permute-start.59 = (bf16[4,144,640]{2,1,0:T(8,128)(2,1)S(1)}, bf16[4,144,640]{2,1,0:T(8,128)(2,1)S(1)}, u32[]{:S(2)}, u32[]{:S(2)}) collective-permute-start(bf16[4,144,640]{2,1,0:T(8,128)(2,1)S(1)} %get-tuple-element.278), channel_id=1, source_target_pairs={{0,4},{4,0},{1,5},{5,1},{2,6},{6,2},{3,7},{7,3},{8,12},{12,8},{9,1... | collective-permute-start | bytes 2211848 | tf_op jit(solution)/shard_map/ppermute | solution.py:311
  614.6 31.8 %collective-permute-start.58 = (bf16[4,144,640]{2,1,0:T(8,128)(2,1)S(1)}, bf16[4,144,640]{2,1,0:T(8,128)(2,1)S(1)}, u32[]{:S(2)}, u32[]{:S(2)}) collective-permute-start(bf16[4,144,640]{2,1,0:T(8,128)(2,1)S(1)} %get-tuple-element.279), channel_id=1, source_target_pairs={{0,1},{1,0},{2,3},{3,2},{4,5},{5,4},{6,7},{7,6},{8,9},{9,8},{10,11... | collective-permute-start | bytes 2211848 | tf_op jit(solution)/shard_map/ppermute | solution.py:311
  645.5 58.6 %collective-permute-start.54 = (bf16[256,1152]{1,0:T(8,128)(2,1)}, bf16[256,1152]{1,0:T(8,128)(2,1)}, u32[]{:S(2)}, u32[]{:S(2)}) collective-permute-start(bf16[256,1152]{1,0:T(8,128)(2,1)} %slice.172), channel_id=1, source_target_pairs={{0,1},{1,0},{2,3},{3,2},{4,5},{5,4},{6,7},{7,6},{8,9},{9,8},{10,11... | collective-permute-start | bytes 1769480 | tf_op jit(solution)/shard_map/ppermute | solution.py:311
  648.7 42.3 %collective-permute-start.62 = (bf16[144,640]{1,0:T(8,128)(2,1)}, bf16[144,640]{1,0:T(8,128)(2,1)}, u32[]{:S(2)}, u32[]{:S(2)}) collective-permute-start(bf16[144,640]{1,0:T(8,128)(2,1)} %get-tuple-element.303), channel_id=1, source_target_pairs={{0,24},{8,16},{16,8},{24,0},{1,25},{9,17},{17,9},{25,1},{2,26},{10... | collective-permute-start | bytes 552968 | tf_op jit(solution)/shard_map/ppermute | solution.py:316
  649.2 41.8 %collective-permute-start.61 = (bf16[144,640]{1,0:T(8,128)(2,1)}, bf16[144,640]{1,0:T(8,128)(2,1)}, u32[]{:S(2)}, u32[]{:S(2)}) collective-permute-start(bf16[144,640]{1,0:T(8,128)(2,1)} %get-tuple-element.304), channel_id=1, source_target_pairs={{0,16},{8,24},{16,0},{24,8},{1,17},{9,25},{17,1},{25,9},{2,18},{10... | collective-permute-start | bytes 552968 | tf_op jit(solution)/shard_map/ppermute | solution.py:316
  650.2 40.8 %collective-permute-start.60 = (bf16[144,640]{1,0:T(8,128)(2,1)}, bf16[144,640]{1,0:T(8,128)(2,1)}, u32[]{:S(2)}, u32[]{:S(2)}) collective-permute-start(bf16[144,640]{1,0:T(8,128)(2,1)} %get-tuple-element.305), channel_id=1, source_target_pairs={{0,8},{8,0},{16,24},{24,16},{1,9},{9,1},{17,25},{25,17},{2,10},{10... | collective-permute-start | bytes 552968 | tf_op jit(solution)/shard_map/ppermute | solution.py:316
  (140 other events, 2210.9 us)

commit v3 on v2

--- a/solution.py
+++ b/solution.py
@@ -174,7 +174,7 @@
     )(*ins)
 
 
-def attn_bwd_kernel(q_ref, k_ref, v_ref, g_ref, lse_ref, *refs, tile, first):
+def attn_bwd_kernel(q_ref, k_ref, v_ref, g_ref, lse_ref, *refs, tile, first, origin):
     dq_ref, dk_ref, dv_ref = refs[-3:]
     head = pl.program_id(0) + first
     rows, width = q_ref.shape
@@ -184,11 +184,12 @@
 
         @pl.when(pl.program_id(0) == 0)
         def _():
-            dq_ref[...] = refs[0][...]
-            dk_ref[...] = refs[1][...]
-            dv_ref[...] = refs[2][...]
-
-    lo, off = head_window(head, width)
+            dq_ref[:, :128] = refs[0][...]
+            dk_ref[:, :128] = refs[1][...]
+            dv_ref[:, :128] = refs[2][...]
+
+    lo, off = head_window(head, origin + dq_ref.shape[1])
+    there = pl.ds(pl.multiple_of(lo - origin, 128), WIN)
     lane = lax.broadcasted_iota(jnp.int32, (1, WIN), 1)
     inside = (lane >= off) & (lane < off + HD)
     keep = inside.astype(jnp.bfloat16)
@@ -210,24 +211,34 @@
         dv = dv + jnp.dot(pt.astype(jnp.bfloat16), gw, preferred_element_type=jnp.float32)
         dk = dk + jnp.dot(dst, qw, preferred_element_type=jnp.float32)
         dq = jnp.dot(ktw, dst, preferred_element_type=jnp.float32).T
-        old = dq_ref[r, pl.ds(lo, WIN)].astype(jnp.float32)
-        dq_ref[r, pl.ds(lo, WIN)] = jnp.where(inside, dq, old).astype(jnp.bfloat16)
-    old = dk_ref[:, pl.ds(lo, WIN)].astype(jnp.float32)
-    dk_ref[:, pl.ds(lo, WIN)] = jnp.where(inside, dk, old).astype(jnp.bfloat16)
-    old = dv_ref[:, pl.ds(lo, WIN)].astype(jnp.float32)
-    dv_ref[:, pl.ds(lo, WIN)] = jnp.where(inside, dv, old).astype(jnp.bfloat16)
-
-
-def attn_bwd(q, k, v, g, lse_rows, heads, into=(), tile=512):
+        old = dq_ref[r, there].astype(jnp.float32)
+        dq_ref[r, there] = jnp.where(inside, dq, old).astype(jnp.bfloat16)
+    old = dk_ref[:, there].astype(jnp.float32)
+    dk_ref[:, there] = jnp.where(inside, dk, old).astype(jnp.bfloat16)
+    old = dv_ref[:, there].astype(jnp.float32)
+    dv_ref[:, there] = jnp.where(inside, dv, old).astype(jnp.bfloat16)
+
+
+def head_columns(heads):
+    first, count = heads
+    return (first * HD) // 128 * 128, -(-((first + count) * HD) // 128) * 128
+
+
+def attn_bwd(q, k, v, g, lse_rows, heads, before=(), tile=512):
     rows, width = q.shape
     keys = k.shape[0]
     first, count = heads
-    outs = [jax.ShapeDtypeStruct(a.shape, jnp.bfloat16) for a in (q, k, v)]
-    ins = (q, k, v, g, lse_rows, *into)
+    start, stop = head_columns(heads)
+    outs = [jax.ShapeDtypeStruct((a.shape[0], stop - start), jnp.bfloat16) for a in (q, k, v)]
+    ins = (q, k, v, g, lse_rows, *before)
+    specs = [whole(a) for a in ins[:5]]
+    for array in before:
+        last = array.shape[1] // 128 - 1
+        specs.append(pl.BlockSpec((array.shape[0], 128), lambda h, last=last: (0, last)))
     return pl.pallas_call(
-        functools.partial(attn_bwd_kernel, tile=tile, first=first),
+        functools.partial(attn_bwd_kernel, tile=tile, first=first, origin=start),
         grid=(count,),
-        in_specs=[whole(a) for a in ins],
+        in_specs=specs,
         out_specs=[whole(a) for a in outs],
         out_shape=outs,
         compiler_params=pltpu.CompilerParams(vmem_limit_bytes=52 << 20),
@@ -246,67 +257,6 @@
     return lax.optimization_barrier((array, earlier))[0]
 
 
-def assemble(pieces, places, where, kind, height):
-    width = pieces[0].shape[-1]
-    blocks = [(i, b) for i, piece in enumerate(pieces) for b in range(piece.shape[0])]
-
-    def body(where_ref, *refs):
-        ins, out = refs[: len(pieces)], refs[len(pieces)]
-        held, arrived, left = refs[len(pieces) + 1 :]
-        zi = where_ref[0]
-        loads, stores = [], []
-        start = 0
-        for piece, (first, x_bit, c_bit, y_bit, offset) in zip(ins, places):
-            xi = where_ref[1] if x_bit == 0 else 1 - where_ref[1]
-            ci = where_ref[2] if c_bit == 0 else 1 - where_ref[2]
-            yi = where_ref[3] if y_bit == 0 else 1 - where_ref[3]
-            size = piece.shape[1]
-            for block in range(piece.shape[0]):
-                slot = start + block
-                row = ((zi ^ (first + block)) * 2 + xi) * height + offset
-                quarter = (ci * 2 + yi) * (8 * height)
-                if kind == "columns":
-                    rows = pl.ds(pl.multiple_of(row, 16), size)
-                    quarter = (ci * 2 + yi) * width
-                    target = out.at[rows, pl.ds(pl.multiple_of(quarter, 128), width)]
-                else:
-                    target = out.at[pl.ds(pl.multiple_of(quarter + row, 16), size), :]
-                here = held.at[slot, pl.ds(0, size)]
-                loads.append(pltpu.make_async_copy(piece.at[block], here, arrived.at[slot]))
-                stores.append(pltpu.make_async_copy(here, target, left.at[slot]))
-            start += piece.shape[0]
-        for load in loads:
-            load.start()
-        for load, store in zip(loads, stores):
-            load.wait()
-            store.start()
-        for store in stores:
-            store.wait()
-
-    shape = (8 * height, 4 * width) if kind == "columns" else (32 * height, width)
-    tallest = max(piece.shape[1] for piece in pieces)
-    return pl.pallas_call(
-        body,
-        grid_spec=pltpu.PrefetchScalarGridSpec(
-            num_scalar_prefetch=1,
-            grid=(1,),
-            in_specs=[pl.BlockSpec(memory_space=pl.ANY)] * len(pieces),
-            out_specs=pl.BlockSpec(memory_space=pl.ANY),
-            scratch_shapes=[
-                pltpu.VMEM((len(blocks), tallest, width), pieces[0].dtype),
-                pltpu.SemaphoreType.DMA((len(blocks),)),
-                pltpu.SemaphoreType.DMA((len(blocks),)),
-            ],
-        ),
-        out_shape=jax.ShapeDtypeStruct(shape, pieces[0].dtype),
-        compiler_params=pltpu.CompilerParams(vmem_limit_bytes=56 << 20),
-        cost_estimate=pl.CostEstimate(
-            flops=0, bytes_accessed=4 * shape[0] * shape[1], transcendentals=0
-        ),
-        name="assemble_" + kind,
-    )(where, *pieces)
-
-
 def swap(array, axis):
     return lax.ppermute(array, axis, SWAP)
 
@@ -334,14 +284,6 @@
     return corner_swap(jnp.where(lax.axis_index("c") == 0, from_x, from_y), 1)
 
 
-PLACES = [(0, 0, 0), (1, 0, 0), (0, 0, 1), (1, 0, 1)]
-
-
-def with_core(pieces, others):
-    places = [(0, x, c, y, 0) for x, c, y in PLACES] + [(0, x, 1 - c, y, 0) for x, c, y in PLACES]
-    return list(pieces) + list(others), places
-
-
 def add_low(*terms):
     total = terms[0].astype(jnp.float32)
     for term in terms[1:]:
@@ -349,7 +291,15 @@
     return total.astype(jnp.bfloat16)
 
 
-def part_columns(half, yy, xx):
+def rows_of(half, yy, xx):
+    width = half.shape[1]
+    cut = lax.dynamic_slice(
+        half.reshape(2, 4, 2, 144, width), (yy, 0, xx, 0, 0), (1, 4, 1, 144, width)
+    )
+    return cut.reshape(4, 144, width)
+
+
+def columns_of(half, yy, xx):
     width = half.shape[1] // 2
     cut = lax.dynamic_slice(
         half.reshape(4, 2, 144, 2 * width), (0, xx, 0, yy * width), (4, 1, 144, width)
@@ -357,26 +307,19 @@
     return cut.reshape(4, 144, width)
 
 
-def part_rows(half, yy, xx):
-    width = half.shape[1]
-    cut = lax.dynamic_slice(
-        half.reshape(2, 4, 2, 144, width), (yy, 0, xx, 0, 0), (1, 4, 1, 144, width)
-    )
-    return cut.reshape(4, 144, width)
-
-
 class ScatterSum:
-    def __init__(self, part, half):
+    def __init__(self, part, half, quarters):
         self.part, self.half = part, half
-        self.zi, self.xi, self.yi = [lax.axis_index(name) for name in ("z", "x", "y")]
+        self.mine, self.theirs = quarters
+        self.zi, self.xi = lax.axis_index("z"), lax.axis_index("x")
 
     def corner(self):
-        self.sent = (self.part(self.half, 1 - self.yi, 1 - self.xi),)
+        self.sent = (self.part(self.half, self.theirs, 1 - self.xi),)
         self.got = (corner_swap(self.sent[0], 0),)
 
     def plane(self, *earlier):
         half, got = after(self.half, *earlier), self.got[0]
-        to_y, to_x = self.part(half, 1 - self.yi, self.xi), self.part(half, self.yi, 1 - self.xi)
+        to_y, to_x = self.part(half, self.theirs, self.xi), self.part(half, self.mine, 1 - self.xi)
         even = lax.axis_index("c") == 0
         to_y = jnp.where(even, add_low(to_y, got), to_y)
         to_x = jnp.where(even, to_x, add_low(to_x, got))
@@ -385,7 +328,7 @@
 
     def line(self, *earlier):
         half = after(self.half, *earlier)
-        own = add_low(self.part(half, self.yi, self.xi), *self.got)
+        own = add_low(self.part(half, self.mine, self.xi), *self.got)
         blocks = [lax.dynamic_index_in_dim(own, self.zi ^ step, 0, False) for step in range(4)]
         self.own, self.sent = blocks[0], blocks[1:]
         self.got = line_hops(lambda step: blocks[step])
@@ -395,6 +338,350 @@
         for hop in self.got:
             total = total + hop.astype(jnp.float32)
         return total
+
+
+def load_quarter(where_ref, pieces, quarter, buf, sems):
+    copies = []
+    for x_bit in range(2):
+        piece = pieces[quarter * 2 + x_bit]
+        xi = where_ref[1] if x_bit == 0 else 1 - where_ref[1]
+        height = piece.shape[1]
+        for block in range(4):
+            row = pl.multiple_of(((where_ref[0] ^ block) * 2 + xi) * height, 16)
+            copies.append(
+                pltpu.make_async_copy(
+                    piece.at[block], buf.at[pl.ds(row, height), :], sems.at[len(copies)]
+                )
+            )
+    return copies
+
+
+def stream_quarters(where_ref, pieces, buf, sems):
+    step = pl.program_id(0)
+    for i in range(4):
+
+        @pl.when(step == i)
+        def _(i=i):
+            quarter = load_quarter(where_ref, pieces, i, buf.at[i % 2], sems.at[i % 2])
+            if i == 0:
+                for copy in quarter:
+                    copy.start()
+            if i < 3:
+                other = (i + 1) % 2
+                for copy in load_quarter(
+                    where_ref, pieces, i + 1, buf.at[other], sems.at[other]
+                ):
+                    copy.start()
+            for copy in quarter:
+                copy.wait()
+
+    return lax.rem(step, 2)
+
+
+def quarter_scratch(width):
+    return [pltpu.VMEM((2, width, width), jnp.bfloat16), pltpu.SemaphoreType.DMA((2, 8))]
+
+
+def times_t(left, right):
+    return lax.dot_general(
+        left, right, (((1,), (1,)), ((), ())), preferred_element_type=jnp.float32
+    )
+
+
+def quarter_call(body, where, ins, in_specs, pieces, outs, out_specs, scratch, flops, name):
+    return pl.pallas_call(
+        body,
+        grid_spec=pltpu.PrefetchScalarGridSpec(
+            num_scalar_prefetch=1,
+            grid=(4,),
+            in_specs=in_specs + [pl.BlockSpec(memory_space=pl.ANY)] * len(pieces),
+            out_specs=out_specs,
+            scratch_shapes=scratch,
+        ),
+        out_shape=outs,
+        compiler_params=pltpu.CompilerParams(vmem_limit_bytes=58 << 20),
+        cost_estimate=pl.CostEstimate(
+            flops=flops, bytes_accessed=30 << 20, transcendentals=0
+        ),
+        name=name,
+    )(where, *ins, *pieces)
+
+
+def fixed(array):
+    shape = array.shape
+    return pl.BlockSpec(shape, lambda i, w: (0,) * len(shape), pipeline_mode=pl.Buffered(1))
+
+
+def moving(rows, width):
+    return pl.BlockSpec((rows, width), lambda i, w: (0, i))
+
+
+TILE = 512
+
+
+def feed_up(where, inputs, bias, pieces):
+    rows, width = inputs.shape
+
+    def body(where_ref, x_ref, bias_ref, *refs):
+        ins, (act_ref, slope_ref, buf, sems) = refs[:8], refs[8:]
+        slot = stream_quarters(where_ref, ins, buf, sems)
+        weights = buf.at[slot]
+        for t in range(rows // TILE):
+            r = pl.ds(t * TILE, TILE)
+            u = jnp.dot(x_ref[r, :], weights[...], preferred_element_type=jnp.float32)
+            u = u + bias_ref[...]
+            square = u * u
+            bend = jnp.tanh(u * (GELU_COEF + (GELU_COEF * 0.044715) * square))
+            half = 0.5 + 0.5 * bend
+            slope = (0.5 * GELU_COEF) + (1.5 * GELU_COEF * 0.044715) * square
+            act_ref[r, :] = (u * half).astype(jnp.bfloat16)
+            slope_ref[r, :] = (half + u * (1.0 - bend * bend) * slope).astype(jnp.bfloat16)
+
+    out = jax.ShapeDtypeStruct((rows, 4 * width), jnp.bfloat16)
+    return quarter_call(
+        body,
+        where,
+        (inputs, bias),
+        [fixed(inputs), moving(1, width)],
+        pieces,
+        [out, out],
+        [moving(rows, width)] * 2,
+        quarter_scratch(width),
+        8 * rows * width * width,
+        "feed_up",
+    )
+
+
+def feed_down(where, activated, middle, gate, bias, pieces):
+    rows, width = middle.shape
+
+    def body(where_ref, act_ref, middle_ref, gate_ref, bias_ref, *refs):
+        ins, (feed_ref, out_ref, buf, sems) = refs[:8], refs[8:]
+        slot = stream_quarters(where_ref, ins, buf, sems)
+        weights = buf.at[slot]
+        step = pl.program_id(0)
+        for t in range(rows // TILE):
+            r = pl.ds(t * TILE, TILE)
+            term = jnp.dot(act_ref[r, :], weights[...], preferred_element_type=jnp.float32)
+
+            @pl.when(step == 0)
+            def _():
+                feed_ref[r, :] = term + bias_ref[...]
+
+            @pl.when((step > 0) & (step < 3))
+            def _():
+                feed_ref[r, :] += term
+
+            @pl.when(step == 3)
+            def _():
+                feed = feed_ref[r, :] + term
+                feed_ref[r, :] = feed
+                out_ref[r, :] = (middle_ref[r, :] + gate_ref[...] * feed).astype(jnp.bfloat16)
+
+    outs = [
+        jax.ShapeDtypeStruct((rows, width), jnp.float32),
+        jax.ShapeDtypeStruct((rows, width), jnp.bfloat16),
+    ]
+    return quarter_call(
+        body,
+        where,
+        (activated, middle, gate, bias),
+        [moving(rows, width), fixed(middle), fixed(gate), fixed(bias)],
+        pieces,
+        outs,
+        [fixed(a) for a in outs],
+        quarter_scratch(width),
+        8 * rows * width * width,
+        "feed_down",
+    )
+
+
+def feed_back(where, d_feed, slope, down_pieces, up_pieces):
+    rows, width = d_feed.shape
+
+    def body(where_ref, d_ref, slope_ref, *refs):
+        down_ins, up_ins = refs[:8], refs[8:16]
+        before_ref, normed_ref, sum_ref, down_buf, down_sems, up_buf, up_sems = refs[16:]
+        slot = stream_quarters(where_ref, down_ins, down_buf, down_sems)
+        stream_quarters(where_ref, up_ins, up_buf, up_sems)
+        down_weights, up_weights = down_buf.at[slot], up_buf.at[slot]
+        step = pl.program_id(0)
+        total = jnp.zeros((1, width), jnp.float32)
+        for t in range(rows // TILE):
+            r = pl.ds(t * TILE, TILE)
+            d_act = times_t(d_ref[r, :], down_weights[...])
+            d_before = (d_act * slope_ref[r, :].astype(jnp.float32)).astype(jnp.bfloat16)
+            before_ref[r, :] = d_before
+            total = total + jnp.sum(d_before.astype(jnp.float32), axis=0, keepdims=True)
+            term = times_t(d_before, up_weights[...])
+
+            @pl.when(step == 0)
+            def _():
+                normed_ref[r, :] = term
+
+            @pl.when(step > 0)
+            def _():
+                normed_ref[r, :] += term
+
+        sum_ref[...] = total
+
+    outs = [
+        jax.ShapeDtypeStruct((rows, 4 * width), jnp.bfloat16),
+        jax.ShapeDtypeStruct((rows, width), jnp.float32),
+        jax.ShapeDtypeStruct((1, 4 * width), jnp.float32),
+    ]
+    return quarter_call(
+        body,
+        where,
+        (d_feed, slope),
+        [fixed(d_feed), moving(rows, width)],
+        list(down_pieces) + list(up_pieces),
+        outs,
+        [moving(rows, width), fixed(outs[1]), moving(1, width)],
+        quarter_scratch(width) * 2,
+        16 * rows * width * width,
+        "feed_back",
+    )
+
+
+def project(where, inputs, query_bias, value_bias, pieces):
+    rows, width = inputs.shape
+
+    def body(where_ref, x_ref, query_ref, value_ref, *refs):
+        ins, (q_ref, k_ref, v_ref, all_ref, buf, sems, out_sems) = refs[:8], refs[8:]
+        base = where_ref[2] * 2 + where_ref[3]
+
+        def loads(quarter, place):
+            return load_quarter(where_ref, ins, quarter, buf.at[place], sems.at[place])
+
+        for place in range(4):
+            for quarter in range(4):
+
+                @pl.when((base ^ place) == quarter)
+                def _(place=place, quarter=quarter):
+                    for copy in loads(quarter, place):
+                        copy.start()
+
+        stores = []
+        biases = (query_ref, None, value_ref, None)
+        for place, out_ref in enumerate((q_ref, k_ref, v_ref, None)):
+            for copy in loads(0, place):
+                copy.wait()
+            stores.append(
+                pltpu.make_async_copy(buf.at[place], all_ref.at[place], out_sems.at[place])
+            )
+            stores[-1].start()
+            if out_ref is None:
+                continue
+            for t in range(rows // TILE):
+                r = pl.ds(t * TILE, TILE)
+                term = jnp.dot(x_ref[r, :], buf[place], preferred_element_type=jnp.float32)
+                if biases[place] is not None:
+                    term = term + biases[place][...]
+                out_ref[r, :] = term.astype(jnp.bfloat16)
+        for store in stores:
+            store.wait()
+
+    low = jax.ShapeDtypeStruct((rows, width), jnp.bfloat16)
+    every = jax.ShapeDtypeStruct((4, width, width), jnp.bfloat16)
+    spec = pl.BlockSpec((rows, width), lambda i, w: (0, 0), pipeline_mode=pl.Buffered(1))
+    return pl.pallas_call(
+        body,
+        grid_spec=pltpu.PrefetchScalarGridSpec(
+            num_scalar_prefetch=1,
+            grid=(1,),
+            in_specs=[spec, fixed(query_bias), fixed(value_bias)]
+            + [pl.BlockSpec(memory_space=pl.ANY)] * 8,
+            out_specs=[spec] * 3 + [pl.BlockSpec(memory_space=pl.ANY)],
+            scratch_shapes=[
+                pltpu.VMEM((4, width, width), jnp.bfloat16),
+                pltpu.SemaphoreType.DMA((4, 8)),
+                pltpu.SemaphoreType.DMA((4,)),
+            ],
+        ),
+        out_shape=[low, low, low, every],
+        compiler_params=pltpu.CompilerParams(vmem_limit_bytes=58 << 20),
+        cost_estimate=pl.CostEstimate(
+            flops=6 * rows * width * width, bytes_accessed=30 << 20, transcendentals=0
+        ),
+        name="project",
+    )(where, inputs, query_bias, value_bias, *pieces)
+
+
+def project_back(parts, matrices):
+    rows = parts[0].shape[0]
+    width = matrices.shape[1]
+    cut = width - parts[1].shape[1]
+
+    def body(*refs):
+        ins, (w_ref, out_ref) = refs[:6], refs[6:]
+        total = None
+        for i in range(3):
+            for ref, start, stop in ((ins[2 * i], 0, cut), (ins[2 * i + 1], cut, width)):
+                term = times_t(ref[:, : stop - start], w_ref[i, :, start:stop])
+                total = term if total is None else total + term
+        out_ref[...] = total
+
+    return pl.pallas_call(
+        body,
+        grid=(rows // TILE,),
+        in_specs=[pl.BlockSpec((TILE, a.shape[1]), lambda i: (i, 0)) for a in parts]
+        + [
+            pl.BlockSpec(
+                (3, width, width), lambda i: (0, 0, 0), pipeline_mode=pl.Buffered(1)
+            )
+        ],
+        out_specs=pl.BlockSpec((TILE, width), lambda i: (i, 0)),
+        out_shape=jax.ShapeDtypeStruct((rows, width), jnp.float32),
+        compiler_params=pltpu.CompilerParams(vmem_limit_bytes=40 << 20),
+        cost_estimate=pl.CostEstimate(
+            flops=6 * rows * width * width, bytes_accessed=20 << 20, transcendentals=0
+        ),
+        name="project_back",
+    )(*parts, matrices)
+
+
+def bias_sums(mods, parts, d_branch, up_sums, d_feed):
+    width = d_feed.shape[1]
+    cut = width - parts[1].shape[1]
+
+    def body(mods_ref, qa_ref, qb_ref, va_ref, vb_ref, branch_ref, up_ref, feed_ref, out_ref):
+        @pl.when(pl.program_id(0) == 0)
+        def _():
+            out_ref[...] = jnp.zeros_like(out_ref)
+            out_ref[0:6, :] = mods_ref[...].astype(jnp.float32)
+            out_ref[9:13, :] = up_ref[...]
+
+        for row, ref, start, stop in (
+            (6, qa_ref, 0, cut),
+            (6, qb_ref, cut, width),
+            (7, va_ref, 0, cut),
+            (7, vb_ref, cut, width),
+            (8, branch_ref, 0, width),
+            (13, feed_ref, 0, width),
+        ):
+            terms = ref[:, : stop - start].astype(jnp.float32)
+            out_ref[row : row + 1, start:stop] += jnp.sum(terms, axis=0, keepdims=True)
+
+    def tile(array):
+        return pl.BlockSpec((256, array.shape[1]), lambda i: (i, 0))
+
+    def held(array):
+        return pl.BlockSpec(array.shape, lambda i: (0, 0))
+
+    out = jax.ShapeDtypeStruct((14, width), jnp.float32)
+    return pl.pallas_call(
+        body,
+        grid=(d_feed.shape[0] // 256,),
+        in_specs=[held(mods)]
+        + [tile(a) for a in parts]
+        + [tile(d_branch), held(up_sums), tile(d_feed)],
+        out_specs=held(out),
+        out_shape=out,
+        compiler_params=pltpu.CompilerParams(vmem_limit_bytes=16 << 20),
+        cost_estimate=pl.CostEstimate(flops=8 << 20, bytes_accessed=10 << 20, transcendentals=0),
+        name="bias_sums",
+    )(mods, *parts, d_branch, up_sums, d_feed)
 
 
 def local_pairs(
@@ -415,8 +702,26 @@
     where = jnp.stack([zi, xi, ci, yi]).astype(jnp.int32)
     rows = width // 32
 
+    quarter = ci * 2 + yi
+
+    def in_order(array):
+        return jnp.stack(
+            [lax.dynamic_index_in_dim(array, quarter ^ step, 0, False) for step in range(4)]
+        )
+
     def exchange(array):
         return lax.all_to_all(array, ALL, 0, 0, tiled=True)
+
+    def exchange_quarters(array):
+        got = [lax.dynamic_index_in_dim(array, quarter, 0, False)]
+        for step, axes in ((1, "y"), (2, "c"), (3, ("c", "y"))):
+            entry = lax.dynamic_index_in_dim(array, quarter ^ step, 0, False)
+            got.append(
+                swap(entry, axes)
+                if step < 3
+                else lax.ppermute(entry, axes, [(i, i ^ 3) for i in range(4)])
+            )
+        return in_order(jnp.stack(got))
 
     def to_all(vector):
         return exchange(jnp.broadcast_to(vector, (32,) + vector.shape))
@@ -437,9 +742,7 @@
         + [proj_weight.reshape(rows, width)]
     )
     up_quarters = up_weight.reshape(rows, 8, 4, 144).transpose(2, 0, 1, 3).reshape(4, rows, width)
-    units = lax.all_to_all(
-        jnp.concatenate([quarters, up_quarters], axis=1), ("c", "y"), 0, 0, tiled=True
-    )
+    units = exchange_quarters(jnp.concatenate([quarters, up_quarters], axis=1))
     unit_a = units[:, :rows].reshape(4 * rows, width)
     unit_u = units[:, rows:].reshape(4 * rows, width)
     unit_d = down_weight.reshape(4 * rows, width)
@@ -460,6 +763,12 @@
     ada_rows = ada_weight.reshape(rows, 6 * width)
     shares = jnp.dot(silu_cut, ada_rows, preferred_element_type=jnp.float32)
     first_shares, later_shares = shares[:, : 2 * width], shares[:, 2 * width :]
+    line_a, plane_a, hops_u, first_shares = lax.optimization_barrier(
+        (line_a, plane_a, hops_u, first_shares)
+    )
+    corner_a = corner_gather(*plane_a)
+    core_a = [swap(p, "c") for p in (line_a, *plane_a)]
+    first_shares = after(first_shares, *core_a)
     modulations = jnp.sum(exchange(first_shares), axis=0, keepdims=True)
     modulations = modulations + biases[: 2 * width]
     shift_attention, scale_attention = jnp.split(modulations, 2, axis=1)
@@ -467,36 +776,27 @@
     tokens_low = jnp.concatenate([own_half, half_received])
     tokens = tokens_low.astype(jnp.float32)
     normed = norm_modulate(tokens, shift_attention, scale_attention).astype(jnp.bfloat16)
-    line_a, plane_a, hops_u = lax.optimization_barrier((line_a, plane_a, hops_u))
-    corner_a = corner_gather(*plane_a)
-    core_a = [swap(p, "c") for p in (line_a, *plane_a)]
     line_u = jnp.stack([unit_u, *hops_u])
     unit_d = after(unit_d, line_u, *core_a)
     hops_d = line_hops(lambda step: unit_d)
-    corner_a = after(corner_a, unit_d)
+    corner_a = after(corner_a, unit_d, modulations)
     core_a.append(swap(corner_a, "c"))
     line_u = after(line_u, core_a[3])
     plane_u = plane_gather(line_u)
-    pieces, places = with_core((line_a, *plane_a, corner_a), core_a)
-    attention_matrix = assemble(after(pieces, line_u, unit_d), places, where, "columns", 4 * rows)
-    qkv_matrix = attention_matrix[:, : 3 * width]
-    proj_matrix = attention_matrix[:, 3 * width :]
-
-    query_bias = biases[6 * width : 7 * width]
-    value_bias = biases[7 * width : 8 * width]
+    query_bias = biases[None, 6 * width : 7 * width]
+    value_bias = biases[None, 7 * width : 8 * width]
     proj_bias = biases[8 * width : 9 * width]
-    up_bias = biases[9 * width : 9 * width + FF].reshape(8, 4, 144).transpose(1, 0, 2).reshape(-1)
-    down_bias = biases[9 * width + FF :]
-
-    later_modulations = jnp.sum(
-        exchange(after(later_shares, attention_matrix)), axis=0, keepdims=True
-    )
-    later_modulations = later_modulations + biases[2 * width : 6 * width]
-    gate_attention, shift_feed, scale_feed, gate_feed = jnp.split(later_modulations, 4, axis=1)
-    projected = jnp.dot(normed, qkv_matrix, preferred_element_type=jnp.float32)
-    queries = (projected[:, :width] + query_bias).astype(jnp.bfloat16)
-    keys = projected[:, width : 2 * width].astype(jnp.bfloat16)
-    values = (projected[:, 2 * width :] + value_bias).astype(jnp.bfloat16)
+    up_bias = biases[9 * width : 9 * width + FF].reshape(8, 4, 144).transpose(1, 0, 2)
+    up_bias = in_order(up_bias.reshape(4, width)).reshape(1, FF)
+    down_bias = biases[None, 9 * width + FF :]
+    queries, keys, values, matrices = project(
+        where,
+        normed,
+        query_bias,
+        value_bias,
+        after([line_a, *plane_a, corner_a, *core_a], line_u, unit_d),
+    )
+    proj_matrix = matrices[3]
     line_d = jnp.stack([after(unit_d, values), *hops_d])
     plane_u = after(plane_u, line_d)
     corner_u = corner_gather(*plane_u)
@@ -508,73 +808,67 @@
     attended, log_total = attn_fwd(
         after(queries, line_d, *core_u[:3]), keys, values, (8, 8), tuple(part_one)
     )
+    later_modulations = jnp.sum(after(exchange(after(later_shares, line_u)), *part_one), axis=0, keepdims=True)
+    later_modulations = later_modulations + biases[2 * width : 6 * width]
+    gate_attention, shift_feed, scale_feed, gate_feed = jnp.split(later_modulations, 4, axis=1)
     branch = (
         jnp.dot(attended, proj_matrix, preferred_element_type=jnp.float32)
         + proj_bias
     )
     middle = tokens + gate_attention * branch
     normed_feed = norm_modulate(middle, shift_feed, scale_feed).astype(jnp.bfloat16)
-    pieces, places = with_core((line_u, *plane_u, corner_u), core_u)
+    pieces_u = after([line_u, *plane_u, corner_u, *core_u], normed_feed)
     plane_d = after(plane_d, normed_feed)
     corner_d = corner_gather(*plane_d)
     core_d = [swap(p, "c") for p in (after(line_d, normed_feed), *plane_d)]
-    up_matrix = assemble(
-        after(pieces, normed_feed, *plane_d), places, where, "columns", 4 * rows
-    )
-    other_cotangent = after(lax.dynamic_index_in_dim(cotangent, 1 - yi, 0, False), corner_d)
+    other_cotangent = after(lax.dynamic_index_in_dim(cotangent, 1 - yi, 0, False), *plane_d)
     cotangent_received = swap(other_cotangent, "y")
+    activated, slope = feed_up(
+        where,
+        after(normed_feed, *core_d[:3], other_cotangent),
+        up_bias,
+        pieces_u,
+    )
+    activated, corner_d = lax.optimization_barrier((activated, corner_d))
     core_d.append(swap(corner_d, "c"))
-    up_matrix = after(up_matrix, *core_d[:3], corner_d, other_cotangent)
-    before = jnp.dot(normed_feed, up_matrix, preferred_element_type=jnp.float32) + up_bias
-    activated = gelu_tanh(before).astype(jnp.bfloat16)
-    activated, core_d[3] = lax.optimization_barrier((activated, core_d[3]))
+    pieces_d = after([line_d, *plane_d, corner_d, *core_d], activated)
+    feed_out, output_low = feed_down(where, activated, middle, gate_feed, down_bias, pieces_d)
+    cotangent_received, output_low = lax.optimization_barrier((cotangent_received, output_low))
     own_cotangent = lax.dynamic_index_in_dim(cotangent, yi, 0, False)
-    def pick(array, core):
-        return lax.dynamic_slice_in_dim(array, core * 2 * width, 2 * width, 1)
-
-    pieces, places = with_core((line_d, *plane_d, corner_d), core_d)
-    down_matrix = assemble(after(pieces, activated), places, where, "rows", 4 * rows)
-    feed_out = jnp.dot(activated, down_matrix, preferred_element_type=jnp.float32) + down_bias
-    output_low = (middle + gate_feed * feed_out).astype(jnp.bfloat16)
-    cotangent_received, output_low = lax.optimization_barrier((cotangent_received, output_low))
     upstream = jnp.concatenate([own_cotangent, cotangent_received]).astype(jnp.float32)
     d_feed = (gate_feed * upstream).astype(jnp.bfloat16)
-    down_sent = over_tokens(pick(after(activated, output_low), 1 - ci), d_feed)
-    down_sent = down_sent.astype(jnp.bfloat16)
+    ours, others = slice(None, 2 * width), slice(2 * width, None)
+    down_sent = over_tokens(activated[:, others], d_feed).astype(jnp.bfloat16)
     down_received = swap(down_sent, "c")
-    output_received = swap(output_low[half_rows:], "y")
+    output_received = swap(after(output_low, down_sent)[half_rows:], "y")
     d_gate_feed = jnp.sum(upstream * feed_out, axis=0, keepdims=True)
-
-    d_activated = times_transposed(after(d_feed, down_sent), down_matrix)
-    unused_gelu, gelu_pull = jax.vjp(gelu_tanh, before)
-    d_before = gelu_pull(d_activated)[0].astype(jnp.bfloat16)
-    up_sent = over_tokens(
-        after(normed_feed, output_received, down_received), pick(d_before, 1 - ci)
-    ).astype(jnp.bfloat16)
+    down_half = over_tokens(after(activated, down_sent)[:, ours], d_feed)
+    down = ScatterSum(rows_of, add_low(down_half, down_received), (0, 1))
+    down.corner()
+    d_before, d_normed_feed, before_sums = feed_back(
+        where, after(d_feed, *down.sent), slope, pieces_d, pieces_u
+    )
+    output_received, d_before = lax.optimization_barrier((output_received, d_before))
+    down.plane(d_normed_feed)
+    up_sent = over_tokens(after(normed_feed, *down.sent), d_before[:, others])
+    up_sent = up_sent.astype(jnp.bfloat16)
     up_received = swap(up_sent, "c")
-    down_half = over_tokens(pick(after(activated, up_sent), ci), d_feed)
-    down = ScatterSum(part_rows, add_low(down_half, down_received))
-    down.corner()
-    d_normed_feed = times_transposed(after(d_before, *down.sent, up_received), up_matrix)
-    down.plane(d_normed_feed)
-    up_half = over_tokens(after(normed_feed, *down.sent), pick(d_before, ci))
-    up = ScatterSum(part_columns, add_low(up_half, up_received))
-    up.corner()
     unused_norm, norm_pull = jax.vjp(norm_modulate, middle, shift_feed, scale_feed)
     d_middle_part, d_shift_feed, d_scale_feed = norm_pull(
-        after(d_normed_feed, *up.sent)
+        after(d_normed_feed, up_sent)
     )
     d_middle = upstream + d_middle_part
     d_gate_attention = jnp.sum(d_middle * branch, axis=0, keepdims=True)
     d_branch = (gate_attention * d_middle).astype(jnp.bfloat16)
-    d_attended = times_transposed(after(d_branch, down.got[0]), proj_matrix).astype(jnp.bfloat16)
+    d_attended = times_transposed(d_branch, proj_matrix).astype(jnp.bfloat16)
     mods_early = jnp.concatenate([d_gate_attention, d_shift_feed, d_scale_feed, d_gate_feed], 1)
     mods_early = mods_early.astype(jnp.bfloat16)
-    early_every = to_all(mods_early[0])
-    down.line(d_attended)
-    up.plane(d_attended)
+    up_half = over_tokens(after(normed_feed, d_attended), d_before[:, ours])
+    up = ScatterSum(columns_of, add_low(up_half, up_received), (0, 1))
+    down.line(up.half)
+    up.corner()
     log_rows = log_total[:, :H].T
-    gradients = attn_bwd(
+    part_a = attn_bwd(
         queries,
         keys,
         values,
@@ -583,8 +877,8 @@
         (0, 8),
     )
 
-    def attention_terms(start, stop, core, *earlier):
-        d_q, d_k, d_v, d_b = [a[:, start:stop] for a in (*gradients, d_branch)]
+    def attention_terms(gradients, d_b, core, *earlier):
+        d_q, d_k, d_v = gradients
         left = after(normed, *earlier)
         first = over_tokens(left, jnp.where(core == 0, d_q, d_v))
         second = over_tokens(
@@ -592,107 +886,102 @@
         )
         return jnp.concatenate([first, second])
 
-    left_sent = attention_terms(
-        0, 512, 1 - ci, *gradients, *down.got, *up.got, early_every
-    ).astype(jnp.bfloat16)
+    left_terms = [a[:, :512] for a in part_a], d_branch[:, :512]
+    left_sent = attention_terms(*left_terms, 1 - ci, *part_a, *down.got, *up.got)
+    left_sent = left_sent.astype(jnp.bfloat16)
     left_received = swap(left_sent, "c")
-    up.line(left_sent)
-    left_half = attention_terms(0, 512, ci, left_sent, *up.sent)
-    left = ScatterSum(part_rows, add_low(left_half, left_received))
+    up.plane(left_sent)
+    left_half = attention_terms(*left_terms, ci, left_sent, *up.sent)
+    left = ScatterSum(rows_of, add_low(left_half, left_received), (yi, 1 - yi))
     left.corner()
     down_sum = down.total(left_half)
-    gradients = attn_bwd(
+    part_b = attn_bwd(
         queries,
         keys,
         values,
         after(d_attended, *left.sent, down_sum),
         log_rows,
         (8, 4),
-        tuple(gradients),
-    )
-    gradients = after(tuple(gradients), *left.got, *up.got)
-    left.plane(*gradients)
-    up_terms = up.total(*gradients).reshape(4, rows, width)
-    up_sum = lax.all_to_all(up_terms, ("c", "y"), 0, 0, tiled=True)
-    gradients = attn_bwd(
+        part_a,
+    )
+    part_b = after(tuple(part_b), *left.got, *up.got)
+    left.plane(*part_b)
+    up.line(*part_b)
+    part_c = attn_bwd(
         queries,
         keys,
         values,
-        after(d_attended, *left.sent, up_terms),
+        after(d_attended, *left.sent, *up.sent),
         log_rows,
         (12, 4),
-        tuple(gradients),
-    )
-    gradients = after(tuple(gradients), *left.got, up_sum)
-    d_queries, d_keys, d_values = gradients
-    left.line(*gradients)
-    right_sent = attention_terms(512, width, 1 - ci, *left.sent).astype(jnp.bfloat16)
+        part_b,
+    )
+    part_c = after(tuple(part_c), *left.got, *up.got)
+    right_parts = [
+        jnp.concatenate([b[:, :256], c], axis=1) for b, c in zip(part_b, part_c)
+    ]
+    right_terms = right_parts, d_branch[:, 512:]
+    left.line(*part_c)
+    right_sent = attention_terms(*right_terms, 1 - ci, *left.sent).astype(jnp.bfloat16)
     right_received = swap(right_sent, "c")
-    right_half = attention_terms(512, width, ci, right_sent)
-    right = ScatterSum(part_rows, add_low(right_half, right_received))
+    right_half = attention_terms(*right_terms, ci, right_sent)
+    right = ScatterSum(rows_of, add_low(right_half, right_received), (yi, 1 - yi))
     right.corner()
-    d_projected = jnp.concatenate(after((d_queries, d_keys, d_values), *right.sent), axis=1)
-    d_normed = times_transposed(d_projected, qkv_matrix)
+    parts = [array for pair in zip(part_a, right_parts) for array in pair]
+    d_normed = project_back(after(parts, *right.sent, *left.got), matrices)
     right.plane(d_normed)
+    up_sum = exchange_quarters(up.total(*right.sent).reshape(4, rows, width))
     unused_first, first_pull = jax.vjp(norm_modulate, tokens, shift_attention, scale_attention)
     d_tokens_part, d_shift_attention, d_scale_attention = first_pull(after(d_normed, *right.sent))
     grad_low = (d_middle + d_tokens_part).astype(jnp.bfloat16)
+    grad_low, up_sum = lax.optimization_barrier((grad_low, up_sum))
+    mods = jnp.concatenate([d_shift_attention, d_scale_attention], axis=1).astype(jnp.bfloat16)
+    mods = jnp.concatenate([mods, mods_early], axis=1)
+    every_mods = to_all(mods.reshape(2, 3 * width)).reshape(32, 6 * width)
+    right.line(grad_low, mods)
     quarter_rows = half_rows // 2
     grad_first = swap(grad_low[half_rows : half_rows + quarter_rows], "y")
-    mods_late = jnp.concatenate([d_shift_attention, d_scale_attention], axis=1)
-    mods_late = mods_late.astype(jnp.bfloat16)
-    left_terms = left.total(grad_low)
-    right.line(grad_low, mods_late, left_terms)
-    late_every = to_all(after(mods_late, *right.sent)[0])
-    bias_terms = jnp.concatenate(
-        [
-            mods_late[0].astype(jnp.float32),
-            mods_early[0].astype(jnp.float32),
-            jnp.sum(after(d_queries, *right.sent), axis=0, dtype=jnp.float32),
-            jnp.sum(after(d_values, *right.sent), axis=0, dtype=jnp.float32),
-            jnp.sum(after(d_branch, *right.sent), axis=0, dtype=jnp.float32),
-            jnp.sum(after(d_before, *right.sent), axis=0, dtype=jnp.float32)
-            .reshape(4, 8, 144)
-            .transpose(1, 0, 2)
-            .reshape(-1),
-            jnp.sum(after(d_feed, *right.sent), axis=0, dtype=jnp.float32),
-        ]
-    )
+
+    def both_halves(own_rows, *received):
+        both = jnp.stack([own_rows, own_rows])
+        row = 0
+        for piece in received:
+            both = lax.dynamic_update_slice(both, piece[None], (1 - yi, row, 0))
+            row += piece.shape[0]
+        return both
+
+    left_totals = left.total(*right.sent)
+    down_sum, output_low, output_received, up_sum = after(
+        (down_sum, output_low, output_received, up_sum), *right.sent
+    )
+    output = both_halves(output_low[:half_rows], output_received)
+    grad_down = down_sum.reshape(-1)
+    grad_up = up_sum.reshape(4, rows, 8, 144).transpose(1, 2, 0, 3).reshape(-1)
+    up_sums = in_order(before_sums.reshape(4, width)).reshape(4, 8, 144).transpose(1, 0, 2)
+    bias_terms = bias_sums(
+        mods.reshape(6, width),
+        after((part_a[0], right_parts[0], part_a[2], right_parts[2]), *right.sent),
+        d_branch,
+        up_sums.reshape(4, width),
+        d_feed,
+    ).reshape(32, -1)
+    right_totals = right.total(left_totals, output, grad_down, grad_up, bias_terms)
+    sums = jnp.concatenate([left_totals, right_totals], axis=1).reshape(4, rows, width)
+    sums = exchange_quarters(sums)
+    every_mods, grad_first = lax.optimization_barrier((every_mods, grad_first))
     grad_last = swap(after(grad_low, grad_first)[half_rows + quarter_rows :], "y")
-    late_every, early_every = after((late_every, early_every), *right.sent)
-
-    late_width = late_every.shape[1]
-    grad_ada = jnp.concatenate(
-        [over_tokens(silu_cut, late_every), over_tokens(silu_cut, early_every)], axis=1
-    ).reshape(-1)
-    d_silu_rows = times_transposed(late_every, ada_rows[:, :late_width])
-    d_silu_rows = d_silu_rows + times_transposed(early_every, ada_rows[:, late_width:])
+    d_silu_rows = times_transposed(every_mods, ada_rows)
     d_silu_parts = jnp.repeat(d_silu_rows.reshape(16, 1, 2, rows), 2, axis=1)
     parts = exchange(
-        jnp.concatenate([d_silu_parts.reshape(32, 2 * rows), bias_terms.reshape(32, -1)], axis=1)
-    )
+        jnp.concatenate([d_silu_parts.reshape(32, 2 * rows), bias_terms], axis=1)
+    )
+    grad_ada = over_tokens(silu_cut, every_mods).reshape(-1)
+    parts, grad_last = lax.optimization_barrier((parts, grad_last))
     d_silu = parts[:, : 2 * rows].reshape(32, 2, rows).transpose(1, 0, 2).reshape(2, width)
     grad_bias = jnp.sum(parts[:, 2 * rows :], axis=0)
     unused_silu, silu_pull = jax.vjp(jax.nn.silu, conditioning.astype(jnp.float32))
     grad_cond = silu_pull(d_silu)[0].astype(jnp.bfloat16)
-
-    right_terms = right.total(d_silu_rows, grad_first)
-    sums = jnp.concatenate([left_terms, right_terms], axis=1).reshape(4, rows, width)
-    sums = lax.all_to_all(sums, ("c", "y"), 0, 0, tiled=True)
-    down_sum, output_low, output_received, grad_last = after(
-        (down_sum, output_low, output_received, grad_last), right_terms
-    )
-    grad_received = jnp.concatenate([grad_first, grad_last])
-    grad_up = after(up_sum, right_terms).reshape(4, rows, 8, 144).transpose(1, 2, 0, 3).reshape(-1)
-    def both_halves(own_rows, received):
-        first = jnp.where(yi == 0, own_rows, received)
-        second = jnp.where(yi == 0, received, own_rows)
-        return jnp.stack([first, second])
-
-    output = both_halves(output_low[:half_rows], output_received)
-    grad_input = both_halves(grad_low[:half_rows], grad_received)
-
-    grad_down = down_sum.reshape(-1)
+    grad_input = both_halves(grad_low[:half_rows], grad_first, grad_last)
     grad_qkv = jnp.concatenate([sums[0], sums[1], sums[2]], axis=1).reshape(-1)
     grad_proj = sums[3].reshape(-1)
     return (

time: 724 us -> 701 us (0.968)
  matrix products: 195 us -> 74.7 us
  Pallas kernels: 150 us -> 242 us
  local copies, waits for them, and re-layouts: 66.3 us -> 81.9 us
  other arithmetic: 104 us -> 92.2 us
    pallas_call x6 -> x9, Pallas kernels: 115 us -> 207 us  [the longest x3 94.2 us: quarter_call(): pl.pallas_call(body, grid_spec=pltpu.PrefetchScalarGridSpec(num_scalar_pr...]
    dot_general x6 -> x2, matrix products: 66.5 us -> 7.96 us  [times_transposed(): lax.dot_general(left, right, (((1,), (1,)), ((), ())), preferred_element_...]
    dot_general x3 -> x0, matrix products: 58 us -> none  [the longest x1 23.6 us: local_pairs(): jnp.dot(normed_feed, up_matrix, preferred_element_type=jnp.float32)]
    all_to_all x3 -> x0, starting transfers between devices: 13.3 us -> none  [the longest x1 4.54 us: local_pairs(): up_sum = lax.all_to_all(up_terms, ('c', 'y'), 0, 0, tiled=True)]
    ppermute x35 -> x41, starting transfers between devices: 26.3 us -> 39.3 us  [swap(): return lax.ppermute(array, axis, SWAP)]
    ppermute x0 -> x3, waiting for transfers between devices: none -> 9.78 us  [exchange_quarters(): lax.ppermute(entry, axes, [(i, i ^ 3) for i in range(4)])]
    all_to_all x6 -> x5, waiting for transfers between devices: 32.8 us -> 23 us  [exchange(): return lax.all_to_all(array, ALL, 0, 0, tiled=True)]
    convert_element_type x2 -> x1, other arithmetic: 10.5 us -> 0.82 us  [local_pairs(): d_branch = (gate_attention * d_middle).astype(jnp.bfloat16)]
  transfers between devices with their start and end apart: 72 -> 77, of which waited for: 12 -> 20; matrix products, arithmetic and copies ran while one was open for 43% -> 24% of each run, Pallas kernels for 21% -> 35%
where the time goes in v3:
time: 701 us; the launch traced here: 690 us
  Pallas kernels  242 us (35%)
  starting transfers between devices  106 us (15%)
  other arithmetic  92.2 us (13%)
  waiting for transfers between devices  90.4 us (13%)
  local copies, waits for them, and re-layouts  81.9 us (12%)
  matrix products  74.7 us (11%)
    pallas_call x3, Pallas kernels, quarter_call(): pl.pallas_call(body, grid_spec=pltpu.PrefetchScalarGridSpec(num_scalar_pr...  94.2 us
    pallas_call x3, Pallas kernels, attn_bwd(): pl.pallas_call(functools.partial(attn_bwd_kernel, tile=tile, first=first,...  77 us
    dot_general x13, matrix products, over_tokens(): lax.dot_general(left, right, (((0,), (0,)), ((), ())), preferred_element_...  57.1 us
    ppermute x41, waiting for transfers between devices, swap(): return lax.ppermute(array, axis, SWAP)  46 us
    ppermute x41, starting transfers between devices, swap(): return lax.ppermute(array, axis, SWAP)  39.3 us
    pallas_call x2, Pallas kernels, attn_fwd(): pl.pallas_call(functools.partial(attn_fwd_kernel, tile=tile, first=first)...  35.3 us
    all_to_all x5, starting transfers between devices, exchange(): return lax.all_to_all(array, ALL, 0, 0, tiled=True)  34.9 us
    unnamed x228, local copies, waits for them, and re-layouts  28.1 us
  transfers between devices with their start and end apart: 77, of which 20 were waited for; matrix products, arithmetic and copies ran while one was open for 24% of the time, Pallas kernels for 35%

profile of v3, /device:TPU:1, one launch (start us, length us, event | category | flops | bytes accessed | tf_op | source)
XLA Modules:
  0.0 690.2 jit_solution(13399376843625950776)
XLA Ops:
  25.9 22.8 %collective-permute-done.3 = bf16[512,1152]{1,0:T(8,128)(2,1)S(1)} collective-permute-done((bf16[512,1152]{1,0:T(8,128)(2,1)}, bf16[512,1152]{1,0:T(8,128)(2,1)S(1)}, u32[]{:S(2)}, u32[]{:S(2)}) %collective-permute-start.3) | collective-permute-done | bytes 1179680 | tf_op jit(solution)/shard_map/ppermute | solution.py:261
  57.1 9.0 %all-to-all-start = ((bf16[32,2,828]{2,1,0:T(2,128)(2,1)}), bf16[32,2,828]{2,1,0:T(2,128)(2,1)S(1)}, u32[]{:S(2)}, u32[]{:S(2)}) async-start(bf16[32,2,828]{2,1,0:T(2,128)(2,1)} %reshape.450), calls=%async_computation | async-start | bytes 229376 | tf_op jit(solution)/shard_map/all_to_all | solution.py:713
  71.8 13.7 %all-to-all-done = bf16[32,2,828]{2,1,0:T(2,128)(2,1)S(1)} async-done(((bf16[32,2,828]{2,1,0:T(2,128)(2,1)}), bf16[32,2,828]{2,1,0:T(2,128)(2,1)S(1)}, u32[]{:S(2)}, u32[]{:S(2)}) %all-to-all-start) | async-done | bytes 106016 | tf_op jit(solution)/shard_map/all_to_all | solution.py:713
  88.6 4.9 collective-permute-done.10
  103.5 10.4 %all-to-all-start.1 = ((f32[32,1,2304]{2,1,0:T(1,128)}), f32[32,1,2304]{2,1,0:T(1,128)S(1)}, u32[]{:S(2)}, u32[]{:S(2)}) async-start(f32[32,1,2304]{2,1,0:T(1,128)} %copy.67), calls=%async_computation.1 | async-start | bytes 589824 | tf_op jit(solution)/shard_map/all_to_all | solution.py:713
  143.6 19.3 %project.1 = (bf16[1024,1152]{1,0:T(8,128)(2,1)}, bf16[1024,1152]{1,0:T(8,128)(2,1)}, bf16[1024,1152]{1,0:T(8,128)(2,1)}, bf16[4,1152,1152]{2,1,0:T(8,128)(2,1)}) custom-call(s32[4]{0:T(128)} %pad_add_fusion.where_ref, bf16[1024,1152]{1,0:T(8,128)(2,1)} %fusion.9.x_ref, f32[1,1152]{1,0:T(1,128)} %broadcast_in_dim.27.query_ref, ...), custom_call_target="tpu_custom_call" | custom-call | flops 8153726976 | bytes 31457280 | tf_op jit(solution)/shard_map/project/pallas_call | solution.py:588
  170.3 4.3 collective-permute-start.24
  180.2 17.1 %attention_forward.2 = (bf16[1024,1152]{1,0:T(8,128)(2,1)S(1)}, f32[1024,128]{1,0:T(8,128)S(1)}) custom-call(bf16[1024,1152]{1,0:T(8,128)(2,1)S(1)} %copy-done.24, bf16[1024,1152]{1,0:T(8,128)(2,1)S(1)} %copy-done.25, bf16[1024,1152]{1,0:T(8,128)(2,1)S(1)} %copy-done.27), custom_call_target="tpu_custom_call" | custom-call | flops 8589934592 | bytes 9437184 | tf_op jit(solution)/shard_map/attention_forward/pallas_call | solution.py:161
  206.3 18.1 %attention_forward.3 = (bf16[1024,1152]{1,0:T(8,128)(2,1)S(1)}, f32[1024,128]{1,0:T(8,128)S(1)}) custom-call(bf16[1024,1152]{1,0:T(8,128)(2,1)S(1)} %copy-done.24, bf16[1024,1152]{1,0:T(8,128)(2,1)S(1)} %copy-done.26, bf16[1024,1152]{1,0:T(8,128)(2,1)S(1)} %copy-done.28, bf16[1024,1152]{1,0:T(8,128)(2,1)S(1)} %copy-done.30, ...), custom_call_target="tpu_custom_call" | custom-call | flops 8589934592 | bytes 9437184 | tf_op jit(solution)/shard_map/attention_forward/pallas_call | solution.py:161
  224.5 8.3 %fusion.105 = (f32[1024]{0:T(1024)S(1)}, f32[1024,1152]{1,0:T(8,128)S(1)}, f32[1024,1152]{1,0:T(8,128)}) fusion(f32[1152]{0:T(1024)S(1)} %get-tuple-element.300, bf16[512,1152]{1,0:T(8,128)(2,1)S(1)} %copy-done.37, bf16[512,1152]{1,0:T(8,128)(2,1)S(1)} %copy-done.33, f32[1152]{0:T(1024)S(1)} %get-tuple-element.368, ...), kind=kOutput, calls=%fused_computation.275 | convolution fusion | flops 2727345152 | bytes 16823296 | tf_op jit(solution)/shard_map/dot_general | solution.py:815
  245.7 25.4 %feed_up.1 = (bf16[1024,4608]{1,0:T(8,128)(2,1)}, bf16[1024,4608]{1,0:T(8,128)(2,1)}) custom-call(s32[4]{0:T(128)} %pad_add_fusion.where_ref, bf16[1024,1152]{1,0:T(8,128)(2,1)} %add_convert_fusion.3.x_ref, f32[1,4608]{1,0:T(1,128)} %bitcast.260, bf16[4,144,1152]{2,1,0:T(8,128)(2,1)} %pad_maximum_fusion.8.refs_0_.refs_8_, ...), custom_call_target="tpu_custom_call" | custom-call | flops 10871635968 | bytes 31457280 | tf_op jit(solution)/shard_map/feed_up/pallas_call | solution.py:392
  275.6 28.0 %feed_down.1 = (f32[1024,1152]{1,0:T(8,128)}, bf16[1024,1152]{1,0:T(8,128)(2,1)}) custom-call(s32[4]{0:T(128)} %pad_add_fusion.where_ref, bf16[1024,4608]{1,0:T(8,128)(2,1)} %get-tuple-element.218.act_ref, f32[1024,1152]{1,0:T(8,128)} %copy-done.31, f32[1,1152]{1,0:T(1,128)} %get-tuple-element.375.gate_ref, f32[1,1152]{1,0:T(1,128)} %broadcast_in_dim.57.bias_ref, ...), custom_call_target="tpu_custom_call" | custom-call | flops 10871635968 | bytes 31457280 | tf_op jit(solution)/shard_map/feed_down/pallas_call | solution.py:392
  304.5 10.6 %convolution_convert_fusion.1 = bf16[2304,1152]{1,0:T(8,128)(2,1)} fusion(bf16[1024,1152]{1,0:T(8,128)(2,1)S(1)} %fusion.13.d_ref.feed_ref, bf16[1024,4608]{1,0:T(8,128)(2,1)} %get-tuple-element.218.act_ref), kind=kOutput, calls=%fused_computation.3 | convolution fusion | flops 5438472192 | bytes 12386304 | tf_op jit(solution)/shard_map/dot_general | solution.py:730
  318.3 6.0 collective-permute-done.35
  324.2 9.0 %add_convert_fusion = bf16[2304,1152]{1,0:T(8,128)(2,1)S(1)} fusion(bf16[2304,1152]{1,0:T(8,128)(2,1)} %collective-permute-done.35, bf16[1024,1152]{1,0:T(8,128)(2,1)S(1)} %fusion.13.d_ref.feed_ref, bf16[1024,4608]{1,0:T(8,128)(2,1)} %get-tuple-element.218.act_ref), kind=kOutput, calls=%fused_computation.4 | convolution fusion | flops 5443780608 | bytes 17694720 | tf_op jit(solution)/shard_map/dot_general | solution.py:730
  336.2 40.8 %feed_back.1 = (bf16[1024,4608]{1,0:T(8,128)(2,1)}, f32[1024,1152]{1,0:T(8,128)}, f32[1,4608]{1,0:T(1,128)}) custom-call(s32[4]{0:T(128)} %pad_add_fusion.where_ref, bf16[1024,1152]{1,0:T(8,128)(2,1)} %copy-done.1, bf16[1024,4608]{1,0:T(8,128)(2,1)} %get-tuple-element.220.slope_ref, bf16[4,144,1152]{2,1,0:T(8,128)(2,1)} %pad_maximum_fusion.9.refs_0_, ...), custom_call_target="tpu_custom_call" | custom-call | flops 21743271936 | bytes 31457280 | tf_op jit(solution)/shard_map/feed_back/pallas_call | solution.py:392
  381.1 9.8 %convolution_convert_fusion = bf16[1152,2304]{1,0:T(8,128)(2,1)} fusion(bf16[1024,1152]{1,0:T(8,128)(2,1)S(1)} %copy-done.55, bf16[1024,4608]{1,0:T(8,128)(2,1)} %get-tuple-element.227), kind=kOutput, calls=%fused_computation.2 | convolution fusion | flops 5438472192 | bytes 12386304 | tf_op jit(solution)/shard_map/dot_general | solution.py:730
  393.3 5.3 multiply_reduce_fusion
  404.7 7.7 %convolution_convert_fusion.2.g_ref = bf16[1024,1152]{1,0:T(8,128)(2,1)} fusion(bf16[1024,1152]{1,0:T(8,128)(2,1)S(1)} %multiply_convert_fusion.branch_ref, bf16[4,1152,1152]{2,1,0:T(8,128)(2,1)} %get-tuple-element.190.refs_6_), kind=kOutput, calls=%fused_computation.43 | convolution fusion | flops 2719088640 | bytes 7372800 | tf_op jit(solution)/shard_map/dot_general | solution.py:735
  412.4 7.7 %fusion = bf16[1152,2304]{1,0:T(8,128)(2,1)S(1)} fusion(bf16[1024,1152]{1,0:T(8,128)(2,1)S(1)} %copy-done.56, bf16[1152,2304]{1,0:T(8,128)(2,1)} %collective-permute-done.38, bf16[1024,4608]{1,0:T(8,128)(2,1)S(1)} %bitcast.262), kind=kOutput, calls=%fused_computation.1 | convolution fusion | flops 5443780608 | bytes 17694720 | tf_op jit(solution)/shard_map/dot_general | solution.py:730
  430.1 36.3 %attention_backward.3 = (bf16[1024,640]{1,0:T(8,128)(2,1)S(1)}, bf16[1024,640]{1,0:T(8,128)(2,1)}, bf16[1024,640]{1,0:T(8,128)(2,1)}) custom-call(bf16[1024,1152]{1,0:T(8,128)(2,1)} %get-tuple-element.188.q_ref, bf16[1024,1152]{1,0:T(8,128)(2,1)} %get-tuple-element.179.k_ref, bf16[1024,1152]{1,0:T(8,128)(2,1)} %get-tuple-element.174.v_ref, ...), custom_call_target="tpu_custom_call" | custom-call | flops 21474836480 | bytes 16515072 | tf_op jit(solution)/shard_map/attention_backward/pallas_call | solution.py:238
  483.8 20.2 %attention_backward.4 = (bf16[1024,384]{1,0:T(8,128)(2,1)S(1)}, bf16[1024,384]{1,0:T(8,128)(2,1)S(1)}, bf16[1024,384]{1,0:T(8,128)(2,1)}) custom-call(bf16[1024,1152]{1,0:T(8,128)(2,1)} %get-tuple-element.188.q_ref, bf16[1024,1152]{1,0:T(8,128)(2,1)} %get-tuple-element.179.k_ref, bf16[1024,1152]{1,0:T(8,128)(2,1)} %get-tuple-element.174.v_ref, ...), custom_call_target="tpu_custom_call" | custom-call | flops 10737418240 | bytes 16515072 | tf_op jit(solution)/shard_map/attention_backward/pallas_call | solution.py:238
  504.0 5.2 collective-permute-done.47
  509.4 6.5 collective-permute-done.46
  525.4 20.4 %attention_backward.5 = (bf16[1024,384]{1,0:T(8,128)(2,1)S(1)}, bf16[1024,384]{1,0:T(8,128)(2,1)S(1)}, bf16[1024,384]{1,0:T(8,128)(2,1)}) custom-call(bf16[1024,1152]{1,0:T(8,128)(2,1)} %get-tuple-element.188.q_ref, bf16[1024,1152]{1,0:T(8,128)(2,1)} %get-tuple-element.179.k_ref, bf16[1024,1152]{1,0:T(8,128)(2,1)} %get-tuple-element.174.v_ref, ...), custom_call_target="tpu_custom_call" | custom-call | flops 10737418240 | bytes 16515072 | tf_op jit(solution)/shard_map/attention_backward/pallas_call | solution.py:238
  579.3 4.3 fusion.5
  584.4 14.2 %project_back.1 = f32[1024,1152]{1,0:T(8,128)S(1)} custom-call(bf16[1024,640]{1,0:T(8,128)(2,1)S(1)} %copy-done.8, bf16[1024,640]{1,0:T(8,128)(2,1)S(1)} %get-tuple-element.278.refs_1_.qb_ref, bf16[1024,640]{1,0:T(8,128)(2,1)S(1)} %copy-done.23, bf16[1024,640]{1,0:T(8,128)(2,1)S(1)} %get-tuple-element.263.refs_3_, bf16[1024,640]{1,0:T(8,128)(2,1)S(1)} %copy-done.11, ...), custom_call_target="tpu_custom_call" | custom-call | flops 8153726976 | bytes 20971520 | tf_op jit(solution)/shard_map/project_back/pallas_call | solution.py:625
  614.3 11.0 %fusion.14 = (bf16[1152]{0:T(1024)(128)(2,1)S(1)}, bf16[1152]{0:T(1024)(128)(2,1)S(1)}, bf16[1024,1152]{1,0:T(8,128)(2,1)}) fusion(f32[1024,1152]{1,0:T(8,128)} %get-tuple-element.271, bf16[512,1152]{1,0:T(8,128)(2,1)} %copy-done.42, bf16[512,1152]{1,0:T(8,128)(2,1)} %get-tuple-element.316, f32[1024,1152]{1,0:T(8,128)} %get-tuple-element.380, ...), kind=kLoop, calls=%fused_computation.27 | loop fusion | flops 27129600 | bytes 25981952 | tf_op jit(solution)/shard_map/reduce_sum | solution.py:844
  626.5 4.4 all-to-all-start.3
  663.2 7.2 %all-to-all-start.4 = ((f32[32,1,576]{2,1,0:T(1,128)}), f32[32,1,576]{2,1,0:T(1,128)S(1)}, u32[]{:S(2)}, u32[]{:S(2)}) async-start(f32[32,1,576]{2,1,0:T(1,128)} %all_to_all.39), calls=%async_computation.4 | async-start | bytes 163840 | tf_op jit(solution)/shard_map/all_to_all | solution.py:713
  675.9 4.3 all-to-all-done.4
  680.2 5.7 collective-permute-done.71
  (543 shorter events, 269.1 us)
Async XLA Ops:
  51.3 42.2 %collective-permute-start.7 = (bf16[4,144,1152]{2,1,0:T(8,128)(2,1)}, bf16[4,144,1152]{2,1,0:T(8,128)(2,1)}, u32[]{:S(2)}, u32[]{:S(2)}) collective-permute-start(bf16[4,144,1152]{2,1,0:T(8,128)(2,1)} %pad_maximum_fusion.7.refs_0_), channel_id=1, source_target_pairs={{0,4},{4,0},{1,5},{5,1},{2,6},{6,2},{3,7},{7,3},{8,12},{12,8},{9,1... | collective-permute-start | bytes 3981320 | tf_op jit(solution)/shard_map/ppermute | solution.py:261
  52.9 40.7 %collective-permute-start.8 = (bf16[4,144,1152]{2,1,0:T(8,128)(2,1)}, bf16[4,144,1152]{2,1,0:T(8,128)(2,1)}, u32[]{:S(2)}, u32[]{:S(2)}) collective-permute-start(bf16[4,144,1152]{2,1,0:T(8,128)(2,1)} %pad_maximum_fusion.7.refs_0_), channel_id=1, source_target_pairs={{0,1},{1,0},{2,3},{3,2},{4,5},{5,4},{6,7},{7,6},{8,9},{9,8},{10,11... | collective-permute-start | bytes 3981320 | tf_op jit(solution)/shard_map/ppermute | solution.py:261
  57.1 28.4 %all-to-all-start = ((bf16[32,2,828]{2,1,0:T(2,128)(2,1)}), bf16[32,2,828]{2,1,0:T(2,128)(2,1)S(1)}, u32[]{:S(2)}, u32[]{:S(2)}) async-start(bf16[32,2,828]{2,1,0:T(2,128)(2,1)} %reshape.450), calls=%async_computation | async-start | bytes 229376 | tf_op jit(solution)/shard_map/all_to_all | solution.py:713
  129.3 33.6 %collective-permute-start.19 = (bf16[144,1152]{1,0:T(8,128)(2,1)}, bf16[144,1152]{1,0:T(8,128)(2,1)S(1)}, u32[]{:S(2)}, u32[]{:S(2)}) collective-permute-start(bf16[144,1152]{1,0:T(8,128)(2,1)} %reshape.383), channel_id=1, source_target_pairs={{0,8},{8,0},{16,24},{24,16},{1,9},{9,1},{17,25},{25,17},{2,10},{10... | collective-permute-start | bytes 995336 | tf_op jit(solution)/shard_map/ppermute | solution.py:266
  130.2 32.8 %collective-permute-start.20 = (bf16[144,1152]{1,0:T(8,128)(2,1)}, bf16[144,1152]{1,0:T(8,128)(2,1)}, u32[]{:S(2)}, u32[]{:S(2)}) collective-permute-start(bf16[144,1152]{1,0:T(8,128)(2,1)} %reshape.383), channel_id=1, source_target_pairs={{0,16},{8,24},{16,0},{24,8},{1,17},{9,25},{17,1},{25,9},{2,18},{10... | collective-permute-start | bytes 995336 | tf_op jit(solution)/shard_map/ppermute | solution.py:266
  131.9 31.1 %collective-permute-start.21 = (bf16[144,1152]{1,0:T(8,128)(2,1)}, bf16[144,1152]{1,0:T(8,128)(2,1)}, u32[]{:S(2)}, u32[]{:S(2)}) collective-permute-start(bf16[144,1152]{1,0:T(8,128)(2,1)} %reshape.383), channel_id=1, source_target_pairs={{0,24},{8,16},{16,8},{24,0},{1,25},{9,17},{17,9},{25,1},{2,26},{10... | collective-permute-start | bytes 995336 | tf_op jit(solution)/shard_map/ppermute | solution.py:266
  133.1 33.3 %collective-permute-start.17 = (bf16[4,144,1152]{2,1,0:T(8,128)(2,1)}, bf16[4,144,1152]{2,1,0:T(8,128)(2,1)}, u32[]{:S(2)}, u32[]{:S(2)}) collective-permute-start(bf16[4,144,1152]{2,1,0:T(8,128)(2,1)} %pad_maximum_fusion.8.refs_0_.refs_8_), channel_id=1, source_target_pairs={{0,4},{4,0},{1,5},{5,1},{2,6},{6,2},{3,7},{7,3},{8,12},{12,8},{9,1... | collective-permute-start | bytes 3981320 | tf_op jit(solution)/shard_map/ppermute | solution.py:261
  134.3 33.2 %collective-permute-start.18 = (bf16[4,144,1152]{2,1,0:T(8,128)(2,1)}, bf16[4,144,1152]{2,1,0:T(8,128)(2,1)}, u32[]{:S(2)}, u32[]{:S(2)}) collective-permute-start(bf16[4,144,1152]{2,1,0:T(8,128)(2,1)} %pad_maximum_fusion.8.refs_0_.refs_8_), channel_id=1, source_target_pairs={{0,1},{1,0},{2,3},{3,2},{4,5},{5,4},{6,7},{7,6},{8,9},{9,8},{10,11... | collective-permute-start | bytes 3981320 | tf_op jit(solution)/shard_map/ppermute | solution.py:261
  139.7 36.3 %all-to-all-start.2 = ((f32[32,1,4608]{2,1,0:T(1,128)}), f32[32,1,4608]{2,1,0:T(1,128)S(1)}, u32[]{:S(2)}, u32[]{:S(2)}) async-start(f32[32,1,4608]{2,1,0:T(1,128)} %copy.68), calls=%async_computation.2 | async-start | bytes 1179648 | tf_op jit(solution)/shard_map/all_to_all | solution.py:713
  165.5 35.0 %collective-permute-start.23 = (bf16[4,144,1152]{2,1,0:T(8,128)(2,1)}, bf16[4,144,1152]{2,1,0:T(8,128)(2,1)}, u32[]{:S(2)}, u32[]{:S(2)}) collective-permute-start(bf16[4,144,1152]{2,1,0:T(8,128)(2,1)} %pad_maximum_fusion.8.refs_0_.refs_8_), channel_id=1, source_target_pairs={{0,2},{2,0},{1,3},{3,1},{4,6},{6,4},{5,7},{7,5},{8,10},{10,8},{9,1... | collective-permute-start | bytes 3981320 | tf_op jit(solution)/shard_map/ppermute | solution.py:261
  170.1 30.4 %collective-permute-start.22 = (bf16[4,144,1152]{2,1,0:T(8,128)(2,1)}, bf16[4,144,1152]{2,1,0:T(8,128)(2,1)}, u32[]{:S(2)}, u32[]{:S(2)}) collective-permute-start(bf16[4,144,1152]{2,1,0:T(8,128)(2,1)} %broadcast_select_fusion.1), channel_id=1, source_target_pairs={{0,1},{1,0},{2,6},{3,7},{4,5},{5,4},{6,2},{7,3},{8,9},{9,8},{10,14... | collective-permute-start | bytes 3981320 | tf_op jit(solution)/shard_map/ppermute | solution.py:280
  170.3 30.2 %collective-permute-start.24 = (bf16[4,144,1152]{2,1,0:T(8,128)(2,1)}, bf16[4,144,1152]{2,1,0:T(8,128)(2,1)}, u32[]{:S(2)}, u32[]{:S(2)}) collective-permute-start(bf16[4,144,1152]{2,1,0:T(8,128)(2,1)} %collective-permute-done.17.refs_1_.refs_9_), channel_id=1, source_target_pairs={{0,2},{2,0},{1,3},{3,1},{4,6},{6,4},{5,7},{7,5},{8,10},{10,8},{9,1... | collective-permute-start | bytes 3981320 | tf_op jit(solution)/shard_map/ppermute | solution.py:261
  200.5 38.3 %collective-permute-start.27 = (bf16[4,144,1152]{2,1,0:T(8,128)(2,1)}, bf16[4,144,1152]{2,1,0:T(8,128)(2,1)}, u32[]{:S(2)}, u32[]{:S(2)}) collective-permute-start(bf16[4,144,1152]{2,1,0:T(8,128)(2,1)} %pad_maximum_fusion.9.refs_0_), channel_id=1, source_target_pairs={{0,4},{4,0},{1,5},{5,1},{2,6},{6,2},{3,7},{7,3},{8,12},{12,8},{9,1... | collective-permute-start | bytes 3981320 | tf_op jit(solution)/shard_map/ppermute | solution.py:261
  201.3 37.6 %collective-permute-start.28 = (bf16[4,144,1152]{2,1,0:T(8,128)(2,1)}, bf16[4,144,1152]{2,1,0:T(8,128)(2,1)}, u32[]{:S(2)}, u32[]{:S(2)}) collective-permute-start(bf16[4,144,1152]{2,1,0:T(8,128)(2,1)} %pad_maximum_fusion.9.refs_0_), channel_id=1, source_target_pairs={{0,1},{1,0},{2,3},{3,2},{4,5},{5,4},{6,7},{7,6},{8,9},{9,8},{10,11... | collective-permute-start | bytes 3981320 | tf_op jit(solution)/shard_map/ppermute | solution.py:261
  242.3 28.8 %collective-permute-start.32 = (bf16[4,144,1152]{2,1,0:T(8,128)(2,1)S(1)}, bf16[4,144,1152]{2,1,0:T(8,128)(2,1)}, u32[]{:S(2)}, u32[]{:S(2)}) collective-permute-start(bf16[4,144,1152]{2,1,0:T(8,128)(2,1)S(1)} %broadcast_select_fusion), channel_id=1, source_target_pairs={{0,1},{1,0},{2,6},{3,7},{4,5},{5,4},{6,2},{7,3},{8,9},{9,8},{10,14... | collective-permute-start | bytes 3981320 | tf_op jit(solution)/shard_map/ppermute | solution.py:280
  271.5 32.0 %collective-permute-start.33 = (bf16[512,1152]{1,0:T(8,128)(2,1)S(1)}, bf16[512,1152]{1,0:T(8,128)(2,1)S(1)}, u32[]{:S(2)}, u32[]{:S(2)}) collective-permute-start(bf16[512,1152]{1,0:T(8,128)(2,1)S(1)} %get-tuple-element.194), channel_id=1, source_target_pairs={{0,1},{1,0},{2,3},{3,2},{4,5},{5,4},{6,7},{7,6},{8,9},{9,8},{10,11... | collective-permute-start | bytes 3538952 | tf_op jit(solution)/shard_map/ppermute | solution.py:261
  317.9 59.1 %collective-permute-start.37 = (bf16[512,1152]{1,0:T(8,128)(2,1)}, bf16[512,1152]{1,0:T(8,128)(2,1)}, u32[]{:S(2)}, u32[]{:S(2)}) collective-permute-start(bf16[512,1152]{1,0:T(8,128)(2,1)} %slice.132), channel_id=1, source_target_pairs={{0,1},{1,0},{2,3},{3,2},{4,5},{5,4},{6,7},{7,6},{8,9},{9,8},{10,11... | collective-permute-start | bytes 3538952 | tf_op jit(solution)/shard_map/ppermute | solution.py:261
  335.7 41.3 %collective-permute-start.36 = (bf16[4,144,1152]{2,1,0:T(8,128)(2,1)S(1)}, bf16[4,144,1152]{2,1,0:T(8,128)(2,1)S(1)}, u32[]{:S(2)}, u32[]{:S(2)}) collective-permute-start(bf16[4,144,1152]{2,1,0:T(8,128)(2,1)S(1)} %dynamic-slice_bitcast_fusion.1), channel_id=1, source_target_pairs={{0,4},{1,5},{2,3},{3,2},{4,0},{5,1},{6,7},{7,6},{8,12},{9,13},{10,... | collective-permute-start | bytes 3981320 | tf_op jit(solution)/shard_map/ppermute | solution.py:280
  392.2 31.0 %collective-permute-start.39 = (bf16[4,144,1152]{2,1,0:T(8,128)(2,1)}, bf16[4,144,1152]{2,1,0:T(8,128)(2,1)S(1)}, u32[]{:S(2)}, u32[]{:S(2)}) collective-permute-start(bf16[4,144,1152]{2,1,0:T(8,128)(2,1)} %get-tuple-element.310), channel_id=1, source_target_pairs={{0,1},{1,0},{2,3},{3,2},{4,5},{5,4},{6,7},{7,6},{8,9},{9,8},{10,11... | collective-permute-start | bytes 3981320 | tf_op jit(solution)/shard_map/ppermute | solution.py:261
  392.3 30.9 %collective-permute-start.40 = (bf16[4,144,1152]{2,1,0:T(8,128)(2,1)}, bf16[4,144,1152]{2,1,0:T(8,128)(2,1)S(1)}, u32[]{:S(2)}, u32[]{:S(2)}) collective-permute-start(bf16[4,144,1152]{2,1,0:T(8,128)(2,1)} %get-tuple-element.311), channel_id=1, source_target_pairs={{0,4},{4,0},{1,5},{5,1},{2,6},{6,2},{3,7},{7,3},{8,12},{12,8},{9,1... | collective-permute-start | bytes 3981320 | tf_op jit(solution)/shard_map/ppermute | solution.py:261
  425.2 41.2 %collective-permute-start.41 = (bf16[144,1152]{1,0:T(8,128)(2,1)S(1)}, bf16[144,1152]{1,0:T(8,128)(2,1)S(1)}, u32[]{:S(2)}, u32[]{:S(2)}) collective-permute-start(bf16[144,1152]{1,0:T(8,128)(2,1)S(1)} %get-tuple-element.327), channel_id=1, source_target_pairs={{0,8},{8,0},{16,24},{24,16},{1,9},{9,1},{17,25},{25,17},{2,10},{10... | collective-permute-start | bytes 995336 | tf_op jit(solution)/shard_map/ppermute | solution.py:266
  426.8 39.6 %collective-permute-start.42 = (bf16[144,1152]{1,0:T(8,128)(2,1)S(1)}, bf16[144,1152]{1,0:T(8,128)(2,1)S(1)}, u32[]{:S(2)}, u32[]{:S(2)}) collective-permute-start(bf16[144,1152]{1,0:T(8,128)(2,1)S(1)} %get-tuple-element.326), channel_id=1, source_target_pairs={{0,16},{8,24},{16,0},{24,8},{1,17},{9,25},{17,1},{25,9},{2,18},{10... | collective-permute-start | bytes 995336 | tf_op jit(solution)/shard_map/ppermute | solution.py:266
  428.6 37.8 %collective-permute-start.43 = (bf16[144,1152]{1,0:T(8,128)(2,1)S(1)}, bf16[144,1152]{1,0:T(8,128)(2,1)S(1)}, u32[]{:S(2)}, u32[]{:S(2)}) collective-permute-start(bf16[144,1152]{1,0:T(8,128)(2,1)S(1)} %get-tuple-element.325), channel_id=1, source_target_pairs={{0,24},{8,16},{16,8},{24,0},{1,25},{9,17},{17,9},{25,1},{2,26},{10... | collective-permute-start | bytes 995336 | tf_op jit(solution)/shard_map/ppermute | solution.py:266
  429.6 36.8 %collective-permute-start.44 = (bf16[4,144,1152]{2,1,0:T(8,128)(2,1)}, bf16[4,144,1152]{2,1,0:T(8,128)(2,1)S(1)}, u32[]{:S(2)}, u32[]{:S(2)}) collective-permute-start(bf16[4,144,1152]{2,1,0:T(8,128)(2,1)} %dynamic-slice_bitcast_fusion), channel_id=1, source_target_pairs={{0,4},{1,5},{2,3},{3,2},{4,0},{5,1},{6,7},{7,6},{8,12},{9,13},{10,... | collective-permute-start | bytes 3981320 | tf_op jit(solution)/shard_map/ppermute | solution.py:280
  478.2 31.0 %collective-permute-start.47 = (bf16[4,144,1152]{2,1,0:T(8,128)(2,1)}, bf16[4,144,1152]{2,1,0:T(8,128)(2,1)}, u32[]{:S(2)}, u32[]{:S(2)}) collective-permute-start(bf16[4,144,1152]{2,1,0:T(8,128)(2,1)} %get-tuple-element.309), channel_id=1, source_target_pairs={{0,1},{1,0},{2,3},{3,2},{4,5},{5,4},{6,7},{7,6},{8,9},{9,8},{10,11... | collective-permute-start | bytes 3981320 | tf_op jit(solution)/shard_map/ppermute | solution.py:261
  478.6 30.7 %collective-permute-start.48 = (bf16[4,144,1152]{2,1,0:T(8,128)(2,1)}, bf16[4,144,1152]{2,1,0:T(8,128)(2,1)}, u32[]{:S(2)}, u32[]{:S(2)}) collective-permute-start(bf16[4,144,1152]{2,1,0:T(8,128)(2,1)} %get-tuple-element.308), channel_id=1, source_target_pairs={{0,4},{4,0},{1,5},{5,1},{2,6},{6,2},{3,7},{7,3},{8,12},{12,8},{9,1... | collective-permute-start | bytes 3981320 | tf_op jit(solution)/shard_map/ppermute | solution.py:261
  483.0 32.8 %collective-permute-start.46 = (bf16[4,144,512]{2,1,0:T(8,128)(2,1)S(1)}, bf16[4,144,512]{2,1,0:T(8,128)(2,1)S(1)}, u32[]{:S(2)}, u32[]{:S(2)}) collective-permute-start(bf16[4,144,512]{2,1,0:T(8,128)(2,1)S(1)} %dynamic-slice_bitcast_fusion.7), channel_id=1, source_target_pairs={{0,4},{1,5},{2,3},{3,2},{4,0},{5,1},{6,7},{7,6},{8,12},{9,13},{10,... | collective-permute-start | bytes 1769480 | tf_op jit(solution)/shard_map/ppermute | solution.py:280
  600.2 36.3 %collective-permute-start.62 = (bf16[4,144,640]{2,1,0:T(8,128)(2,1)}, bf16[4,144,640]{2,1,0:T(8,128)(2,1)}, u32[]{:S(2)}, u32[]{:S(2)}) collective-permute-start(bf16[4,144,640]{2,1,0:T(8,128)(2,1)} %get-tuple-element.313), channel_id=1, source_target_pairs={{0,1},{1,0},{2,3},{3,2},{4,5},{5,4},{6,7},{7,6},{8,9},{9,8},{10,11... | collective-permute-start | bytes 2211848 | tf_op jit(solution)/shard_map/ppermute | solution.py:261
  601.0 35.6 %collective-permute-start.63 = (bf16[4,144,640]{2,1,0:T(8,128)(2,1)}, bf16[4,144,640]{2,1,0:T(8,128)(2,1)}, u32[]{:S(2)}, u32[]{:S(2)}) collective-permute-start(bf16[4,144,640]{2,1,0:T(8,128)(2,1)} %get-tuple-element.312), channel_id=1, source_target_pairs={{0,4},{4,0},{1,5},{5,1},{2,6},{6,2},{3,7},{7,3},{8,12},{12,8},{9,1... | collective-permute-start | bytes 2211848 | tf_op jit(solution)/shard_map/ppermute | solution.py:261
  626.5 29.9 %all-to-all-start.3 = ((bf16[32,2,3456]{2,1,0:T(2,128)(2,1)}), bf16[32,2,3456]{2,1,0:T(2,128)(2,1)}, u32[]{:S(2)}, u32[]{:S(2)}) async-start(bf16[32,2,3456]{2,1,0:T(2,128)(2,1)} %broadcast_in_dim.63), calls=%async_computation.3 | async-start | bytes 884736 | tf_op jit(solution)/shard_map/all_to_all | solution.py:713
  639.5 30.9 %collective-permute-start.66 = (bf16[144,640]{1,0:T(8,128)(2,1)}, bf16[144,640]{1,0:T(8,128)(2,1)}, u32[]{:S(2)}, u32[]{:S(2)}) collective-permute-start(bf16[144,640]{1,0:T(8,128)(2,1)} %get-tuple-element.339), channel_id=1, source_target_pairs={{0,8},{8,0},{16,24},{24,16},{1,9},{9,1},{17,25},{25,17},{2,10},{10... | collective-permute-start | bytes 552968 | tf_op jit(solution)/shard_map/ppermute | solution.py:266
  640.7 29.8 %collective-permute-start.67 = (bf16[144,640]{1,0:T(8,128)(2,1)}, bf16[144,640]{1,0:T(8,128)(2,1)}, u32[]{:S(2)}, u32[]{:S(2)}) collective-permute-start(bf16[144,640]{1,0:T(8,128)(2,1)} %get-tuple-element.338), channel_id=1, source_target_pairs={{0,16},{8,24},{16,0},{24,8},{1,17},{9,25},{17,1},{25,9},{2,18},{10... | collective-permute-start | bytes 552968 | tf_op jit(solution)/shard_map/ppermute | solution.py:266
  (154 other events, 1776.2 us)

commit v4 on v3

--- a/solution.py
+++ b/solution.py
@@ -164,7 +164,7 @@
         in_specs=[whole(a) for a in ins],
         out_specs=[whole(a) for a in outs],
         out_shape=outs,
-        compiler_params=pltpu.CompilerParams(vmem_limit_bytes=40 << 20),
+        compiler_params=pltpu.CompilerParams(vmem_limit_bytes=60 << 20),
         cost_estimate=pl.CostEstimate(
             flops=4 * count * rows * keys * WIN,
             bytes_accessed=8 * rows * width,
@@ -241,7 +241,7 @@
         in_specs=specs,
         out_specs=[whole(a) for a in outs],
         out_shape=outs,
-        compiler_params=pltpu.CompilerParams(vmem_limit_bytes=52 << 20),
+        compiler_params=pltpu.CompilerParams(vmem_limit_bytes=60 << 20),
         cost_estimate=pl.CostEstimate(
             flops=10 * count * rows * keys * WIN,
             bytes_accessed=14 * rows * width,
@@ -354,6 +354,28 @@
                 )
             )
     return copies
+
+
+class Quarters:
+    def __init__(self, where_ref, pieces, buf, sems):
+        self.buf, self.first = buf, pl.program_id(0) == 0
+        self.loads = [
+            load_quarter(where_ref, pieces, i, buf.at[i], sems.at[i]) for i in range(4)
+        ]
+
+    def start(self, i):
+        @pl.when(self.first)
+        def _():
+            for copy in self.loads[i]:
+                copy.start()
+
+    def wait(self, i):
+        @pl.when(self.first)
+        def _():
+            for copy in self.loads[i]:
+                copy.wait()
+
+        return self.buf.at[i]
 
 
 def stream_quarters(where_ref, pieces, buf, sems):
@@ -457,43 +479,49 @@
 
     def body(where_ref, act_ref, middle_ref, gate_ref, bias_ref, *refs):
         ins, (feed_ref, out_ref, buf, sems) = refs[:8], refs[8:]
-        slot = stream_quarters(where_ref, ins, buf, sems)
-        weights = buf.at[slot]
-        step = pl.program_id(0)
-        for t in range(rows // TILE):
-            r = pl.ds(t * TILE, TILE)
-            term = jnp.dot(act_ref[r, :], weights[...], preferred_element_type=jnp.float32)
-
-            @pl.when(step == 0)
-            def _():
-                feed_ref[r, :] = term + bias_ref[...]
-
-            @pl.when((step > 0) & (step < 3))
-            def _():
-                feed_ref[r, :] += term
-
-            @pl.when(step == 3)
-            def _():
-                feed = feed_ref[r, :] + term
-                feed_ref[r, :] = feed
-                out_ref[r, :] = (middle_ref[r, :] + gate_ref[...] * feed).astype(jnp.bfloat16)
+        quarters = Quarters(where_ref, ins, buf, sems)
+        for i in range(4):
+            quarters.start(i)
+        feed = None
+        for i in range(4):
+            weights = quarters.wait(i)
+            term = jnp.dot(
+                act_ref[:, i * width : (i + 1) * width],
+                weights[...],
+                preferred_element_type=jnp.float32,
+            )
+            feed = term if feed is None else feed + term
+        feed = feed + bias_ref[...]
+        feed_ref[...] = feed
+        out_ref[...] = (middle_ref[...] + gate_ref[...] * feed).astype(jnp.bfloat16)
 
     outs = [
         jax.ShapeDtypeStruct((rows, width), jnp.float32),
         jax.ShapeDtypeStruct((rows, width), jnp.bfloat16),
     ]
-    return quarter_call(
+    def tiles(array):
+        return pl.BlockSpec((256, array.shape[1]), lambda i, w: (i, 0))
+
+    return pl.pallas_call(
         body,
-        where,
-        (activated, middle, gate, bias),
-        [moving(rows, width), fixed(middle), fixed(gate), fixed(bias)],
-        pieces,
-        outs,
-        [fixed(a) for a in outs],
-        quarter_scratch(width),
-        8 * rows * width * width,
-        "feed_down",
-    )
+        grid_spec=pltpu.PrefetchScalarGridSpec(
+            num_scalar_prefetch=1,
+            grid=(rows // 256,),
+            in_specs=[tiles(activated), tiles(middle), fixed(gate), fixed(bias)]
+            + [pl.BlockSpec(memory_space=pl.ANY)] * 8,
+            out_specs=[tiles(a) for a in outs],
+            scratch_shapes=[
+                pltpu.VMEM((4, width, width), jnp.bfloat16),
+                pltpu.SemaphoreType.DMA((4, 8)),
+            ],
+        ),
+        out_shape=outs,
+        compiler_params=pltpu.CompilerParams(vmem_limit_bytes=58 << 20),
+        cost_estimate=pl.CostEstimate(
+            flops=8 * rows * width * width, bytes_accessed=30 << 20, transcendentals=0
+        ),
+        name="feed_down",
+    )(where, activated, middle, gate, bias, *pieces)
 
 
 def feed_back(where, d_feed, slope, down_pieces, up_pieces):
@@ -877,22 +905,23 @@
         (0, 8),
     )
 
-    def attention_terms(gradients, d_b, core, *earlier):
+    def attention_terms(gradients, d_b, core, received, *earlier):
         d_q, d_k, d_v = gradients
         left = after(normed, *earlier)
         first = over_tokens(left, jnp.where(core == 0, d_q, d_v))
         second = over_tokens(
             jnp.where(core == 0, left, attended), jnp.where(core == 0, d_k, d_b)
         )
-        return jnp.concatenate([first, second])
+        if received is not None:
+            first, second = first + received[:width], second + received[width:]
+        return jnp.concatenate([first.astype(jnp.bfloat16), second.astype(jnp.bfloat16)])
 
     left_terms = [a[:, :512] for a in part_a], d_branch[:, :512]
-    left_sent = attention_terms(*left_terms, 1 - ci, *part_a, *down.got, *up.got)
-    left_sent = left_sent.astype(jnp.bfloat16)
+    left_sent = attention_terms(*left_terms, 1 - ci, None, *part_a, *down.got, *up.got)
     left_received = swap(left_sent, "c")
     up.plane(left_sent)
-    left_half = attention_terms(*left_terms, ci, left_sent, *up.sent)
-    left = ScatterSum(rows_of, add_low(left_half, left_received), (yi, 1 - yi))
+    left_half = attention_terms(*left_terms, ci, left_received, left_sent, *up.sent)
+    left = ScatterSum(rows_of, left_half, (yi, 1 - yi))
     left.corner()
     down_sum = down.total(left_half)
     part_b = attn_bwd(
@@ -922,10 +951,10 @@
     ]
     right_terms = right_parts, d_branch[:, 512:]
     left.line(*part_c)
-    right_sent = attention_terms(*right_terms, 1 - ci, *left.sent).astype(jnp.bfloat16)
+    right_sent = attention_terms(*right_terms, 1 - ci, None, *left.sent)
     right_received = swap(right_sent, "c")
-    right_half = attention_terms(*right_terms, ci, right_sent)
-    right = ScatterSum(rows_of, add_low(right_half, right_received), (yi, 1 - yi))
+    right_half = attention_terms(*right_terms, ci, right_received, right_sent)
+    right = ScatterSum(rows_of, right_half, (yi, 1 - yi))
     right.corner()
     parts = [array for pair in zip(part_a, right_parts) for array in pair]
     d_normed = project_back(after(parts, *right.sent, *left.got), matrices)

time: 701 us -> 695 us (level)
  local copies, waits for them, and re-layouts: 81.9 us -> 74.8 us
    pallas_call x3 -> x2, Pallas kernels: 94.2 us -> 66.4 us  [quarter_call(): pl.pallas_call(body, grid_spec=pltpu.PrefetchScalarGridSpec(num_scalar_pr...]
    pallas_call x0 -> x1, Pallas kernels: none -> 23.6 us  [feed_down(): pl.pallas_call(body, grid_spec=pltpu.PrefetchScalarGridSpec(num_scalar_pr...]
    pallas_call x2, Pallas kernels: 35.3 us -> 45.2 us  [attn_fwd(): pl.pallas_call(functools.partial(attn_fwd_kernel, tile=tile, first=first)...]
    unnamed x228 -> x214, local copies, waits for them, and re-layouts: 28.1 us -> 20.5 us
  transfers between devices with their start and end apart: 77 -> 77, of which waited for: 20 -> 20; matrix products, arithmetic and copies ran while one was open for 24% -> 23% of each run, Pallas kernels for 35% -> 36%
where the time goes in v4:
time: 695 us; the launch traced here: 684 us
  Pallas kernels  249 us (36%)
  starting transfers between devices  106 us (15%)
  other arithmetic  89.4 us (13%)
  waiting for transfers between devices  86.6 us (12%)
  matrix products  75.2 us (11%)
  local copies, waits for them, and re-layouts  74.8 us (11%)
    pallas_call x3, Pallas kernels, attn_bwd(): pl.pallas_call(functools.partial(attn_bwd_kernel, tile=tile, first=first,...  79.2 us
    pallas_call x2, Pallas kernels, quarter_call(): pl.pallas_call(body, grid_spec=pltpu.PrefetchScalarGridSpec(num_scalar_pr...  66.4 us
    dot_general x13, matrix products, over_tokens(): lax.dot_general(left, right, (((0,), (0,)), ((), ())), preferred_element_...  57.7 us
    pallas_call x2, Pallas kernels, attn_fwd(): pl.pallas_call(functools.partial(attn_fwd_kernel, tile=tile, first=first)...  45.2 us
    ppermute x41, waiting for transfers between devices, swap(): return lax.ppermute(array, axis, SWAP)  42.2 us
    ppermute x41, starting transfers between devices, swap(): return lax.ppermute(array, axis, SWAP)  39.8 us
    all_to_all x5, starting transfers between devices, exchange(): return lax.all_to_all(array, ALL, 0, 0, tiled=True)  35.2 us
    ppermute x21, starting transfers between devices, line_hops(): lax.ppermute(block_of(step), 'z', [(i, i ^ step) for i in range(4)])  26 us
  transfers between devices with their start and end apart: 77, of which 20 were waited for; matrix products, arithmetic and copies ran while one was open for 23% of the time, Pallas kernels for 36%

profile of v4, /device:TPU:1, one launch (start us, length us, event | category | flops | bytes accessed | tf_op | source)
XLA Modules:
  0.0 684.5 jit_solution(5520909589814435087)
XLA Ops:
  14.5 4.1 collective-permute-done.2
  25.9 22.8 %collective-permute-done.3 = bf16[512,1152]{1,0:T(8,128)(2,1)S(1)} collective-permute-done((bf16[512,1152]{1,0:T(8,128)(2,1)}, bf16[512,1152]{1,0:T(8,128)(2,1)S(1)}, u32[]{:S(2)}, u32[]{:S(2)}) %collective-permute-start.3) | collective-permute-done | bytes 1179680 | tf_op jit(solution)/shard_map/ppermute | solution.py:261
  57.1 9.0 %all-to-all-start = ((bf16[32,2,828]{2,1,0:T(2,128)(2,1)}), bf16[32,2,828]{2,1,0:T(2,128)(2,1)S(1)}, u32[]{:S(2)}, u32[]{:S(2)}) async-start(bf16[32,2,828]{2,1,0:T(2,128)(2,1)} %reshape.450), calls=%async_computation | async-start | bytes 229376 | tf_op jit(solution)/shard_map/all_to_all | solution.py:741
  71.8 13.7 %all-to-all-done = bf16[32,2,828]{2,1,0:T(2,128)(2,1)S(1)} async-done(((bf16[32,2,828]{2,1,0:T(2,128)(2,1)}), bf16[32,2,828]{2,1,0:T(2,128)(2,1)S(1)}, u32[]{:S(2)}, u32[]{:S(2)}) %all-to-all-start) | async-done | bytes 106016 | tf_op jit(solution)/shard_map/all_to_all | solution.py:741
  88.5 4.9 collective-permute-done.10
  103.4 10.4 %all-to-all-start.1 = ((f32[32,1,2304]{2,1,0:T(1,128)}), f32[32,1,2304]{2,1,0:T(1,128)S(1)}, u32[]{:S(2)}, u32[]{:S(2)}) async-start(f32[32,1,2304]{2,1,0:T(1,128)} %copy.67), calls=%async_computation.1 | async-start | bytes 589824 | tf_op jit(solution)/shard_map/all_to_all | solution.py:741
  144.2 19.3 %project.1 = (bf16[1024,1152]{1,0:T(8,128)(2,1)}, bf16[1024,1152]{1,0:T(8,128)(2,1)}, bf16[1024,1152]{1,0:T(8,128)(2,1)}, bf16[4,1152,1152]{2,1,0:T(8,128)(2,1)}) custom-call(s32[4]{0:T(128)} %pad_add_fusion.where_ref, bf16[1024,1152]{1,0:T(8,128)(2,1)} %fusion.8.x_ref, f32[1,1152]{1,0:T(1,128)} %broadcast_in_dim.27.query_ref, ...), custom_call_target="tpu_custom_call" | custom-call | flops 8153726976 | bytes 31457280 | tf_op jit(solution)/shard_map/project/pallas_call | solution.py:616
  170.9 4.3 collective-permute-start.24
  176.6 21.7 %attention_forward.2 = (bf16[1024,1152]{1,0:T(8,128)(2,1)}, f32[1024,128]{1,0:T(8,128)}) custom-call(bf16[1024,1152]{1,0:T(8,128)(2,1)} %get-tuple-element.188.q_ref, bf16[1024,1152]{1,0:T(8,128)(2,1)} %get-tuple-element.179.k_ref, bf16[1024,1152]{1,0:T(8,128)(2,1)} %get-tuple-element.174.v_ref), custom_call_target="tpu_custom_call" | custom-call | flops 8589934592 | bytes 9437184 | tf_op jit(solution)/shard_map/attention_forward/pallas_call | solution.py:161
  201.2 23.5 %attention_forward.3 = (bf16[1024,1152]{1,0:T(8,128)(2,1)}, f32[1024,128]{1,0:T(8,128)}) custom-call(bf16[1024,1152]{1,0:T(8,128)(2,1)} %get-tuple-element.188.q_ref, bf16[1024,1152]{1,0:T(8,128)(2,1)} %get-tuple-element.179.k_ref, bf16[1024,1152]{1,0:T(8,128)(2,1)} %get-tuple-element.174.v_ref, bf16[1024,1152]{1,0:T(8,128)(2,1)} %get-tuple-element.180.refs_0_, ...), custom_call_target="tpu_custom_call" | custom-call | flops 8589934592 | bytes 9437184 | tf_op jit(solution)/shard_map/attention_forward/pallas_call | solution.py:161
  224.7 8.2 %fusion.116 = (f32[1024]{0:T(1024)S(1)}, f32[1024,1152]{1,0:T(8,128)S(1)}, f32[1024,1152]{1,0:T(8,128)}) fusion(f32[1152]{0:T(1024)S(1)} %get-tuple-element.300, bf16[512,1152]{1,0:T(8,128)(2,1)S(1)} %collective-permute-done.3, bf16[512,1152]{1,0:T(8,128)(2,1)S(1)} %get-tuple-element.318, f32[1152]{0:T(1024)S(1)} %get-tuple-element.368, ...), kind=kOutput, calls=%fused_computation.277 | convolution fusion | flops 2727345152 | bytes 16823296 | tf_op jit(solution)/shard_map/dot_general | solution.py:843
  245.7 25.6 %feed_up.1 = (bf16[1024,4608]{1,0:T(8,128)(2,1)}, bf16[1024,4608]{1,0:T(8,128)(2,1)}) custom-call(s32[4]{0:T(128)} %pad_add_fusion.where_ref, bf16[1024,1152]{1,0:T(8,128)(2,1)} %add_convert_fusion.2.x_ref, f32[1,4608]{1,0:T(1,128)} %bitcast.260, bf16[4,144,1152]{2,1,0:T(8,128)(2,1)} %pad_maximum_fusion.9.refs_0_.refs_8_, ...), custom_call_target="tpu_custom_call" | custom-call | flops 10871635968 | bytes 31457280 | tf_op jit(solution)/shard_map/feed_up/pallas_call | solution.py:414
  275.8 23.6 %feed_down.1 = (f32[1024,1152]{1,0:T(8,128)}, bf16[1024,1152]{1,0:T(8,128)(2,1)}) custom-call(s32[4]{0:T(128)} %pad_add_fusion.where_ref, bf16[1024,4608]{1,0:T(8,128)(2,1)} %get-tuple-element.218.act_ref, f32[1024,1152]{1,0:T(8,128)} %copy-done.15, f32[1,1152]{1,0:T(1,128)} %get-tuple-element.375.gate_ref, f32[1,1152]{1,0:T(1,128)} %broadcast_in_dim.57.bias_ref, ...), custom_call_target="tpu_custom_call" | custom-call | flops 10871635968 | bytes 31457280 | tf_op jit(solution)/shard_map/feed_down/pallas_call | solution.py:505
  300.4 10.6 %convolution_convert_fusion.1 = bf16[2304,1152]{1,0:T(8,128)(2,1)} fusion(bf16[1024,1152]{1,0:T(8,128)(2,1)S(1)} %fusion.12.d_ref.feed_ref, bf16[1024,4608]{1,0:T(8,128)(2,1)} %get-tuple-element.218.act_ref), kind=kOutput, calls=%fused_computation.3 | convolution fusion | flops 5438472192 | bytes 12386304 | tf_op jit(solution)/shard_map/dot_general | solution.py:758
  314.5 6.0 collective-permute-done.35
  320.5 9.0 %add_convert_fusion = bf16[2304,1152]{1,0:T(8,128)(2,1)S(1)} fusion(bf16[2304,1152]{1,0:T(8,128)(2,1)} %collective-permute-done.35, bf16[1024,1152]{1,0:T(8,128)(2,1)S(1)} %fusion.12.d_ref.feed_ref, bf16[1024,4608]{1,0:T(8,128)(2,1)} %get-tuple-element.218.act_ref), kind=kOutput, calls=%fused_computation.4 | convolution fusion | flops 5443780608 | bytes 17694720 | tf_op jit(solution)/shard_map/dot_general | solution.py:758
  332.4 40.8 %feed_back.1 = (bf16[1024,4608]{1,0:T(8,128)(2,1)}, f32[1024,1152]{1,0:T(8,128)}, f32[1,4608]{1,0:T(1,128)}) custom-call(s32[4]{0:T(128)} %pad_add_fusion.where_ref, bf16[1024,1152]{1,0:T(8,128)(2,1)} %copy-done.1, bf16[1024,4608]{1,0:T(8,128)(2,1)} %get-tuple-element.220.slope_ref, bf16[4,144,1152]{2,1,0:T(8,128)(2,1)} %pad_maximum_fusion.10.refs_0_, ...), custom_call_target="tpu_custom_call" | custom-call | flops 21743271936 | bytes 31457280 | tf_op jit(solution)/shard_map/feed_back/pallas_call | solution.py:414
  373.3 4.1 fusion.46
  377.4 9.8 %convolution_convert_fusion = bf16[1152,2304]{1,0:T(8,128)(2,1)} fusion(bf16[1024,1152]{1,0:T(8,128)(2,1)S(1)} %copy-done.38, bf16[1024,4608]{1,0:T(8,128)(2,1)} %get-tuple-element.227), kind=kOutput, calls=%fused_computation.2 | convolution fusion | flops 5438472192 | bytes 12386304 | tf_op jit(solution)/shard_map/dot_general | solution.py:758
  390.2 5.4 multiply_reduce_fusion
  401.6 7.7 %convolution_convert_fusion.2.g_ref = bf16[1024,1152]{1,0:T(8,128)(2,1)} fusion(bf16[1024,1152]{1,0:T(8,128)(2,1)S(1)} %multiply_convert_fusion.branch_ref, bf16[4,1152,1152]{2,1,0:T(8,128)(2,1)} %get-tuple-element.190.refs_6_), kind=kOutput, calls=%fused_computation.39 | convolution fusion | flops 2719088640 | bytes 7372800 | tf_op jit(solution)/shard_map/dot_general | solution.py:763
  409.3 7.8 %fusion = bf16[1152,2304]{1,0:T(8,128)(2,1)S(1)} fusion(bf16[1024,1152]{1,0:T(8,128)(2,1)S(1)} %copy-done.39, bf16[1152,2304]{1,0:T(8,128)(2,1)} %collective-permute-done.38, bf16[1024,4608]{1,0:T(8,128)(2,1)S(1)} %bitcast.262), kind=kOutput, calls=%fused_computation.1 | convolution fusion | flops 5443780608 | bytes 17694720 | tf_op jit(solution)/shard_map/dot_general | solution.py:758
  427.1 37.0 %attention_backward.3 = (bf16[1024,640]{1,0:T(8,128)(2,1)}, bf16[1024,640]{1,0:T(8,128)(2,1)}, bf16[1024,640]{1,0:T(8,128)(2,1)}) custom-call(bf16[1024,1152]{1,0:T(8,128)(2,1)} %get-tuple-element.188.q_ref, bf16[1024,1152]{1,0:T(8,128)(2,1)} %get-tuple-element.179.k_ref, bf16[1024,1152]{1,0:T(8,128)(2,1)} %get-tuple-element.174.v_ref, ...), custom_call_target="tpu_custom_call" | custom-call | flops 21474836480 | bytes 16515072 | tf_op jit(solution)/shard_map/attention_backward/pallas_call | solution.py:238
  484.7 21.0 %attention_backward.4 = (bf16[1024,384]{1,0:T(8,128)(2,1)}, bf16[1024,384]{1,0:T(8,128)(2,1)}, bf16[1024,384]{1,0:T(8,128)(2,1)}) custom-call(bf16[1024,1152]{1,0:T(8,128)(2,1)} %get-tuple-element.188.q_ref, bf16[1024,1152]{1,0:T(8,128)(2,1)} %get-tuple-element.179.k_ref, bf16[1024,1152]{1,0:T(8,128)(2,1)} %get-tuple-element.174.v_ref, ...), custom_call_target="tpu_custom_call" | custom-call | flops 10737418240 | bytes 16515072 | tf_op jit(solution)/shard_map/attention_backward/pallas_call | solution.py:238
  507.4 6.5 collective-permute-done.46
  523.6 21.2 %attention_backward.5 = (bf16[1024,384]{1,0:T(8,128)(2,1)}, bf16[1024,384]{1,0:T(8,128)(2,1)}, bf16[1024,384]{1,0:T(8,128)(2,1)}) custom-call(bf16[1024,1152]{1,0:T(8,128)(2,1)} %get-tuple-element.188.q_ref, bf16[1024,1152]{1,0:T(8,128)(2,1)} %get-tuple-element.179.k_ref, bf16[1024,1152]{1,0:T(8,128)(2,1)} %get-tuple-element.174.v_ref, ...), custom_call_target="tpu_custom_call" | custom-call | flops 10737418240 | bytes 16515072 | tf_op jit(solution)/shard_map/attention_backward/pallas_call | solution.py:238
  579.6 13.8 %project_back.1 = f32[1024,1152]{1,0:T(8,128)S(1)} custom-call(bf16[1024,640]{1,0:T(8,128)(2,1)S(1)} %copy-done.8, bf16[1024,640]{1,0:T(8,128)(2,1)S(1)} %get-tuple-element.278.refs_1_.qb_ref, bf16[1024,640]{1,0:T(8,128)(2,1)S(1)} %copy-done.14, bf16[1024,640]{1,0:T(8,128)(2,1)S(1)} %get-tuple-element.263.refs_3_, bf16[1024,640]{1,0:T(8,128)(2,1)S(1)} %copy-done.11, ...), custom_call_target="tpu_custom_call" | custom-call | flops 8153726976 | bytes 20971520 | tf_op jit(solution)/shard_map/project_back/pallas_call | solution.py:653
  608.4 10.8 %fusion.13 = (bf16[1152]{0:T(1024)(128)(2,1)S(1)}, bf16[1152]{0:T(1024)(128)(2,1)S(1)}, bf16[1024,1152]{1,0:T(8,128)(2,1)}) fusion(f32[1024,1152]{1,0:T(8,128)} %get-tuple-element.271, bf16[512,1152]{1,0:T(8,128)(2,1)} %copy-done.23, bf16[512,1152]{1,0:T(8,128)(2,1)} %copy-done.21, f32[1024,1152]{1,0:T(8,128)} %get-tuple-element.380, ...), kind=kLoop, calls=%fused_computation.25 | loop fusion | flops 27129600 | bytes 25981952 | tf_op jit(solution)/shard_map/reduce_sum | solution.py:872
  620.4 4.7 all-to-all-start.3
  657.4 7.2 %all-to-all-start.4 = ((f32[32,1,576]{2,1,0:T(1,128)}), f32[32,1,576]{2,1,0:T(1,128)S(1)}, u32[]{:S(2)}, u32[]{:S(2)}) async-start(f32[32,1,576]{2,1,0:T(1,128)} %all_to_all.39), calls=%async_computation.4 | async-start | bytes 163840 | tf_op jit(solution)/shard_map/all_to_all | solution.py:741
  670.1 4.3 all-to-all-done.4
  674.5 5.7 collective-permute-done.71
  (529 shorter events, 256.9 us)
Async XLA Ops:
  51.3 42.2 %collective-permute-start.7 = (bf16[4,144,1152]{2,1,0:T(8,128)(2,1)}, bf16[4,144,1152]{2,1,0:T(8,128)(2,1)}, u32[]{:S(2)}, u32[]{:S(2)}) collective-permute-start(bf16[4,144,1152]{2,1,0:T(8,128)(2,1)} %pad_maximum_fusion.8.refs_0_), channel_id=1, source_target_pairs={{0,4},{4,0},{1,5},{5,1},{2,6},{6,2},{3,7},{7,3},{8,12},{12,8},{9,1... | collective-permute-start | bytes 3981320 | tf_op jit(solution)/shard_map/ppermute | solution.py:261
  52.8 40.7 %collective-permute-start.8 = (bf16[4,144,1152]{2,1,0:T(8,128)(2,1)}, bf16[4,144,1152]{2,1,0:T(8,128)(2,1)}, u32[]{:S(2)}, u32[]{:S(2)}) collective-permute-start(bf16[4,144,1152]{2,1,0:T(8,128)(2,1)} %pad_maximum_fusion.8.refs_0_), channel_id=1, source_target_pairs={{0,1},{1,0},{2,3},{3,2},{4,5},{5,4},{6,7},{7,6},{8,9},{9,8},{10,11... | collective-permute-start | bytes 3981320 | tf_op jit(solution)/shard_map/ppermute | solution.py:261
  129.9 33.6 %collective-permute-start.19 = (bf16[144,1152]{1,0:T(8,128)(2,1)}, bf16[144,1152]{1,0:T(8,128)(2,1)S(1)}, u32[]{:S(2)}, u32[]{:S(2)}) collective-permute-start(bf16[144,1152]{1,0:T(8,128)(2,1)} %reshape.383), channel_id=1, source_target_pairs={{0,8},{8,0},{16,24},{24,16},{1,9},{9,1},{17,25},{25,17},{2,10},{10... | collective-permute-start | bytes 995336 | tf_op jit(solution)/shard_map/ppermute | solution.py:266
  130.7 32.7 %collective-permute-start.20 = (bf16[144,1152]{1,0:T(8,128)(2,1)}, bf16[144,1152]{1,0:T(8,128)(2,1)}, u32[]{:S(2)}, u32[]{:S(2)}) collective-permute-start(bf16[144,1152]{1,0:T(8,128)(2,1)} %reshape.383), channel_id=1, source_target_pairs={{0,16},{8,24},{16,0},{24,8},{1,17},{9,25},{17,1},{25,9},{2,18},{10... | collective-permute-start | bytes 995336 | tf_op jit(solution)/shard_map/ppermute | solution.py:266
  132.5 31.0 %collective-permute-start.21 = (bf16[144,1152]{1,0:T(8,128)(2,1)}, bf16[144,1152]{1,0:T(8,128)(2,1)}, u32[]{:S(2)}, u32[]{:S(2)}) collective-permute-start(bf16[144,1152]{1,0:T(8,128)(2,1)} %reshape.383), channel_id=1, source_target_pairs={{0,24},{8,16},{16,8},{24,0},{1,25},{9,17},{17,9},{25,1},{2,26},{10... | collective-permute-start | bytes 995336 | tf_op jit(solution)/shard_map/ppermute | solution.py:266
  133.7 33.3 %collective-permute-start.17 = (bf16[4,144,1152]{2,1,0:T(8,128)(2,1)}, bf16[4,144,1152]{2,1,0:T(8,128)(2,1)}, u32[]{:S(2)}, u32[]{:S(2)}) collective-permute-start(bf16[4,144,1152]{2,1,0:T(8,128)(2,1)} %pad_maximum_fusion.9.refs_0_.refs_8_), channel_id=1, source_target_pairs={{0,4},{4,0},{1,5},{5,1},{2,6},{6,2},{3,7},{7,3},{8,12},{12,8},{9,1... | collective-permute-start | bytes 3981320 | tf_op jit(solution)/shard_map/ppermute | solution.py:261
  134.9 33.2 %collective-permute-start.18 = (bf16[4,144,1152]{2,1,0:T(8,128)(2,1)}, bf16[4,144,1152]{2,1,0:T(8,128)(2,1)}, u32[]{:S(2)}, u32[]{:S(2)}) collective-permute-start(bf16[4,144,1152]{2,1,0:T(8,128)(2,1)} %pad_maximum_fusion.9.refs_0_.refs_8_), channel_id=1, source_target_pairs={{0,1},{1,0},{2,3},{3,2},{4,5},{5,4},{6,7},{7,6},{8,9},{9,8},{10,11... | collective-permute-start | bytes 3981320 | tf_op jit(solution)/shard_map/ppermute | solution.py:261
  140.3 36.3 %all-to-all-start.2 = ((f32[32,1,4608]{2,1,0:T(1,128)}), f32[32,1,4608]{2,1,0:T(1,128)S(1)}, u32[]{:S(2)}, u32[]{:S(2)}) async-start(f32[32,1,4608]{2,1,0:T(1,128)} %copy.68), calls=%async_computation.2 | async-start | bytes 1179648 | tf_op jit(solution)/shard_map/all_to_all | solution.py:741
  166.1 34.3 %collective-permute-start.23 = (bf16[4,144,1152]{2,1,0:T(8,128)(2,1)}, bf16[4,144,1152]{2,1,0:T(8,128)(2,1)}, u32[]{:S(2)}, u32[]{:S(2)}) collective-permute-start(bf16[4,144,1152]{2,1,0:T(8,128)(2,1)} %pad_maximum_fusion.9.refs_0_.refs_8_), channel_id=1, source_target_pairs={{0,2},{2,0},{1,3},{3,1},{4,6},{6,4},{5,7},{7,5},{8,10},{10,8},{9,1... | collective-permute-start | bytes 3981320 | tf_op jit(solution)/shard_map/ppermute | solution.py:261
  170.7 29.7 %collective-permute-start.22 = (bf16[4,144,1152]{2,1,0:T(8,128)(2,1)}, bf16[4,144,1152]{2,1,0:T(8,128)(2,1)}, u32[]{:S(2)}, u32[]{:S(2)}) collective-permute-start(bf16[4,144,1152]{2,1,0:T(8,128)(2,1)} %broadcast_select_fusion.1), channel_id=1, source_target_pairs={{0,1},{1,0},{2,6},{3,7},{4,5},{5,4},{6,2},{7,3},{8,9},{9,8},{10,14... | collective-permute-start | bytes 3981320 | tf_op jit(solution)/shard_map/ppermute | solution.py:280
  170.9 29.5 %collective-permute-start.24 = (bf16[4,144,1152]{2,1,0:T(8,128)(2,1)}, bf16[4,144,1152]{2,1,0:T(8,128)(2,1)}, u32[]{:S(2)}, u32[]{:S(2)}) collective-permute-start(bf16[4,144,1152]{2,1,0:T(8,128)(2,1)} %collective-permute-done.17.refs_1_.refs_9_), channel_id=1, source_target_pairs={{0,2},{2,0},{1,3},{3,1},{4,6},{6,4},{5,7},{7,5},{8,10},{10,8},{9,1... | collective-permute-start | bytes 3981320 | tf_op jit(solution)/shard_map/ppermute | solution.py:261
  200.4 38.5 %collective-permute-start.27 = (bf16[4,144,1152]{2,1,0:T(8,128)(2,1)}, bf16[4,144,1152]{2,1,0:T(8,128)(2,1)}, u32[]{:S(2)}, u32[]{:S(2)}) collective-permute-start(bf16[4,144,1152]{2,1,0:T(8,128)(2,1)} %pad_maximum_fusion.10.refs_0_), channel_id=1, source_target_pairs={{0,4},{4,0},{1,5},{5,1},{2,6},{6,2},{3,7},{7,3},{8,12},{12,8},{9,1... | collective-permute-start | bytes 3981320 | tf_op jit(solution)/shard_map/ppermute | solution.py:261
  201.2 37.7 %collective-permute-start.28 = (bf16[4,144,1152]{2,1,0:T(8,128)(2,1)}, bf16[4,144,1152]{2,1,0:T(8,128)(2,1)}, u32[]{:S(2)}, u32[]{:S(2)}) collective-permute-start(bf16[4,144,1152]{2,1,0:T(8,128)(2,1)} %pad_maximum_fusion.10.refs_0_), channel_id=1, source_target_pairs={{0,1},{1,0},{2,3},{3,2},{4,5},{5,4},{6,7},{7,6},{8,9},{9,8},{10,11... | collective-permute-start | bytes 3981320 | tf_op jit(solution)/shard_map/ppermute | solution.py:261
  242.5 28.8 %collective-permute-start.32 = (bf16[4,144,1152]{2,1,0:T(8,128)(2,1)S(1)}, bf16[4,144,1152]{2,1,0:T(8,128)(2,1)}, u32[]{:S(2)}, u32[]{:S(2)}) collective-permute-start(bf16[4,144,1152]{2,1,0:T(8,128)(2,1)S(1)} %broadcast_select_fusion), channel_id=1, source_target_pairs={{0,1},{1,0},{2,6},{3,7},{4,5},{5,4},{6,2},{7,3},{8,9},{9,8},{10,14... | collective-permute-start | bytes 3981320 | tf_op jit(solution)/shard_map/ppermute | solution.py:280
  314.2 59.1 %collective-permute-start.37 = (bf16[512,1152]{1,0:T(8,128)(2,1)}, bf16[512,1152]{1,0:T(8,128)(2,1)}, u32[]{:S(2)}, u32[]{:S(2)}) collective-permute-start(bf16[512,1152]{1,0:T(8,128)(2,1)} %slice.144), channel_id=1, source_target_pairs={{0,1},{1,0},{2,3},{3,2},{4,5},{5,4},{6,7},{7,6},{8,9},{9,8},{10,11... | collective-permute-start | bytes 3538952 | tf_op jit(solution)/shard_map/ppermute | solution.py:261
  332.0 41.3 %collective-permute-start.36 = (bf16[4,144,1152]{2,1,0:T(8,128)(2,1)S(1)}, bf16[4,144,1152]{2,1,0:T(8,128)(2,1)S(1)}, u32[]{:S(2)}, u32[]{:S(2)}) collective-permute-start(bf16[4,144,1152]{2,1,0:T(8,128)(2,1)S(1)} %dynamic-slice_bitcast_fusion.1), channel_id=1, source_target_pairs={{0,4},{1,5},{2,3},{3,2},{4,0},{5,1},{6,7},{7,6},{8,12},{9,13},{10,... | collective-permute-start | bytes 3981320 | tf_op jit(solution)/shard_map/ppermute | solution.py:280
  389.1 31.0 %collective-permute-start.39 = (bf16[4,144,1152]{2,1,0:T(8,128)(2,1)}, bf16[4,144,1152]{2,1,0:T(8,128)(2,1)S(1)}, u32[]{:S(2)}, u32[]{:S(2)}) collective-permute-start(bf16[4,144,1152]{2,1,0:T(8,128)(2,1)} %get-tuple-element.310), channel_id=1, source_target_pairs={{0,1},{1,0},{2,3},{3,2},{4,5},{5,4},{6,7},{7,6},{8,9},{9,8},{10,11... | collective-permute-start | bytes 3981320 | tf_op jit(solution)/shard_map/ppermute | solution.py:261
  389.2 30.9 %collective-permute-start.40 = (bf16[4,144,1152]{2,1,0:T(8,128)(2,1)}, bf16[4,144,1152]{2,1,0:T(8,128)(2,1)S(1)}, u32[]{:S(2)}, u32[]{:S(2)}) collective-permute-start(bf16[4,144,1152]{2,1,0:T(8,128)(2,1)} %get-tuple-element.311), channel_id=1, source_target_pairs={{0,4},{4,0},{1,5},{5,1},{2,6},{6,2},{3,7},{7,3},{8,12},{12,8},{9,1... | collective-permute-start | bytes 3981320 | tf_op jit(solution)/shard_map/ppermute | solution.py:261
  422.1 42.1 %collective-permute-start.41 = (bf16[144,1152]{1,0:T(8,128)(2,1)S(1)}, bf16[144,1152]{1,0:T(8,128)(2,1)}, u32[]{:S(2)}, u32[]{:S(2)}) collective-permute-start(bf16[144,1152]{1,0:T(8,128)(2,1)S(1)} %get-tuple-element.327), channel_id=1, source_target_pairs={{0,8},{8,0},{16,24},{24,16},{1,9},{9,1},{17,25},{25,17},{2,10},{10... | collective-permute-start | bytes 995336 | tf_op jit(solution)/shard_map/ppermute | solution.py:266
  423.6 40.6 %collective-permute-start.42 = (bf16[144,1152]{1,0:T(8,128)(2,1)S(1)}, bf16[144,1152]{1,0:T(8,128)(2,1)}, u32[]{:S(2)}, u32[]{:S(2)}) collective-permute-start(bf16[144,1152]{1,0:T(8,128)(2,1)S(1)} %get-tuple-element.326), channel_id=1, source_target_pairs={{0,16},{8,24},{16,0},{24,8},{1,17},{9,25},{17,1},{25,9},{2,18},{10... | collective-permute-start | bytes 995336 | tf_op jit(solution)/shard_map/ppermute | solution.py:266
  425.5 38.7 %collective-permute-start.43 = (bf16[144,1152]{1,0:T(8,128)(2,1)S(1)}, bf16[144,1152]{1,0:T(8,128)(2,1)}, u32[]{:S(2)}, u32[]{:S(2)}) collective-permute-start(bf16[144,1152]{1,0:T(8,128)(2,1)S(1)} %get-tuple-element.325), channel_id=1, source_target_pairs={{0,24},{8,16},{16,8},{24,0},{1,25},{9,17},{17,9},{25,1},{2,26},{10... | collective-permute-start | bytes 995336 | tf_op jit(solution)/shard_map/ppermute | solution.py:266
  426.4 37.8 %collective-permute-start.44 = (bf16[4,144,1152]{2,1,0:T(8,128)(2,1)}, bf16[4,144,1152]{2,1,0:T(8,128)(2,1)}, u32[]{:S(2)}, u32[]{:S(2)}) collective-permute-start(bf16[4,144,1152]{2,1,0:T(8,128)(2,1)} %dynamic-slice_bitcast_fusion), channel_id=1, source_target_pairs={{0,4},{1,5},{2,3},{3,2},{4,0},{5,1},{6,7},{7,6},{8,12},{9,13},{10,... | collective-permute-start | bytes 3981320 | tf_op jit(solution)/shard_map/ppermute | solution.py:280
  476.2 31.0 %collective-permute-start.47 = (bf16[4,144,1152]{2,1,0:T(8,128)(2,1)}, bf16[4,144,1152]{2,1,0:T(8,128)(2,1)}, u32[]{:S(2)}, u32[]{:S(2)}) collective-permute-start(bf16[4,144,1152]{2,1,0:T(8,128)(2,1)} %get-tuple-element.309), channel_id=1, source_target_pairs={{0,1},{1,0},{2,3},{3,2},{4,5},{5,4},{6,7},{7,6},{8,9},{9,8},{10,11... | collective-permute-start | bytes 3981320 | tf_op jit(solution)/shard_map/ppermute | solution.py:261
  476.6 30.7 %collective-permute-start.48 = (bf16[4,144,1152]{2,1,0:T(8,128)(2,1)}, bf16[4,144,1152]{2,1,0:T(8,128)(2,1)}, u32[]{:S(2)}, u32[]{:S(2)}) collective-permute-start(bf16[4,144,1152]{2,1,0:T(8,128)(2,1)} %get-tuple-element.308), channel_id=1, source_target_pairs={{0,4},{4,0},{1,5},{5,1},{2,6},{6,2},{3,7},{7,3},{8,12},{12,8},{9,1... | collective-permute-start | bytes 3981320 | tf_op jit(solution)/shard_map/ppermute | solution.py:261
  481.9 32.0 %collective-permute-start.46 = (bf16[4,144,512]{2,1,0:T(8,128)(2,1)S(1)}, bf16[4,144,512]{2,1,0:T(8,128)(2,1)S(1)}, u32[]{:S(2)}, u32[]{:S(2)}) collective-permute-start(bf16[4,144,512]{2,1,0:T(8,128)(2,1)S(1)} %dynamic-slice_bitcast_fusion.7), channel_id=1, source_target_pairs={{0,4},{1,5},{2,3},{3,2},{4,0},{5,1},{6,7},{7,6},{8,12},{9,13},{10,... | collective-permute-start | bytes 1769480 | tf_op jit(solution)/shard_map/ppermute | solution.py:280
  517.5 29.8 %collective-permute-start.51 = (bf16[144,1152]{1,0:T(8,128)(2,1)}, bf16[144,1152]{1,0:T(8,128)(2,1)}, u32[]{:S(2)}, u32[]{:S(2)}) collective-permute-start(bf16[144,1152]{1,0:T(8,128)(2,1)} %get-tuple-element.323), channel_id=1, source_target_pairs={{0,8},{8,0},{16,24},{24,16},{1,9},{9,1},{17,25},{25,17},{2,10},{10... | collective-permute-start | bytes 995336 | tf_op jit(solution)/shard_map/ppermute | solution.py:266
  517.8 29.5 %collective-permute-start.52 = (bf16[144,1152]{1,0:T(8,128)(2,1)}, bf16[144,1152]{1,0:T(8,128)(2,1)}, u32[]{:S(2)}, u32[]{:S(2)}) collective-permute-start(bf16[144,1152]{1,0:T(8,128)(2,1)} %get-tuple-element.322), channel_id=1, source_target_pairs={{0,16},{8,24},{16,0},{24,8},{1,17},{9,25},{17,1},{25,9},{2,18},{10... | collective-permute-start | bytes 995336 | tf_op jit(solution)/shard_map/ppermute | solution.py:266
  595.0 35.8 %collective-permute-start.62 = (bf16[4,144,640]{2,1,0:T(8,128)(2,1)}, bf16[4,144,640]{2,1,0:T(8,128)(2,1)}, u32[]{:S(2)}, u32[]{:S(2)}) collective-permute-start(bf16[4,144,640]{2,1,0:T(8,128)(2,1)} %get-tuple-element.313), channel_id=1, source_target_pairs={{0,1},{1,0},{2,3},{3,2},{4,5},{5,4},{6,7},{7,6},{8,9},{9,8},{10,11... | collective-permute-start | bytes 2211848 | tf_op jit(solution)/shard_map/ppermute | solution.py:261
  595.9 34.9 %collective-permute-start.63 = (bf16[4,144,640]{2,1,0:T(8,128)(2,1)}, bf16[4,144,640]{2,1,0:T(8,128)(2,1)}, u32[]{:S(2)}, u32[]{:S(2)}) collective-permute-start(bf16[4,144,640]{2,1,0:T(8,128)(2,1)} %get-tuple-element.312), channel_id=1, source_target_pairs={{0,4},{4,0},{1,5},{5,1},{2,6},{6,2},{3,7},{7,3},{8,12},{12,8},{9,1... | collective-permute-start | bytes 2211848 | tf_op jit(solution)/shard_map/ppermute | solution.py:261
  620.4 30.3 %all-to-all-start.3 = ((bf16[32,2,3456]{2,1,0:T(2,128)(2,1)}), bf16[32,2,3456]{2,1,0:T(2,128)(2,1)}, u32[]{:S(2)}, u32[]{:S(2)}) async-start(bf16[32,2,3456]{2,1,0:T(2,128)(2,1)} %broadcast_in_dim.63), calls=%async_computation.3 | async-start | bytes 884736 | tf_op jit(solution)/shard_map/all_to_all | solution.py:741
  633.7 30.9 %collective-permute-start.66 = (bf16[144,640]{1,0:T(8,128)(2,1)}, bf16[144,640]{1,0:T(8,128)(2,1)}, u32[]{:S(2)}, u32[]{:S(2)}) collective-permute-start(bf16[144,640]{1,0:T(8,128)(2,1)} %get-tuple-element.339), channel_id=1, source_target_pairs={{0,8},{8,0},{16,24},{24,16},{1,9},{9,1},{17,25},{25,17},{2,10},{10... | collective-permute-start | bytes 552968 | tf_op jit(solution)/shard_map/ppermute | solution.py:266
  634.9 29.8 %collective-permute-start.67 = (bf16[144,640]{1,0:T(8,128)(2,1)}, bf16[144,640]{1,0:T(8,128)(2,1)}, u32[]{:S(2)}, u32[]{:S(2)}) collective-permute-start(bf16[144,640]{1,0:T(8,128)(2,1)} %get-tuple-element.338), channel_id=1, source_target_pairs={{0,16},{8,24},{16,0},{24,8},{1,17},{9,25},{17,1},{25,9},{2,18},{10... | collective-permute-start | bytes 552968 | tf_op jit(solution)/shard_map/ppermute | solution.py:266
  (147 other events, 1973.8 us)

commit v5 on v4

--- a/solution.py
+++ b/solution.py
@@ -782,7 +782,8 @@
     unit_u = after(unit_u, line_a)
     hops_u = line_hops(lambda step: unit_u)
     own_condition = lax.dynamic_index_in_dim(conditioning, yi, 0, False)
-    small = to_all(after(jnp.concatenate([bias_pack, own_condition]), line_a))
+    small = jnp.concatenate([bias_pack, own_condition]).reshape(2, -1)
+    small = to_all(after(small, line_a)).reshape(32, -1)
     bias_share = bias_pack.shape[0]
     biases = small[:, :bias_share].reshape(-1).astype(jnp.float32)
     conditions = small[:, bias_share:].astype(jnp.float32)

time: 695 us -> 693 us (level)
    unnamed x214 -> x211, local copies, waits for them, and re-layouts: 20.5 us -> 19.4 us
  transfers between devices with their start and end apart: 77 -> 77, of which waited for: 20 -> 20; matrix products, arithmetic and copies ran while one was open for 23% -> 23% of each run, Pallas kernels for 36% -> 37%
where the time goes in v5:
time: 693 us; the launch traced here: 683 us
  Pallas kernels  249 us (36%)
  starting transfers between devices  107 us (15%)
  other arithmetic  88.1 us (13%)
  waiting for transfers between devices  86.4 us (12%)
  matrix products  75.3 us (11%)
  local copies, waits for them, and re-layouts  74.1 us (11%)
    pallas_call x3, Pallas kernels, attn_bwd(): pl.pallas_call(functools.partial(attn_bwd_kernel, tile=tile, first=first,...  79.2 us
    pallas_call x2, Pallas kernels, quarter_call(): pl.pallas_call(body, grid_spec=pltpu.PrefetchScalarGridSpec(num_scalar_pr...  66.5 us
    dot_general x13, matrix products, over_tokens(): lax.dot_general(left, right, (((0,), (0,)), ((), ())), preferred_element_...  57.7 us
    pallas_call x2, Pallas kernels, attn_fwd(): pl.pallas_call(functools.partial(attn_fwd_kernel, tile=tile, first=first)...  45.2 us
    ppermute x41, waiting for transfers between devices, swap(): return lax.ppermute(array, axis, SWAP)  42 us
    ppermute x41, starting transfers between devices, swap(): return lax.ppermute(array, axis, SWAP)  39.7 us
    all_to_all x5, starting transfers between devices, exchange(): return lax.all_to_all(array, ALL, 0, 0, tiled=True)  35.5 us
    ppermute x21, starting transfers between devices, line_hops(): lax.ppermute(block_of(step), 'z', [(i, i ^ step) for i in range(4)])  25.9 us
  transfers between devices with their start and end apart: 77, of which 20 were waited for; matrix products, arithmetic and copies ran while one was open for 23% of the time, Pallas kernels for 37%

profile of v5, /device:TPU:1, one launch (start us, length us, event | category | flops | bytes accessed | tf_op | source)
XLA Modules:
  0.0 682.9 jit_solution(17222777465209744818)
XLA Ops:
  14.5 4.1 collective-permute-done.2
  25.9 22.8 %collective-permute-done.3 = bf16[512,1152]{1,0:T(8,128)(2,1)S(1)} collective-permute-done((bf16[512,1152]{1,0:T(8,128)(2,1)}, bf16[512,1152]{1,0:T(8,128)(2,1)S(1)}, u32[]{:S(2)}, u32[]{:S(2)}) %collective-permute-start.3) | collective-permute-done | bytes 1179680 | tf_op jit(solution)/shard_map/ppermute | solution.py:261
  55.2 9.0 %all-to-all-start = ((bf16[32,2,828]{2,1,0:T(2,128)(2,1)}), bf16[32,2,828]{2,1,0:T(2,128)(2,1)S(1)}, u32[]{:S(2)}, u32[]{:S(2)}) async-start(bf16[32,2,828]{2,1,0:T(2,128)(2,1)} %broadcast_in_dim.26), calls=%async_computation | async-start | bytes 229376 | tf_op jit(solution)/shard_map/all_to_all | solution.py:741
  69.8 15.7 %all-to-all-done = bf16[32,2,828]{2,1,0:T(2,128)(2,1)S(1)} async-done(((bf16[32,2,828]{2,1,0:T(2,128)(2,1)}), bf16[32,2,828]{2,1,0:T(2,128)(2,1)S(1)}, u32[]{:S(2)}, u32[]{:S(2)}) %all-to-all-start) | async-done | bytes 106016 | tf_op jit(solution)/shard_map/all_to_all | solution.py:741
  101.5 10.4 %all-to-all-start.1 = ((f32[32,1,2304]{2,1,0:T(1,128)}), f32[32,1,2304]{2,1,0:T(1,128)S(1)}, u32[]{:S(2)}, u32[]{:S(2)}) async-start(f32[32,1,2304]{2,1,0:T(1,128)} %copy.67), calls=%async_computation.1 | async-start | bytes 589824 | tf_op jit(solution)/shard_map/all_to_all | solution.py:741
  138.4 4.2 all-to-all-start.2
  142.6 19.3 %project.1 = (bf16[1024,1152]{1,0:T(8,128)(2,1)}, bf16[1024,1152]{1,0:T(8,128)(2,1)}, bf16[1024,1152]{1,0:T(8,128)(2,1)}, bf16[4,1152,1152]{2,1,0:T(8,128)(2,1)}) custom-call(s32[4]{0:T(128)} %pad_add_fusion.where_ref, bf16[1024,1152]{1,0:T(8,128)(2,1)} %fusion.8.x_ref, f32[1,1152]{1,0:T(1,128)} %broadcast_in_dim.27.query_ref, ...), custom_call_target="tpu_custom_call" | custom-call | flops 8153726976 | bytes 31457280 | tf_op jit(solution)/shard_map/project/pallas_call | solution.py:616
  169.0 4.3 collective-permute-start.24
  174.8 21.7 %attention_forward.2 = (bf16[1024,1152]{1,0:T(8,128)(2,1)}, f32[1024,128]{1,0:T(8,128)}) custom-call(bf16[1024,1152]{1,0:T(8,128)(2,1)} %get-tuple-element.188.q_ref, bf16[1024,1152]{1,0:T(8,128)(2,1)} %get-tuple-element.179.k_ref, bf16[1024,1152]{1,0:T(8,128)(2,1)} %get-tuple-element.174.v_ref), custom_call_target="tpu_custom_call" | custom-call | flops 8589934592 | bytes 9437184 | tf_op jit(solution)/shard_map/attention_forward/pallas_call | solution.py:161
  199.3 23.5 %attention_forward.3 = (bf16[1024,1152]{1,0:T(8,128)(2,1)}, f32[1024,128]{1,0:T(8,128)}) custom-call(bf16[1024,1152]{1,0:T(8,128)(2,1)} %get-tuple-element.188.q_ref, bf16[1024,1152]{1,0:T(8,128)(2,1)} %get-tuple-element.179.k_ref, bf16[1024,1152]{1,0:T(8,128)(2,1)} %get-tuple-element.174.v_ref, bf16[1024,1152]{1,0:T(8,128)(2,1)} %get-tuple-element.180.refs_0_, ...), custom_call_target="tpu_custom_call" | custom-call | flops 8589934592 | bytes 9437184 | tf_op jit(solution)/shard_map/attention_forward/pallas_call | solution.py:161
  222.8 8.2 %fusion.116 = (f32[1024]{0:T(1024)S(1)}, f32[1024,1152]{1,0:T(8,128)S(1)}, f32[1024,1152]{1,0:T(8,128)}) fusion(f32[1152]{0:T(1024)S(1)} %get-tuple-element.300, bf16[512,1152]{1,0:T(8,128)(2,1)S(1)} %collective-permute-done.3, bf16[512,1152]{1,0:T(8,128)(2,1)S(1)} %get-tuple-element.318, f32[1152]{0:T(1024)S(1)} %get-tuple-element.368, ...), kind=kOutput, calls=%fused_computation.276 | convolution fusion | flops 2727345152 | bytes 16823296 | tf_op jit(solution)/shard_map/dot_general | solution.py:844
  243.9 25.6 %feed_up.1 = (bf16[1024,4608]{1,0:T(8,128)(2,1)}, bf16[1024,4608]{1,0:T(8,128)(2,1)}) custom-call(s32[4]{0:T(128)} %pad_add_fusion.where_ref, bf16[1024,1152]{1,0:T(8,128)(2,1)} %add_convert_fusion.2.x_ref, f32[1,4608]{1,0:T(1,128)} %bitcast.255, bf16[4,144,1152]{2,1,0:T(8,128)(2,1)} %pad_maximum_fusion.9.refs_0_.refs_8_, ...), custom_call_target="tpu_custom_call" | custom-call | flops 10871635968 | bytes 31457280 | tf_op jit(solution)/shard_map/feed_up/pallas_call | solution.py:414
  273.9 23.6 %feed_down.1 = (f32[1024,1152]{1,0:T(8,128)}, bf16[1024,1152]{1,0:T(8,128)(2,1)}) custom-call(s32[4]{0:T(128)} %pad_add_fusion.where_ref, bf16[1024,4608]{1,0:T(8,128)(2,1)} %get-tuple-element.218.act_ref, f32[1024,1152]{1,0:T(8,128)} %copy-done.15, f32[1,1152]{1,0:T(1,128)} %get-tuple-element.375.gate_ref, f32[1,1152]{1,0:T(1,128)} %broadcast_in_dim.57.bias_ref, ...), custom_call_target="tpu_custom_call" | custom-call | flops 10871635968 | bytes 31457280 | tf_op jit(solution)/shard_map/feed_down/pallas_call | solution.py:505
  298.6 10.6 %convolution_convert_fusion.1 = bf16[2304,1152]{1,0:T(8,128)(2,1)} fusion(bf16[1024,1152]{1,0:T(8,128)(2,1)S(1)} %fusion.12.d_ref.feed_ref, bf16[1024,4608]{1,0:T(8,128)(2,1)} %get-tuple-element.218.act_ref), kind=kOutput, calls=%fused_computation.3 | convolution fusion | flops 5438472192 | bytes 12386304 | tf_op jit(solution)/shard_map/dot_general | solution.py:758
  312.7 5.9 collective-permute-done.35
  318.6 9.0 %add_convert_fusion = bf16[2304,1152]{1,0:T(8,128)(2,1)S(1)} fusion(bf16[2304,1152]{1,0:T(8,128)(2,1)} %collective-permute-done.35, bf16[1024,1152]{1,0:T(8,128)(2,1)S(1)} %fusion.12.d_ref.feed_ref, bf16[1024,4608]{1,0:T(8,128)(2,1)} %get-tuple-element.218.act_ref), kind=kOutput, calls=%fused_computation.4 | convolution fusion | flops 5443780608 | bytes 17694720 | tf_op jit(solution)/shard_map/dot_general | solution.py:758
  330.6 40.9 %feed_back.1 = (bf16[1024,4608]{1,0:T(8,128)(2,1)}, f32[1024,1152]{1,0:T(8,128)}, f32[1,4608]{1,0:T(1,128)}) custom-call(s32[4]{0:T(128)} %pad_add_fusion.where_ref, bf16[1024,1152]{1,0:T(8,128)(2,1)} %copy-done.1, bf16[1024,4608]{1,0:T(8,128)(2,1)} %get-tuple-element.220.slope_ref, bf16[4,144,1152]{2,1,0:T(8,128)(2,1)} %pad_maximum_fusion.10.refs_0_, ...), custom_call_target="tpu_custom_call" | custom-call | flops 21743271936 | bytes 31457280 | tf_op jit(solution)/shard_map/feed_back/pallas_call | solution.py:414
  371.5 4.1 fusion.46
  375.7 9.9 %convolution_convert_fusion = bf16[1152,2304]{1,0:T(8,128)(2,1)} fusion(bf16[1024,1152]{1,0:T(8,128)(2,1)S(1)} %copy-done.38, bf16[1024,4608]{1,0:T(8,128)(2,1)} %get-tuple-element.227), kind=kOutput, calls=%fused_computation.2 | convolution fusion | flops 5438472192 | bytes 12386304 | tf_op jit(solution)/shard_map/dot_general | solution.py:758
  388.5 5.4 multiply_reduce_fusion
  399.9 7.7 %convolution_convert_fusion.2.g_ref = bf16[1024,1152]{1,0:T(8,128)(2,1)} fusion(bf16[1024,1152]{1,0:T(8,128)(2,1)S(1)} %multiply_convert_fusion.branch_ref, bf16[4,1152,1152]{2,1,0:T(8,128)(2,1)} %get-tuple-element.190.refs_6_), kind=kOutput, calls=%fused_computation.39 | convolution fusion | flops 2719088640 | bytes 7372800 | tf_op jit(solution)/shard_map/dot_general | solution.py:763
  407.6 7.8 %fusion = bf16[1152,2304]{1,0:T(8,128)(2,1)S(1)} fusion(bf16[1024,1152]{1,0:T(8,128)(2,1)S(1)} %copy-done.39, bf16[1152,2304]{1,0:T(8,128)(2,1)} %collective-permute-done.38, bf16[1024,4608]{1,0:T(8,128)(2,1)S(1)} %bitcast.257), kind=kOutput, calls=%fused_computation.1 | convolution fusion | flops 5443780608 | bytes 17694720 | tf_op jit(solution)/shard_map/dot_general | solution.py:758
  425.4 37.0 %attention_backward.3 = (bf16[1024,640]{1,0:T(8,128)(2,1)}, bf16[1024,640]{1,0:T(8,128)(2,1)}, bf16[1024,640]{1,0:T(8,128)(2,1)}) custom-call(bf16[1024,1152]{1,0:T(8,128)(2,1)} %get-tuple-element.188.q_ref, bf16[1024,1152]{1,0:T(8,128)(2,1)} %get-tuple-element.179.k_ref, bf16[1024,1152]{1,0:T(8,128)(2,1)} %get-tuple-element.174.v_ref, ...), custom_call_target="tpu_custom_call" | custom-call | flops 21474836480 | bytes 16515072 | tf_op jit(solution)/shard_map/attention_backward/pallas_call | solution.py:238
  483.0 21.0 %attention_backward.4 = (bf16[1024,384]{1,0:T(8,128)(2,1)}, bf16[1024,384]{1,0:T(8,128)(2,1)}, bf16[1024,384]{1,0:T(8,128)(2,1)}) custom-call(bf16[1024,1152]{1,0:T(8,128)(2,1)} %get-tuple-element.188.q_ref, bf16[1024,1152]{1,0:T(8,128)(2,1)} %get-tuple-element.179.k_ref, bf16[1024,1152]{1,0:T(8,128)(2,1)} %get-tuple-element.174.v_ref, ...), custom_call_target="tpu_custom_call" | custom-call | flops 10737418240 | bytes 16515072 | tf_op jit(solution)/shard_map/attention_backward/pallas_call | solution.py:238
  505.6 6.5 collective-permute-done.46
  521.9 21.2 %attention_backward.5 = (bf16[1024,384]{1,0:T(8,128)(2,1)}, bf16[1024,384]{1,0:T(8,128)(2,1)}, bf16[1024,384]{1,0:T(8,128)(2,1)}) custom-call(bf16[1024,1152]{1,0:T(8,128)(2,1)} %get-tuple-element.188.q_ref, bf16[1024,1152]{1,0:T(8,128)(2,1)} %get-tuple-element.179.k_ref, bf16[1024,1152]{1,0:T(8,128)(2,1)} %get-tuple-element.174.v_ref, ...), custom_call_target="tpu_custom_call" | custom-call | flops 10737418240 | bytes 16515072 | tf_op jit(solution)/shard_map/attention_backward/pallas_call | solution.py:238
  577.9 13.8 %project_back.1 = f32[1024,1152]{1,0:T(8,128)S(1)} custom-call(bf16[1024,640]{1,0:T(8,128)(2,1)S(1)} %copy-done.8, bf16[1024,640]{1,0:T(8,128)(2,1)S(1)} %get-tuple-element.278.refs_1_.qb_ref, bf16[1024,640]{1,0:T(8,128)(2,1)S(1)} %copy-done.14, bf16[1024,640]{1,0:T(8,128)(2,1)S(1)} %get-tuple-element.263.refs_3_, bf16[1024,640]{1,0:T(8,128)(2,1)S(1)} %copy-done.11, ...), custom_call_target="tpu_custom_call" | custom-call | flops 8153726976 | bytes 20971520 | tf_op jit(solution)/shard_map/project_back/pallas_call | solution.py:653
  606.7 10.9 %fusion.13 = (bf16[1152]{0:T(1024)(128)(2,1)S(1)}, bf16[1152]{0:T(1024)(128)(2,1)S(1)}, bf16[1024,1152]{1,0:T(8,128)(2,1)}) fusion(f32[1024,1152]{1,0:T(8,128)} %get-tuple-element.271, bf16[512,1152]{1,0:T(8,128)(2,1)} %copy-done.23, bf16[512,1152]{1,0:T(8,128)(2,1)} %copy-done.21, f32[1024,1152]{1,0:T(8,128)} %get-tuple-element.380, ...), kind=kLoop, calls=%fused_computation.25 | loop fusion | flops 27129600 | bytes 25981952 | tf_op jit(solution)/shard_map/reduce_sum | solution.py:873
  618.8 4.7 all-to-all-start.3
  655.8 7.2 %all-to-all-start.4 = ((f32[32,1,576]{2,1,0:T(1,128)}), f32[32,1,576]{2,1,0:T(1,128)S(1)}, u32[]{:S(2)}, u32[]{:S(2)}) async-start(f32[32,1,576]{2,1,0:T(1,128)} %all_to_all.35), calls=%async_computation.4 | async-start | bytes 163840 | tf_op jit(solution)/shard_map/all_to_all | solution.py:741
  668.5 4.3 all-to-all-done.4
  672.9 5.7 collective-permute-done.71
  (526 shorter events, 254.0 us)
Async XLA Ops:
  51.3 40.3 %collective-permute-start.7 = (bf16[4,144,1152]{2,1,0:T(8,128)(2,1)}, bf16[4,144,1152]{2,1,0:T(8,128)(2,1)}, u32[]{:S(2)}, u32[]{:S(2)}) collective-permute-start(bf16[4,144,1152]{2,1,0:T(8,128)(2,1)} %pad_maximum_fusion.8.refs_0_), channel_id=1, source_target_pairs={{0,4},{4,0},{1,5},{5,1},{2,6},{6,2},{3,7},{7,3},{8,12},{12,8},{9,1... | collective-permute-start | bytes 3981320 | tf_op jit(solution)/shard_map/ppermute | solution.py:261
  52.8 38.8 %collective-permute-start.8 = (bf16[4,144,1152]{2,1,0:T(8,128)(2,1)}, bf16[4,144,1152]{2,1,0:T(8,128)(2,1)}, u32[]{:S(2)}, u32[]{:S(2)}) collective-permute-start(bf16[4,144,1152]{2,1,0:T(8,128)(2,1)} %pad_maximum_fusion.8.refs_0_), channel_id=1, source_target_pairs={{0,1},{1,0},{2,3},{3,2},{4,5},{5,4},{6,7},{7,6},{8,9},{9,8},{10,11... | collective-permute-start | bytes 3981320 | tf_op jit(solution)/shard_map/ppermute | solution.py:261
  55.2 30.3 %all-to-all-start = ((bf16[32,2,828]{2,1,0:T(2,128)(2,1)}), bf16[32,2,828]{2,1,0:T(2,128)(2,1)S(1)}, u32[]{:S(2)}, u32[]{:S(2)}) async-start(bf16[32,2,828]{2,1,0:T(2,128)(2,1)} %broadcast_in_dim.26), calls=%async_computation | async-start | bytes 229376 | tf_op jit(solution)/shard_map/all_to_all | solution.py:741
  128.0 33.9 %collective-permute-start.19 = (bf16[144,1152]{1,0:T(8,128)(2,1)}, bf16[144,1152]{1,0:T(8,128)(2,1)S(1)}, u32[]{:S(2)}, u32[]{:S(2)}) collective-permute-start(bf16[144,1152]{1,0:T(8,128)(2,1)} %reshape.387), channel_id=1, source_target_pairs={{0,8},{8,0},{16,24},{24,16},{1,9},{9,1},{17,25},{25,17},{2,10},{10... | collective-permute-start | bytes 995336 | tf_op jit(solution)/shard_map/ppermute | solution.py:266
  128.9 33.1 %collective-permute-start.20 = (bf16[144,1152]{1,0:T(8,128)(2,1)}, bf16[144,1152]{1,0:T(8,128)(2,1)}, u32[]{:S(2)}, u32[]{:S(2)}) collective-permute-start(bf16[144,1152]{1,0:T(8,128)(2,1)} %reshape.387), channel_id=1, source_target_pairs={{0,16},{8,24},{16,0},{24,8},{1,17},{9,25},{17,1},{25,9},{2,18},{10... | collective-permute-start | bytes 995336 | tf_op jit(solution)/shard_map/ppermute | solution.py:266
  130.6 31.4 %collective-permute-start.21 = (bf16[144,1152]{1,0:T(8,128)(2,1)}, bf16[144,1152]{1,0:T(8,128)(2,1)}, u32[]{:S(2)}, u32[]{:S(2)}) collective-permute-start(bf16[144,1152]{1,0:T(8,128)(2,1)} %reshape.387), channel_id=1, source_target_pairs={{0,24},{8,16},{16,8},{24,0},{1,25},{9,17},{17,9},{25,1},{2,26},{10... | collective-permute-start | bytes 995336 | tf_op jit(solution)/shard_map/ppermute | solution.py:266
  131.8 33.3 %collective-permute-start.17 = (bf16[4,144,1152]{2,1,0:T(8,128)(2,1)}, bf16[4,144,1152]{2,1,0:T(8,128)(2,1)}, u32[]{:S(2)}, u32[]{:S(2)}) collective-permute-start(bf16[4,144,1152]{2,1,0:T(8,128)(2,1)} %pad_maximum_fusion.9.refs_0_.refs_8_), channel_id=1, source_target_pairs={{0,4},{4,0},{1,5},{5,1},{2,6},{6,2},{3,7},{7,3},{8,12},{12,8},{9,1... | collective-permute-start | bytes 3981320 | tf_op jit(solution)/shard_map/ppermute | solution.py:261
  133.0 33.2 %collective-permute-start.18 = (bf16[4,144,1152]{2,1,0:T(8,128)(2,1)}, bf16[4,144,1152]{2,1,0:T(8,128)(2,1)}, u32[]{:S(2)}, u32[]{:S(2)}) collective-permute-start(bf16[4,144,1152]{2,1,0:T(8,128)(2,1)} %pad_maximum_fusion.9.refs_0_.refs_8_), channel_id=1, source_target_pairs={{0,1},{1,0},{2,3},{3,2},{4,5},{5,4},{6,7},{7,6},{8,9},{9,8},{10,11... | collective-permute-start | bytes 3981320 | tf_op jit(solution)/shard_map/ppermute | solution.py:261
  138.4 36.3 %all-to-all-start.2 = ((f32[32,1,4608]{2,1,0:T(1,128)}), f32[32,1,4608]{2,1,0:T(1,128)S(1)}, u32[]{:S(2)}, u32[]{:S(2)}) async-start(f32[32,1,4608]{2,1,0:T(1,128)} %copy.68), calls=%async_computation.2 | async-start | bytes 1179648 | tf_op jit(solution)/shard_map/all_to_all | solution.py:741
  164.5 34.0 %collective-permute-start.23 = (bf16[4,144,1152]{2,1,0:T(8,128)(2,1)}, bf16[4,144,1152]{2,1,0:T(8,128)(2,1)}, u32[]{:S(2)}, u32[]{:S(2)}) collective-permute-start(bf16[4,144,1152]{2,1,0:T(8,128)(2,1)} %pad_maximum_fusion.9.refs_0_.refs_8_), channel_id=1, source_target_pairs={{0,2},{2,0},{1,3},{3,1},{4,6},{6,4},{5,7},{7,5},{8,10},{10,8},{9,1... | collective-permute-start | bytes 3981320 | tf_op jit(solution)/shard_map/ppermute | solution.py:261
  168.8 29.8 %collective-permute-start.22 = (bf16[4,144,1152]{2,1,0:T(8,128)(2,1)}, bf16[4,144,1152]{2,1,0:T(8,128)(2,1)}, u32[]{:S(2)}, u32[]{:S(2)}) collective-permute-start(bf16[4,144,1152]{2,1,0:T(8,128)(2,1)} %broadcast_select_fusion.1), channel_id=1, source_target_pairs={{0,1},{1,0},{2,6},{3,7},{4,5},{5,4},{6,2},{7,3},{8,9},{9,8},{10,14... | collective-permute-start | bytes 3981320 | tf_op jit(solution)/shard_map/ppermute | solution.py:280
  169.0 29.6 %collective-permute-start.24 = (bf16[4,144,1152]{2,1,0:T(8,128)(2,1)}, bf16[4,144,1152]{2,1,0:T(8,128)(2,1)}, u32[]{:S(2)}, u32[]{:S(2)}) collective-permute-start(bf16[4,144,1152]{2,1,0:T(8,128)(2,1)} %collective-permute-done.17.refs_1_.refs_9_), channel_id=1, source_target_pairs={{0,2},{2,0},{1,3},{3,1},{4,6},{6,4},{5,7},{7,5},{8,10},{10,8},{9,1... | collective-permute-start | bytes 3981320 | tf_op jit(solution)/shard_map/ppermute | solution.py:261
  198.6 38.5 %collective-permute-start.27 = (bf16[4,144,1152]{2,1,0:T(8,128)(2,1)}, bf16[4,144,1152]{2,1,0:T(8,128)(2,1)}, u32[]{:S(2)}, u32[]{:S(2)}) collective-permute-start(bf16[4,144,1152]{2,1,0:T(8,128)(2,1)} %pad_maximum_fusion.10.refs_0_), channel_id=1, source_target_pairs={{0,4},{4,0},{1,5},{5,1},{2,6},{6,2},{3,7},{7,3},{8,12},{12,8},{9,1... | collective-permute-start | bytes 3981320 | tf_op jit(solution)/shard_map/ppermute | solution.py:261
  199.3 37.7 %collective-permute-start.28 = (bf16[4,144,1152]{2,1,0:T(8,128)(2,1)}, bf16[4,144,1152]{2,1,0:T(8,128)(2,1)}, u32[]{:S(2)}, u32[]{:S(2)}) collective-permute-start(bf16[4,144,1152]{2,1,0:T(8,128)(2,1)} %pad_maximum_fusion.10.refs_0_), channel_id=1, source_target_pairs={{0,1},{1,0},{2,3},{3,2},{4,5},{5,4},{6,7},{7,6},{8,9},{9,8},{10,11... | collective-permute-start | bytes 3981320 | tf_op jit(solution)/shard_map/ppermute | solution.py:261
  312.3 59.2 %collective-permute-start.37 = (bf16[512,1152]{1,0:T(8,128)(2,1)}, bf16[512,1152]{1,0:T(8,128)(2,1)}, u32[]{:S(2)}, u32[]{:S(2)}) collective-permute-start(bf16[512,1152]{1,0:T(8,128)(2,1)} %slice.144), channel_id=1, source_target_pairs={{0,1},{1,0},{2,3},{3,2},{4,5},{5,4},{6,7},{7,6},{8,9},{9,8},{10,11... | collective-permute-start | bytes 3538952 | tf_op jit(solution)/shard_map/ppermute | solution.py:261
  330.1 41.4 %collective-permute-start.36 = (bf16[4,144,1152]{2,1,0:T(8,128)(2,1)S(1)}, bf16[4,144,1152]{2,1,0:T(8,128)(2,1)S(1)}, u32[]{:S(2)}, u32[]{:S(2)}) collective-permute-start(bf16[4,144,1152]{2,1,0:T(8,128)(2,1)S(1)} %dynamic-slice_bitcast_fusion.1), channel_id=1, source_target_pairs={{0,4},{1,5},{2,3},{3,2},{4,0},{5,1},{6,7},{7,6},{8,12},{9,13},{10,... | collective-permute-start | bytes 3981320 | tf_op jit(solution)/shard_map/ppermute | solution.py:280
  387.4 31.0 %collective-permute-start.39 = (bf16[4,144,1152]{2,1,0:T(8,128)(2,1)}, bf16[4,144,1152]{2,1,0:T(8,128)(2,1)S(1)}, u32[]{:S(2)}, u32[]{:S(2)}) collective-permute-start(bf16[4,144,1152]{2,1,0:T(8,128)(2,1)} %get-tuple-element.310), channel_id=1, source_target_pairs={{0,1},{1,0},{2,3},{3,2},{4,5},{5,4},{6,7},{7,6},{8,9},{9,8},{10,11... | collective-permute-start | bytes 3981320 | tf_op jit(solution)/shard_map/ppermute | solution.py:261
  387.5 30.9 %collective-permute-start.40 = (bf16[4,144,1152]{2,1,0:T(8,128)(2,1)}, bf16[4,144,1152]{2,1,0:T(8,128)(2,1)S(1)}, u32[]{:S(2)}, u32[]{:S(2)}) collective-permute-start(bf16[4,144,1152]{2,1,0:T(8,128)(2,1)} %get-tuple-element.311), channel_id=1, source_target_pairs={{0,4},{4,0},{1,5},{5,1},{2,6},{6,2},{3,7},{7,3},{8,12},{12,8},{9,1... | collective-permute-start | bytes 3981320 | tf_op jit(solution)/shard_map/ppermute | solution.py:261
  420.4 42.1 %collective-permute-start.41 = (bf16[144,1152]{1,0:T(8,128)(2,1)S(1)}, bf16[144,1152]{1,0:T(8,128)(2,1)}, u32[]{:S(2)}, u32[]{:S(2)}) collective-permute-start(bf16[144,1152]{1,0:T(8,128)(2,1)S(1)} %get-tuple-element.327), channel_id=1, source_target_pairs={{0,8},{8,0},{16,24},{24,16},{1,9},{9,1},{17,25},{25,17},{2,10},{10... | collective-permute-start | bytes 995336 | tf_op jit(solution)/shard_map/ppermute | solution.py:266
  421.9 40.6 %collective-permute-start.42 = (bf16[144,1152]{1,0:T(8,128)(2,1)S(1)}, bf16[144,1152]{1,0:T(8,128)(2,1)}, u32[]{:S(2)}, u32[]{:S(2)}) collective-permute-start(bf16[144,1152]{1,0:T(8,128)(2,1)S(1)} %get-tuple-element.326), channel_id=1, source_target_pairs={{0,16},{8,24},{16,0},{24,8},{1,17},{9,25},{17,1},{25,9},{2,18},{10... | collective-permute-start | bytes 995336 | tf_op jit(solution)/shard_map/ppermute | solution.py:266
  423.8 38.7 %collective-permute-start.43 = (bf16[144,1152]{1,0:T(8,128)(2,1)S(1)}, bf16[144,1152]{1,0:T(8,128)(2,1)}, u32[]{:S(2)}, u32[]{:S(2)}) collective-permute-start(bf16[144,1152]{1,0:T(8,128)(2,1)S(1)} %get-tuple-element.325), channel_id=1, source_target_pairs={{0,24},{8,16},{16,8},{24,0},{1,25},{9,17},{17,9},{25,1},{2,26},{10... | collective-permute-start | bytes 995336 | tf_op jit(solution)/shard_map/ppermute | solution.py:266
  424.6 37.8 %collective-permute-start.44 = (bf16[4,144,1152]{2,1,0:T(8,128)(2,1)}, bf16[4,144,1152]{2,1,0:T(8,128)(2,1)}, u32[]{:S(2)}, u32[]{:S(2)}) collective-permute-start(bf16[4,144,1152]{2,1,0:T(8,128)(2,1)} %dynamic-slice_bitcast_fusion), channel_id=1, source_target_pairs={{0,4},{1,5},{2,3},{3,2},{4,0},{5,1},{6,7},{7,6},{8,12},{9,13},{10,... | collective-permute-start | bytes 3981320 | tf_op jit(solution)/shard_map/ppermute | solution.py:280
  474.5 31.0 %collective-permute-start.47 = (bf16[4,144,1152]{2,1,0:T(8,128)(2,1)}, bf16[4,144,1152]{2,1,0:T(8,128)(2,1)}, u32[]{:S(2)}, u32[]{:S(2)}) collective-permute-start(bf16[4,144,1152]{2,1,0:T(8,128)(2,1)} %get-tuple-element.309), channel_id=1, source_target_pairs={{0,1},{1,0},{2,3},{3,2},{4,5},{5,4},{6,7},{7,6},{8,9},{9,8},{10,11... | collective-permute-start | bytes 3981320 | tf_op jit(solution)/shard_map/ppermute | solution.py:261
  474.9 30.7 %collective-permute-start.48 = (bf16[4,144,1152]{2,1,0:T(8,128)(2,1)}, bf16[4,144,1152]{2,1,0:T(8,128)(2,1)}, u32[]{:S(2)}, u32[]{:S(2)}) collective-permute-start(bf16[4,144,1152]{2,1,0:T(8,128)(2,1)} %get-tuple-element.308), channel_id=1, source_target_pairs={{0,4},{4,0},{1,5},{5,1},{2,6},{6,2},{3,7},{7,3},{8,12},{12,8},{9,1... | collective-permute-start | bytes 3981320 | tf_op jit(solution)/shard_map/ppermute | solution.py:261
  480.2 31.9 %collective-permute-start.46 = (bf16[4,144,512]{2,1,0:T(8,128)(2,1)S(1)}, bf16[4,144,512]{2,1,0:T(8,128)(2,1)S(1)}, u32[]{:S(2)}, u32[]{:S(2)}) collective-permute-start(bf16[4,144,512]{2,1,0:T(8,128)(2,1)S(1)} %dynamic-slice_bitcast_fusion.7), channel_id=1, source_target_pairs={{0,4},{1,5},{2,3},{3,2},{4,0},{5,1},{6,7},{7,6},{8,12},{9,13},{10,... | collective-permute-start | bytes 1769480 | tf_op jit(solution)/shard_map/ppermute | solution.py:280
  515.8 29.8 %collective-permute-start.51 = (bf16[144,1152]{1,0:T(8,128)(2,1)}, bf16[144,1152]{1,0:T(8,128)(2,1)}, u32[]{:S(2)}, u32[]{:S(2)}) collective-permute-start(bf16[144,1152]{1,0:T(8,128)(2,1)} %get-tuple-element.323), channel_id=1, source_target_pairs={{0,8},{8,0},{16,24},{24,16},{1,9},{9,1},{17,25},{25,17},{2,10},{10... | collective-permute-start | bytes 995336 | tf_op jit(solution)/shard_map/ppermute | solution.py:266
  516.1 29.5 %collective-permute-start.52 = (bf16[144,1152]{1,0:T(8,128)(2,1)}, bf16[144,1152]{1,0:T(8,128)(2,1)}, u32[]{:S(2)}, u32[]{:S(2)}) collective-permute-start(bf16[144,1152]{1,0:T(8,128)(2,1)} %get-tuple-element.322), channel_id=1, source_target_pairs={{0,16},{8,24},{16,0},{24,8},{1,17},{9,25},{17,1},{25,9},{2,18},{10... | collective-permute-start | bytes 995336 | tf_op jit(solution)/shard_map/ppermute | solution.py:266
  593.3 35.8 %collective-permute-start.62 = (bf16[4,144,640]{2,1,0:T(8,128)(2,1)}, bf16[4,144,640]{2,1,0:T(8,128)(2,1)}, u32[]{:S(2)}, u32[]{:S(2)}) collective-permute-start(bf16[4,144,640]{2,1,0:T(8,128)(2,1)} %get-tuple-element.313), channel_id=1, source_target_pairs={{0,1},{1,0},{2,3},{3,2},{4,5},{5,4},{6,7},{7,6},{8,9},{9,8},{10,11... | collective-permute-start | bytes 2211848 | tf_op jit(solution)/shard_map/ppermute | solution.py:261
  594.1 35.0 %collective-permute-start.63 = (bf16[4,144,640]{2,1,0:T(8,128)(2,1)}, bf16[4,144,640]{2,1,0:T(8,128)(2,1)}, u32[]{:S(2)}, u32[]{:S(2)}) collective-permute-start(bf16[4,144,640]{2,1,0:T(8,128)(2,1)} %get-tuple-element.312), channel_id=1, source_target_pairs={{0,4},{4,0},{1,5},{5,1},{2,6},{6,2},{3,7},{7,3},{8,12},{12,8},{9,1... | collective-permute-start | bytes 2211848 | tf_op jit(solution)/shard_map/ppermute | solution.py:261
  618.8 30.3 %all-to-all-start.3 = ((bf16[32,2,3456]{2,1,0:T(2,128)(2,1)}), bf16[32,2,3456]{2,1,0:T(2,128)(2,1)}, u32[]{:S(2)}, u32[]{:S(2)}) async-start(bf16[32,2,3456]{2,1,0:T(2,128)(2,1)} %broadcast_in_dim.63), calls=%async_computation.3 | async-start | bytes 884736 | tf_op jit(solution)/shard_map/all_to_all | solution.py:741
  632.1 31.0 %collective-permute-start.66 = (bf16[144,640]{1,0:T(8,128)(2,1)}, bf16[144,640]{1,0:T(8,128)(2,1)}, u32[]{:S(2)}, u32[]{:S(2)}) collective-permute-start(bf16[144,640]{1,0:T(8,128)(2,1)} %get-tuple-element.339), channel_id=1, source_target_pairs={{0,8},{8,0},{16,24},{24,16},{1,9},{9,1},{17,25},{25,17},{2,10},{10... | collective-permute-start | bytes 552968 | tf_op jit(solution)/shard_map/ppermute | solution.py:266
  633.3 29.8 %collective-permute-start.67 = (bf16[144,640]{1,0:T(8,128)(2,1)}, bf16[144,640]{1,0:T(8,128)(2,1)}, u32[]{:S(2)}, u32[]{:S(2)}) collective-permute-start(bf16[144,640]{1,0:T(8,128)(2,1)} %get-tuple-element.338), channel_id=1, source_target_pairs={{0,16},{8,24},{16,0},{24,8},{1,17},{9,25},{17,1},{25,9},{2,18},{10... | collective-permute-start | bytes 552968 | tf_op jit(solution)/shard_map/ppermute | solution.py:266
  (147 other events, 1967.5 us)
